TPU v7x, 128 devices: a whole 4x4x4 slice. The times are simulated.
128 devices in a mesh: row: 8 (over x, core), col: 16 (over y, z).
Axes of the slice: x: 4, y: 4, z: 4, core: 2. Of those that a mesh axis runs over, the one named last changes fastest.
Arguments:
- right_side: float32 [131072, 128], P(('row', 'col')), may hold values from -6 to 6
- leaf_inverse: bfloat16 [131072, 1024], P(('row', 'col')), may hold values from -0.1875 to 0.1875
- compress: bfloat16 [131072, 2048], P(('row', 'col')), may hold values from -0.1875 to 0.1875
- middle: bfloat16 [262144, 2048], P(('row', 'col')), may hold values from -0.125 to 0.125
- expand: bfloat16 [131072, 2048], P(('row', 'col')), may hold values from -0.125 to 0.125
- row_project: bfloat16 [3, 131072, 256], P(None, ('row', 'col')), may hold values from -0.1875 to 0.1875
- row_expand: bfloat16 [3, 131072, 256], P(None, ('row', 'col')), may hold values from -0.25 to 0.25
- root_project: bfloat16 [131072, 256], P(('row', 'col')), may hold values from -0.015625 to 0.015625
- root_expand: bfloat16 [131072, 256], P(('row', 'col')), may hold values from -0.375 to 0.375
- owner_map: int32 [16], replicated, may hold values from 0 to 15, each once
Outputs:
- applied: float32 [131072, 128], P(('row', 'col'))
Inputs may be any that keep to these rules, and one draw needn't show every extreme that they name: owner_map names each of the 16 column positions exactly once.
All inputs are finite; a program needn't handle non-finite values.
Results may differ from a plain program's by a relative error of at most 0.004.
Values may be sent and summed in bfloat16 or wider, within the bound.
A program may use at most 128 MiB of HBM per device.

v0:
```python
import jax
import jax.numpy as jnp
from jax import lax
from jax.sharding import PartitionSpec as P

contract_first = (((0,), (0,)), ((), ()))


def swapped(x, axis, bit):
    return lax.ppermute(x, axis, [(i, i ^ 1 << bit) for i in range(lax.axis_size(axis))])


def per_device(
    right_side,
    leaf_inverse,
    compress,
    middle,
    expand,
    row_project,
    row_expand,
    root_project,
    root_expand,
    owner_map,
):
    lowered = right_side.astype(jnp.bfloat16)
    columns = lowered.shape[1]
    dense_part = jnp.dot(leaf_inverse, lowered, preferred_element_type=jnp.float32)
    coeffs = lax.dot_general(
        compress, lowered, contract_first, preferred_element_type=jnp.float32
    ).astype(jnp.bfloat16)
    col_count = lax.axis_size("col")
    pieces = coeffs.reshape(col_count, -1, columns)
    inverse = jnp.argsort(owner_map)
    outgoing = jnp.take(pieces, inverse, axis=0)
    arrived = lax.all_to_all(outgoing, "col", split_axis=0, concat_axis=0, tiled=True)
    shape_now = arrived.shape
    mixed_rows = jnp.dot(
        middle, arrived.reshape(-1, shape_now[2]), preferred_element_type=jnp.float32
    )
    mixed_rows = mixed_rows.astype(jnp.bfloat16).reshape(shape_now)
    returned = lax.all_to_all(mixed_rows, "col", split_axis=0, concat_axis=0, tiled=True)
    ordered = jnp.take(returned, owner_map, axis=0).reshape(-1, columns)
    cluster_part = jnp.dot(expand, ordered, preferred_element_type=jnp.float32)
    level_coeffs = jnp.einsum(
        "blr,lw->brw", row_project, lowered, preferred_element_type=jnp.float32
    )
    root_term = lax.dot_general(
        root_project, lowered, contract_first, preferred_element_type=jnp.float32
    )
    levels = lax.axis_size("row").bit_length() - 1
    running = level_coeffs
    siblings = []
    for level_bit in range(levels):
        partner = swapped(running[level_bit:], "row", level_bit)
        siblings.append(partner[0])
        running = jnp.concatenate(
            [running[: level_bit + 1], running[level_bit + 1 :] + partner[1:]], axis=0
        )
    sibling_sum = jnp.stack(siblings, axis=0)
    root_sum = lax.psum(root_term, ("row", "col"))
    coupled = jnp.einsum(
        "blr,brw->lw",
        row_expand,
        sibling_sum.astype(jnp.bfloat16),
        preferred_element_type=jnp.float32,
    )
    root_part = jnp.dot(
        root_expand, root_sum.astype(jnp.bfloat16), preferred_element_type=jnp.float32
    )
    return dense_part + cluster_part + coupled + root_part


def solution(mesh):
    in_specs = (
        P(("row", "col"), None),
        P(("row", "col"), None),
        P(("row", "col"), None),
        P(("row", "col"), None),
        P(("row", "col"), None),
        P(None, ("row", "col"), None),
        P(None, ("row", "col"), None),
        P(("row", "col"), None),
        P(("row", "col"), None),
        P(),
    )
    out_specs = P(("row", "col"), None)
    return jax.shard_map(
        per_device, mesh=mesh, in_specs=in_specs, out_specs=out_specs, check_vma=False
    )
```

profile of v0, /device:TPU:1, one launch (start us, length us, event | category | flops | bytes accessed | tf_op | source)
XLA Modules:
  0.0 125.4 jit_solution(11228932543114464092)
XLA Ops:
  0.0 0.0 copy-start
  0.0 1.2 convert_element_type.16
  1.2 2.8 %fusion.4 = f32[3,256,128]{2,1,0:T(8,128)} fusion(bf16[3,1024,256]{2,1,0:T(8,128)(2,1)} %param.17, bf16[1024,128]{1,0:T(8,128)(2,1)S(1)} %convert_element_type.16), kind=kOutput, calls=%fused_computation.14 | convolution fusion | flops 201326592 | bytes 2228224 | tf_op jit(solution)/shard_map/blr,lw->brw/dot_general | solution.py:44
  4.0 1.4 %collective-permute-start = (f32[3,256,128]{2,1,0:T(8,128)}, f32[3,256,128]{2,1,0:T(8,128)}, u32[]{:S(2)}, u32[]{:S(2)}) collective-permute-start(f32[3,256,128]{2,1,0:T(8,128)} %fusion.4), channel_id=1, source_target_pairs={{0,16},{16,0},{32,48},{48,32},{64,80},{80,64},{96,112},{112,96},{1... | collective-permute-start | bytes 1179656 | tf_op jit(solution)/shard_map/ppermute | solution.py:10
  5.4 1.9 %sort.17 = (s32[16]{0:T(128)}, s32[16]{0:T(128)S(1)}) sort(s32[16]{0:T(128)} %param.21, s32[16]{0:T(128)S(1)} %iota.4), dimensions={0}, to_apply=%region_0.0 | sort | flops 64 | bytes 256 | tf_op jit(solution)/shard_map/jit(argsort)/sort | solution.py:33
  7.3 3.5 %convolution_convert_fusion.1 = bf16[2048,128]{1,0:T(8,128)(2,1)S(1)} fusion(bf16[1024,2048]{1,0:T(8,128)(2,1)} %param.14, bf16[1024,128]{1,0:T(8,128)(2,1)S(1)} %convert_element_type.16), kind=kOutput, calls=%fused_computation.3 | convolution fusion | flops 537133056 | bytes 4980736 | tf_op jit(solution)/shard_map/dot_general | solution.py:28
  10.8 0.0 copy-start.2
  10.8 0.6 gather_fusion
  11.5 0.9 broadcast_select_fusion.1
  12.4 7.9 %all-to-all-start = ((bf16[16,128,128]{2,1,0:T(8,128)(2,1)}), bf16[16,128,128]{2,1,0:T(8,128)(2,1)S(1)}, u32[]{:S(2)}, u32[]{:S(2)}) async-start(bf16[16,128,128]{2,1,0:T(8,128)(2,1)} %broadcast_select_fusion.1), calls=%async_computation | async-start | bytes 1048576 | tf_op jit(solution)/shard_map/all_to_all | solution.py:35
  20.3 0.0 copy-done
  20.3 0.7 fusion.14
  21.0 1.4 %fusion.15 = f32[256,128]{1,0:T(8,128)S(1)} fusion(bf16[1024,256]{1,0:T(8,128)(2,1)} %param.19, bf16[1024,128]{1,0:T(8,128)(2,1)S(1)} %convert_element_type.16), kind=kOutput, calls=%fused_computation.34 | convolution fusion | flops 67108864 | bytes 917504 | tf_op jit(solution)/shard_map/dot_general | solution.py:47
  22.4 0.0 copy-done.2
  22.4 0.0 collective-permute-done
  22.4 1.8 %slice_add_fusion = f32[2,256,128]{2,1,0:T(8,128)} fusion(f32[3,256,128]{2,1,0:T(8,128)} %collective-permute-done, f32[3,256,128]{2,1,0:T(8,128)} %fusion.4), kind=kLoop, calls=%fused_computation.13 | loop fusion | flops 65536 | bytes 786432 | tf_op jit(solution)/shard_map/add | solution.py:57
  24.2 1.2 collective-permute-start.1
  25.4 5.0 %all-to-all-done = bf16[16,128,128]{2,1,0:T(8,128)(2,1)S(1)} async-done(((bf16[16,128,128]{2,1,0:T(8,128)(2,1)}), bf16[16,128,128]{2,1,0:T(8,128)(2,1)S(1)}, u32[]{:S(2)}, u32[]{:S(2)}) %all-to-all-start) | async-done | bytes 524320 | tf_op jit(solution)/shard_map/all_to_all | solution.py:35
  30.4 7.1 %fusion = bf16[2048,128]{0,1:T(8,128)(2,1)} fusion(bf16[2048,128]{1,0:T(8,128)(2,1)S(1)} %bitcast.37, bf16[2048,2048]{1,0:T(8,128)(2,1)} %param.15), kind=kOutput, calls=%fused_computation.4 | convolution fusion | flops 1074003968 | bytes 9437184 | tf_op jit(solution)/shard_map/dot_general | solution.py:37
  37.5 2.1 %copy.27 = bf16[2048,128]{1,0:T(8,128)(2,1)} copy(bf16[2048,128]{0,1:T(8,128)(2,1)} %fusion) | data formatting | bytes 1048576 | tf_op jit(solution)/shard_map/reshape | solution.py:40
  39.6 4.4 %all-to-all-start.1 = ((bf16[16,128,128]{2,1,0:T(8,128)(2,1)}), bf16[16,128,128]{2,1,0:T(8,128)(2,1)}, u32[]{:S(2)}, u32[]{:S(2)}) async-start(bf16[16,128,128]{2,1,0:T(8,128)(2,1)} %bitcast.3), calls=%async_computation.1 | async-start | bytes 1048576 | tf_op jit(solution)/shard_map/all_to_all | solution.py:41
  44.0 67.2 %all-reduce.1 = bf16[256,128]{1,0:T(8,128)(2,1)S(1)} all-reduce(f32[256,128]{1,0:T(8,128)S(1)} %fusion.15), channel_id=1, replica_groups=mesh['row'=8,'col'=16] {'row','col'}, use_global_device_ids=true, to_apply=%region_1.3 | all-reduce | flops 32768 | bytes 196608 | tf_op jit(solution)/shard_map/psum | solution.py:60
  111.2 1.3 %convolution_bitcast_fusion = f32[1024,128]{1,0:T(8,128)S(1)} fusion(bf16[1024,256]{1,0:T(8,128)(2,1)} %param.20, bf16[256,128]{1,0:T(8,128)(2,1)S(1)} %all-reduce.1), kind=kOutput, calls=%fused_computation.5 | convolution fusion | flops 67108864 | bytes 1114112 | tf_op jit(solution)/shard_map/dot_general | solution.py:67
  112.6 0.9 slice.43
  113.5 0.0 collective-permute-done.1
  113.5 1.1 fusion.13
  114.5 2.2 %collective-permute-start.2 = (bf16[1,256,128]{2,1,0:T(8,128)(2,1)S(1)}, bf16[1,256,128]{2,1,0:T(8,128)(2,1)S(1)}, u32[]{:S(2)}, u32[]{:S(2)}) collective-permute-start(bf16[1,256,128]{2,1,0:T(8,128)(2,1)S(1)} %get-tuple-element.9), channel_id=1, source_target_pairs={{0,64},{16,80},{32,96},{48,112},{64,0},{80,16},{96,32},{112,48},{1... | collective-permute-start | bytes 196616 | tf_op jit(solution)/shard_map/ppermute | solution.py:10
  116.7 0.0 all-to-all-done.1
  116.7 2.4 %gather_fusion.1 = bf16[16,128,128]{2,1,0:T(8,128)(2,1)} fusion(bf16[16,128,128]{2,1,0:T(8,128)(2,1)} %all-to-all-done.1, s32[1024]{0:T(1024)S(1)} %pad_clamp_fusion), kind=kCustom, calls=%fused_computation.1.clone | custom fusion | bytes 1048640 | tf_op jit(solution)/shard_map/jit(_take)/gather | solution.py:42
  119.2 0.0 copy-start.1
  119.2 1.3 %broadcast_select_fusion = bf16[16,128,128]{2,1,0:T(8,128)(2,1)S(1)} fusion(bf16[16,128,128]{2,1,0:T(8,128)(2,1)} %gather_fusion.1, pred[16]{0:T(512)(128)(4,1)S(1)} %compare_and_fusion), kind=kLoop, calls=%fused_computation.11 | loop fusion | flops 262144 | bytes 1048592 | tf_op jit(solution)/shard_map/jit(_take)/select_n | solution.py:42
  120.5 3.5 %fusion.1 = f32[1024,128]{1,0:T(8,128)S(1)} fusion(f32[1024,128]{1,0:T(8,128)S(1)} %fusion.14, bf16[1024,2048]{1,0:T(8,128)(2,1)} %param.16, bf16[2048,128]{1,0:T(8,128)(2,1)S(1)} %bitcast.38), kind=kOutput, calls=%fused_computation.8 | convolution fusion | flops 537001984 | bytes 5767168 | tf_op jit(solution)/shard_map/dot_general | solution.py:43
  123.9 0.0 collective-permute-done.2
  124.0 0.0 copy-done.1
  124.0 1.4 %fusion.3 = f32[1024,128]{1,0:T(8,128)} fusion(f32[1024,128]{1,0:T(8,128)S(1)} %convolution_bitcast_fusion, f32[1024,128]{1,0:T(8,128)S(1)} %fusion.1, bf16[3,1024,256]{2,1,0:T(8,128)(2,1)S(1)} %copy-done.1, bf16[1,256,128]{2,1,0:T(8,128)(2,1)S(1)} %collective-permute-done.2, bf16[1,256,128]{2,1,0:T(8,128)(2,1)S(1)} %get-tuple-element.8, ...), kind=kOutput, calls=%fused_computation.10 | convolution fusion | flops 201785344 | bytes 3342336 | tf_op jit(solution)/shard_map/blr,brw->lw/dot_general | solution.py:61
  (7 shorter events, 0.0 us)
Async XLA Ops:
  0.0 20.3 %copy-start = (bf16[1024,1024]{1,0:T(8,128)(2,1)S(1)}, bf16[1024,1024]{1,0:T(8,128)(2,1)}, u32[]{:S(2)}) copy-start(bf16[1024,1024]{1,0:T(8,128)(2,1)} %param.13) | copy-start | bytes 6291460
  4.0 18.4 %collective-permute-start = (f32[3,256,128]{2,1,0:T(8,128)}, f32[3,256,128]{2,1,0:T(8,128)}, u32[]{:S(2)}, u32[]{:S(2)}) collective-permute-start(f32[3,256,128]{2,1,0:T(8,128)} %fusion.4), channel_id=1, source_target_pairs={{0,16},{16,0},{32,48},{48,32},{64,80},{80,64},{96,112},{112,96},{1... | collective-permute-start | bytes 1179656 | tf_op jit(solution)/shard_map/ppermute | solution.py:10
  10.8 11.6 %copy-start.2 = (s32[16]{0:T(128)S(1)}, s32[16]{0:T(128)}, u32[]{:S(2)}) copy-start(s32[16]{0:T(128)} %param.21) | copy-start | bytes 196
  12.4 18.0 %all-to-all-start = ((bf16[16,128,128]{2,1,0:T(8,128)(2,1)}), bf16[16,128,128]{2,1,0:T(8,128)(2,1)S(1)}, u32[]{:S(2)}, u32[]{:S(2)}) async-start(bf16[16,128,128]{2,1,0:T(8,128)(2,1)} %broadcast_select_fusion.1), calls=%async_computation | async-start | bytes 1048576 | tf_op jit(solution)/shard_map/all_to_all | solution.py:35
  24.2 89.3 %collective-permute-start.1 = (f32[2,256,128]{2,1,0:T(8,128)}, f32[2,256,128]{2,1,0:T(8,128)}, u32[]{:S(2)}, u32[]{:S(2)}) collective-permute-start(f32[2,256,128]{2,1,0:T(8,128)} %slice_add_fusion), channel_id=1, source_target_pairs={{0,32},{16,48},{32,0},{48,16},{64,96},{80,112},{96,64},{112,80},{1... | collective-permute-start | bytes 786440 | tf_op jit(solution)/shard_map/ppermute | solution.py:10
  39.6 77.2 %all-to-all-start.1 = ((bf16[16,128,128]{2,1,0:T(8,128)(2,1)}), bf16[16,128,128]{2,1,0:T(8,128)(2,1)}, u32[]{:S(2)}, u32[]{:S(2)}) async-start(bf16[16,128,128]{2,1,0:T(8,128)(2,1)} %bitcast.3), calls=%async_computation.1 | async-start | bytes 1048576 | tf_op jit(solution)/shard_map/all_to_all | solution.py:41
  114.5 9.4 %collective-permute-start.2 = (bf16[1,256,128]{2,1,0:T(8,128)(2,1)S(1)}, bf16[1,256,128]{2,1,0:T(8,128)(2,1)S(1)}, u32[]{:S(2)}, u32[]{:S(2)}) collective-permute-start(bf16[1,256,128]{2,1,0:T(8,128)(2,1)S(1)} %get-tuple-element.9), channel_id=1, source_target_pairs={{0,64},{16,80},{32,96},{48,112},{64,0},{80,16},{96,32},{112,48},{1... | collective-permute-start | bytes 196616 | tf_op jit(solution)/shard_map/ppermute | solution.py:10
  119.2 4.8 %copy-start.1 = (bf16[3,1024,256]{2,1,0:T(8,128)(2,1)S(1)}, bf16[3,1024,256]{2,1,0:T(8,128)(2,1)}, u32[]{:S(2)}) copy-start(bf16[3,1024,256]{2,1,0:T(8,128)(2,1)} %param.18) | copy-start | bytes 4718596
where the time goes:
time: 126 us; the launch traced here: 125 us
  blocking collectives  67.2 us (53%)
  matrix products  21.6 us (17%)
  starting transfers between devices  17.1 us (14%)
  other arithmetic  8.15 us (6%)
  local copies, waits for them, and re-layouts  6.08 us (5%)
  waiting for transfers between devices  5.01 us (4%)
    psum x1, blocking collectives, per_device(): root_sum = lax.psum(root_term, ('row', 'col'))  67.2 us
    all_to_all x1, starting transfers between devices, per_device(): lax.all_to_all(outgoing, 'col', split_axis=0, concat_axis=0, tiled=True)  7.85 us
    dot_general x1, matrix products, per_device(): jnp.dot(middle, arrived.reshape(-1, shape_now[2]), preferred_element_type...  7.1 us
    all_to_all x1, waiting for transfers between devices, per_device(): lax.all_to_all(outgoing, 'col', split_axis=0, concat_axis=0, tiled=True)  5 us
    ppermute x3, starting transfers between devices, swapped(): lax.ppermute(x, axis, [(i, i ^ 1 << bit) for i in range(lax.axis_size(axi...  4.81 us
    all_to_all x1, starting transfers between devices, per_device(): lax.all_to_all(mixed_rows, 'col', split_axis=0, concat_axis=0, tiled=True)  4.44 us
    dot_general x1, matrix products, per_device(): lax.dot_general(compress, lowered, contract_first, preferred_element_type...  3.5 us
    dot_general x1, matrix products, per_device(): cluster_part = jnp.dot(expand, ordered, preferred_element_type=jnp.float32)  3.48 us
  transfers between devices with their start and end apart: 5, of which 1 were waited for; matrix products, arithmetic and copies ran while one was open for 24% of the time, Pallas kernels for 0%

commit v1 on v0

--- a/solution.py
+++ b/solution.py
@@ -57,7 +57,7 @@
             [running[: level_bit + 1], running[level_bit + 1 :] + partner[1:]], axis=0
         )
     sibling_sum = jnp.stack(siblings, axis=0)
-    root_sum = lax.psum(root_term, ("row", "col"))
+    root_sum = jnp.sum(lax.all_gather(lax.psum(root_term, "row"), "col", axis=0), axis=0)
     coupled = jnp.einsum(
         "blr,brw->lw",
         row_expand,

time: 126 us -> 140 us (1.11)
  the two profiles are of different devices: /device:TPU:1 before, /device:TPU:6 now
where the time goes in v1:
time: 140 us
  waiting for transfers between devices  80.3 us (57%)
  matrix products  21.3 us (15%)
  between operations  13.6 us (10%)
  starting transfers between devices  11.1 us (8%)
  other arithmetic  8.62 us (6%)
  local copies, waits for them, and re-layouts  4.72 us (3%)
    psum x1, waiting for transfers between devices, per_device(): lax.psum(root_term, 'row')  57.5 us
    all_to_all x1, waiting for transfers between devices, per_device(): lax.all_to_all(mixed_rows, 'col', split_axis=0, concat_axis=0, tiled=True)  13 us
    all_to_all x1, waiting for transfers between devices, per_device(): lax.all_to_all(outgoing, 'col', split_axis=0, concat_axis=0, tiled=True)  9.2 us
    all_to_all x1, starting transfers between devices, per_device(): lax.all_to_all(outgoing, 'col', split_axis=0, concat_axis=0, tiled=True)  7.03 us
    dot_general x1, matrix products, per_device(): jnp.dot(middle, arrived.reshape(-1, shape_now[2]), preferred_element_type...  6.49 us
    all_to_all x1, starting transfers between devices, per_device(): lax.all_to_all(mixed_rows, 'col', split_axis=0, concat_axis=0, tiled=True)  3.57 us
    dot_general x1, matrix products, per_device(): lax.dot_general(compress, lowered, contract_first, preferred_element_type...  3.5 us
    dot_general x1, matrix products, per_device(): cluster_part = jnp.dot(expand, ordered, preferred_element_type=jnp.float32)  3.45 us
  transfers between devices with their start and end apart: 7, of which 4 were waited for; matrix products, arithmetic and copies ran while one was open for 20% of the time, Pallas kernels for 0%

profile of v1, /device:TPU:6, one launch (start us, length us, event | category | flops | bytes accessed | tf_op | source)
XLA Modules:
  0.0 139.6 jit_solution(6744168782270515428)
XLA Ops:
  6.5 0.0 copy-start
  6.5 0.0 all-reduce.2.cloned.1.call-start
  6.5 1.2 convert_element_type.16
  7.8 2.0 %convolution_bitcast_fusion.3 = f32[1,256,128]{2,1,0:T(8,128)} fusion(bf16[1024,256]{1,0:T(8,128)(2,1)} %param.19, bf16[1024,128]{1,0:T(8,128)(2,1)S(1)} %convert_element_type.16), kind=kOutput, calls=%fused_computation.11 | convolution fusion | flops 67108864 | bytes 917504 | tf_op jit(solution)/shard_map/dot_general | solution.py:47
  9.8 0.0 all-reduce.2.cloned.1.call-update
  9.8 0.0 all-gather.2.cloned.1.call-start
  9.9 1.9 %sort.17 = (s32[16]{0:T(128)}, s32[16]{0:T(128)S(1)}) sort(s32[16]{0:T(128)} %param.21, s32[16]{0:T(128)S(1)} %iota.4), dimensions={0}, to_apply=%region_0.0 | sort | flops 64 | bytes 256 | tf_op jit(solution)/shard_map/jit(argsort)/sort | solution.py:33
  11.8 57.5 %all-reduce.2.cloned.1.call-done = f32[1,256,128]{2,1,0:T(8,128)} async-done(((f32[1,256,128]{2,1,0:T(8,128)}), f32[1,256,128]{2,1,0:T(8,128)}) %all-reduce.2.cloned.1.call-update) | async-done | bytes 131088 | tf_op jit(solution)/shard_map/psum | solution.py:60
  69.2 0.0 all-gather.2.cloned.1.call-update
  69.3 3.5 %convolution_convert_fusion.1 = bf16[2048,128]{1,0:T(8,128)(2,1)S(1)} fusion(bf16[1024,2048]{1,0:T(8,128)(2,1)} %param.14, bf16[1024,128]{1,0:T(8,128)(2,1)S(1)} %convert_element_type.16), kind=kOutput, calls=%fused_computation.3 | convolution fusion | flops 537133056 | bytes 4980736 | tf_op jit(solution)/shard_map/dot_general | solution.py:28
  72.8 0.6 gather_fusion
  73.5 0.9 broadcast_select_fusion.1
  74.4 7.0 %all-to-all-start = ((bf16[16,128,128]{2,1,0:T(8,128)(2,1)}), bf16[16,128,128]{2,1,0:T(8,128)(2,1)}, u32[]{:S(2)}, u32[]{:S(2)}) async-start(bf16[16,128,128]{2,1,0:T(8,128)(2,1)} %broadcast_select_fusion.1), calls=%async_computation | async-start | bytes 1048576 | tf_op jit(solution)/shard_map/all_to_all | solution.py:35
  81.4 0.0 copy-start.3
  81.4 2.1 %fusion.4 = f32[3,256,128]{2,1,0:T(8,128)S(1)} fusion(bf16[3,1024,256]{2,1,0:T(8,128)(2,1)} %param.17, bf16[1024,128]{1,0:T(8,128)(2,1)S(1)} %convert_element_type.16), kind=kOutput, calls=%fused_computation.15 | convolution fusion | flops 201326592 | bytes 2228224 | tf_op jit(solution)/shard_map/blr,lw->brw/dot_general | solution.py:44
  83.5 0.4 collective-permute-start
  83.9 0.0 copy-done
  83.9 0.7 fusion.14
  84.6 0.0 copy-done.3
  84.7 0.6 collective-permute-done
  85.3 0.0 copy-start.2
  85.3 0.7 copy-done.2
  86.0 0.0 collective-permute-start.1
  86.1 9.2 %all-to-all-done = bf16[16,128,128]{2,1,0:T(8,128)(2,1)} async-done(((bf16[16,128,128]{2,1,0:T(8,128)(2,1)}), bf16[16,128,128]{2,1,0:T(8,128)(2,1)}, u32[]{:S(2)}, u32[]{:S(2)}) %all-to-all-start) | async-done | bytes 524320 | tf_op jit(solution)/shard_map/all_to_all | solution.py:35
  95.3 6.5 %fusion = bf16[2048,128]{0,1:T(8,128)(2,1)S(1)} fusion(bf16[2048,128]{1,0:T(8,128)(2,1)} %bitcast.1, bf16[2048,2048]{1,0:T(8,128)(2,1)} %param.15), kind=kOutput, calls=%fused_computation.4 | convolution fusion | flops 1074003968 | bytes 9437184 | tf_op jit(solution)/shard_map/dot_general | solution.py:37
  101.8 1.0 copy.33
  102.8 3.6 %all-to-all-start.1 = ((bf16[16,128,128]{2,1,0:T(8,128)(2,1)}), bf16[16,128,128]{2,1,0:T(8,128)(2,1)S(1)}, u32[]{:S(2)}, u32[]{:S(2)}) async-start(bf16[16,128,128]{2,1,0:T(8,128)(2,1)} %bitcast.40), calls=%async_computation.1 | async-start | bytes 1048576 | tf_op jit(solution)/shard_map/all_to_all | solution.py:41
  106.4 0.9 slice.43
  107.3 0.0 collective-permute-done.1
  107.3 1.6 %fusion.13 = (bf16[1,256,128]{2,1,0:T(8,128)(2,1)S(1)}, bf16[1,256,128]{2,1,0:T(8,128)(2,1)}) fusion(f32[2,256,128]{2,1,0:T(8,128)} %collective-permute-done.1, f32[2,256,128]{2,1,0:T(8,128)S(1)} %slice_add_fusion), kind=kLoop, calls=%fused_computation.33 | loop fusion | flops 65536 | bytes 458752 | tf_op jit(solution)/shard_map/slice | solution.py:55
  108.9 0.0 collective-permute-start.2
  108.9 13.0 %all-to-all-done.1 = bf16[16,128,128]{2,1,0:T(8,128)(2,1)S(1)} async-done(((bf16[16,128,128]{2,1,0:T(8,128)(2,1)}), bf16[16,128,128]{2,1,0:T(8,128)(2,1)S(1)}, u32[]{:S(2)}, u32[]{:S(2)}) %all-to-all-start.1) | async-done | bytes 524320 | tf_op jit(solution)/shard_map/all_to_all | solution.py:41
  121.9 1.4 %gather_fusion.1 = bf16[16,128,128]{2,1,0:T(8,128)(2,1)} fusion(bf16[16,128,128]{2,1,0:T(8,128)(2,1)S(1)} %all-to-all-done.1, s32[1024]{0:T(1024)S(1)} %pad_clamp_fusion), kind=kCustom, calls=%fused_computation.1.clone | custom fusion | bytes 1048640 | tf_op jit(solution)/shard_map/jit(_take)/gather | solution.py:42
  123.3 1.2 broadcast_select_fusion
  124.5 3.5 %fusion.1 = f32[1024,128]{1,0:T(8,128)S(1)} fusion(f32[1024,128]{1,0:T(8,128)S(1)} %fusion.14, bf16[1024,2048]{1,0:T(8,128)(2,1)} %param.16, bf16[2048,128]{1,0:T(8,128)(2,1)S(1)} %bitcast.39), kind=kOutput, calls=%fused_computation.8 | convolution fusion | flops 537001984 | bytes 5767168 | tf_op jit(solution)/shard_map/dot_general | solution.py:43
  127.9 0.0 copy-start.1
  127.9 0.0 all-gather.2.cloned.1.call-done
  128.0 1.7 %reduce_sum.9 = bf16[256,128]{1,0:T(8,128)(2,1)S(1)} reduce(f32[16,256,128]{2,1,0:T(8,128)} %all-gather.2.cloned.1.call-done, f32[]{:T(128)} %constant.1.clone.1), dimensions={0}, to_apply=%region_2.4 | reduce | flops 491520 | bytes 2162692 | tf_op jit(solution)/shard_map/reduce_sum | solution.py:60
  129.7 0.0 copy-done.1
  129.7 0.3 convolution_bitcast_fusion
  130.0 0.0 collective-permute-done.2
  130.0 2.8 %fusion.3 = f32[1024,128]{1,0:T(8,128)} fusion(f32[1024,128]{1,0:T(8,128)S(1)} %convolution_bitcast_fusion, f32[1024,128]{1,0:T(8,128)S(1)} %fusion.1, bf16[3,1024,256]{2,1,0:T(8,128)(2,1)} %param.18, bf16[1,256,128]{2,1,0:T(8,128)(2,1)} %collective-permute-done.2, bf16[1,256,128]{2,1,0:T(8,128)(2,1)S(1)} %get-tuple-element.8, ...), kind=kOutput, calls=%fused_computation.10 | convolution fusion | flops 201785344 | bytes 3342336 | tf_op jit(solution)/shard_map/blr,brw->lw/dot_general | solution.py:61
  (8 shorter events, 0.1 us)
Async XLA Ops:
  6.5 77.4 %copy-start = (bf16[1024,1024]{1,0:T(8,128)(2,1)S(1)}, bf16[1024,1024]{1,0:T(8,128)(2,1)}, u32[]{:S(2)}) copy-start(bf16[1024,1024]{1,0:T(8,128)(2,1)} %param.13) | copy-start | bytes 6291460
  6.5 62.7 %all-reduce.2.cloned.1.call-start = ((), (), s32[]{:S(2)}) async-start(), calls=%async_computation.2 | async-start | bytes 262144 | tf_op jit(solution)/shard_map/psum | solution.py:60
  9.8 118.1 %all-gather.2.cloned.1.call-start = ((), (), s32[]{:S(2)}) async-start(), calls=%async_computation.3 | async-start | bytes 2228224 | tf_op jit(solution)/shard_map/all_gather | solution.py:60
  74.4 20.9 %all-to-all-start = ((bf16[16,128,128]{2,1,0:T(8,128)(2,1)}), bf16[16,128,128]{2,1,0:T(8,128)(2,1)}, u32[]{:S(2)}, u32[]{:S(2)}) async-start(bf16[16,128,128]{2,1,0:T(8,128)(2,1)} %broadcast_select_fusion.1), calls=%async_computation | async-start | bytes 1048576 | tf_op jit(solution)/shard_map/all_to_all | solution.py:35
  81.4 3.2 %copy-start.3 = (s32[16]{0:T(128)S(1)}, s32[16]{0:T(128)}, u32[]{:S(2)}) copy-start(s32[16]{0:T(128)} %param.21) | copy-start | bytes 196
  83.5 1.8 %collective-permute-start = (f32[3,256,128]{2,1,0:T(8,128)S(1)}, f32[3,256,128]{2,1,0:T(8,128)S(1)}, u32[]{:S(2)}, u32[]{:S(2)}) collective-permute-start(f32[3,256,128]{2,1,0:T(8,128)S(1)} %fusion.4), channel_id=1, source_target_pairs={{0,16},{16,0},{32,48},{48,32},{64,80},{80,64},{96,112},{112,96},{1... | collective-permute-start | bytes 1179656 | tf_op jit(solution)/shard_map/ppermute | solution.py:10
  85.3 0.8 copy-start.2
  86.0 21.2 %collective-permute-start.1 = (f32[2,256,128]{2,1,0:T(8,128)S(1)}, f32[2,256,128]{2,1,0:T(8,128)}, u32[]{:S(2)}, u32[]{:S(2)}) collective-permute-start(f32[2,256,128]{2,1,0:T(8,128)S(1)} %slice_add_fusion), channel_id=1, source_target_pairs={{0,32},{16,48},{32,0},{48,16},{64,96},{80,112},{96,64},{112,80},{1... | collective-permute-start | bytes 786440 | tf_op jit(solution)/shard_map/ppermute | solution.py:10
  102.8 19.1 %all-to-all-start.1 = ((bf16[16,128,128]{2,1,0:T(8,128)(2,1)}), bf16[16,128,128]{2,1,0:T(8,128)(2,1)S(1)}, u32[]{:S(2)}, u32[]{:S(2)}) async-start(bf16[16,128,128]{2,1,0:T(8,128)(2,1)} %bitcast.40), calls=%async_computation.1 | async-start | bytes 1048576 | tf_op jit(solution)/shard_map/all_to_all | solution.py:41
  108.9 21.1 %collective-permute-start.2 = (bf16[1,256,128]{2,1,0:T(8,128)(2,1)}, bf16[1,256,128]{2,1,0:T(8,128)(2,1)}, u32[]{:S(2)}, u32[]{:S(2)}) collective-permute-start(bf16[1,256,128]{2,1,0:T(8,128)(2,1)} %get-tuple-element.9), channel_id=1, source_target_pairs={{0,64},{16,80},{32,96},{48,112},{64,0},{80,16},{96,32},{112,48},{1... | collective-permute-start | bytes 196616 | tf_op jit(solution)/shard_map/ppermute | solution.py:10
  127.9 1.8 %copy-start.1 = (bf16[1024,256]{1,0:T(8,128)(2,1)S(1)}, bf16[1024,256]{1,0:T(8,128)(2,1)}, u32[]{:S(2)}) copy-start(bf16[1024,256]{1,0:T(8,128)(2,1)} %param.20) | copy-start | bytes 1572868
Sparse Core Ops, SparseCore 0:
  9.9 59.2 all-reduce.1
  71.6 53.5 all-gather.1

commit v2 on v1

--- a/solution.py
+++ b/solution.py
@@ -1,13 +1,73 @@
+import functools
+
 import jax
 import jax.numpy as jnp
 from jax import lax
+from jax.experimental import pallas as pl
+from jax.experimental.pallas import tpu as pltpu
 from jax.sharding import PartitionSpec as P
 
 contract_first = (((0,), (0,)), ((), ()))
+MESH_ID = pl.DeviceIdType.MESH
 
 
 def swapped(x, axis, bit):
     return lax.ppermute(x, axis, [(i, i ^ 1 << bit) for i in range(lax.axis_size(axis))])
+
+
+def exchange_kernel(n, x_ref, o_ref, send_sem, recv_sem, local_sem):
+    me = lax.axis_index("col")
+    row = lax.axis_index("row")
+    barrier = pltpu.get_barrier_semaphore()
+    for s in range(1, n):
+        peer = lax.rem(me + s, n)
+        pl.semaphore_signal(barrier, inc=1, device_id=(row, peer), device_id_type=MESH_ID)
+    pl.semaphore_wait(barrier, n - 1)
+
+    local = pltpu.make_async_copy(x_ref.at[me], o_ref.at[me], local_sem)
+    local.start()
+    copies = []
+    for s in range(1, n):
+        peer = lax.rem(me + s, n)
+        copy = pltpu.make_async_remote_copy(
+            src_ref=x_ref.at[peer],
+            dst_ref=o_ref.at[me],
+            send_sem=send_sem.at[s],
+            recv_sem=recv_sem.at[s],
+            device_id=(row, peer),
+            device_id_type=MESH_ID,
+        )
+        copy.start()
+        copies.append(copy)
+    for s in range(1, n):
+        source = lax.rem(me + n - s, n)
+        arriving = pltpu.make_async_remote_copy(
+            src_ref=x_ref.at[source],
+            dst_ref=o_ref.at[source],
+            send_sem=send_sem.at[s],
+            recv_sem=recv_sem.at[s],
+            device_id=(row, source),
+            device_id_type=MESH_ID,
+        )
+        copies[s - 1].wait_send()
+        arriving.wait_recv()
+    local.wait()
+
+
+def exchange(x, cid):
+    n = x.shape[0]
+    return pl.pallas_call(
+        functools.partial(exchange_kernel, n),
+        out_shape=jax.ShapeDtypeStruct(x.shape, x.dtype),
+        in_specs=[pl.BlockSpec(memory_space=pl.ANY)],
+        out_specs=pl.BlockSpec(memory_space=pl.ANY),
+        scratch_shapes=[
+            pltpu.SemaphoreType.DMA((n,)),
+            pltpu.SemaphoreType.DMA((n,)),
+            pltpu.SemaphoreType.DMA,
+        ],
+        compiler_params=pltpu.CompilerParams(collective_id=cid, has_side_effects=True),
+    )(x)
 
 
 def per_device(
@@ -24,6 +84,12 @@
 ):
     lowered = right_side.astype(jnp.bfloat16)
     columns = lowered.shape[1]
+    root_term = lax.dot_general(
+        root_project, lowered, contract_first, preferred_element_type=jnp.float32
+    )
+    level_coeffs = jnp.einsum(
+        "blr,lw->brw", row_project, lowered, preferred_element_type=jnp.float32
+    )
     dense_part = jnp.dot(leaf_inverse, lowered, preferred_element_type=jnp.float32)
     coeffs = lax.dot_general(
         compress, lowered, contract_first, preferred_element_type=jnp.float32
@@ -32,23 +98,18 @@
     pieces = coeffs.reshape(col_count, -1, columns)
     inverse = jnp.argsort(owner_map)
     outgoing = jnp.take(pieces, inverse, axis=0)
-    arrived = lax.all_to_all(outgoing, "col", split_axis=0, concat_axis=0, tiled=True)
+    arrived = exchange(outgoing, 0)
     shape_now = arrived.shape
     mixed_rows = jnp.dot(
         middle, arrived.reshape(-1, shape_now[2]), preferred_element_type=jnp.float32
     )
     mixed_rows = mixed_rows.astype(jnp.bfloat16).reshape(shape_now)
-    returned = lax.all_to_all(mixed_rows, "col", split_axis=0, concat_axis=0, tiled=True)
+    returned = exchange(mixed_rows, 1)
     ordered = jnp.take(returned, owner_map, axis=0).reshape(-1, columns)
     cluster_part = jnp.dot(expand, ordered, preferred_element_type=jnp.float32)
-    level_coeffs = jnp.einsum(
-        "blr,lw->brw", row_project, lowered, preferred_element_type=jnp.float32
-    )
-    root_term = lax.dot_general(
-        root_project, lowered, contract_first, preferred_element_type=jnp.float32
-    )
+
     levels = lax.axis_size("row").bit_length() - 1
-    running = level_coeffs
+    running = jnp.concatenate([level_coeffs, root_term[None]], axis=0)
     siblings = []
     for level_bit in range(levels):
         partner = swapped(running[level_bit:], "row", level_bit)
@@ -57,7 +118,9 @@
             [running[: level_bit + 1], running[level_bit + 1 :] + partner[1:]], axis=0
         )
     sibling_sum = jnp.stack(siblings, axis=0)
-    root_sum = jnp.sum(lax.all_gather(lax.psum(root_term, "row"), "col", axis=0), axis=0)
+    root_sum = running[levels]
+    for bit in range(lax.axis_size("col").bit_length() - 1):
+        root_sum = root_sum + swapped(root_sum, "col", bit)
     coupled = jnp.einsum(
         "blr,brw->lw",
         row_expand,

time: 140 us -> 86.9 us (0.62)
  the two profiles are of different devices: /device:TPU:6 before, /device:TPU:0 now
where the time goes in v2:
time: 86.9 us; the launch traced here: 86.6 us
  Pallas kernels  28.5 us (33%)
  waiting for transfers between devices  18.1 us (21%)
  matrix products  16 us (18%)
  starting transfers between devices  10.9 us (13%)
  other arithmetic  6.65 us (8%)
  local copies, waits for them, and re-layouts  6.25 us (7%)
    pallas_call x2, Pallas kernels, exchange(): pl.pallas_call(functools.partial(exchange_kernel, n), out_shape=jax.Shape...  28.5 us
    ppermute x7, waiting for transfers between devices, swapped(): lax.ppermute(x, axis, [(i, i ^ 1 << bit) for i in range(lax.axis_size(axi...  18.1 us
    ppermute x7, starting transfers between devices, swapped(): lax.ppermute(x, axis, [(i, i ^ 1 << bit) for i in range(lax.axis_size(axi...  10.9 us
    dot_general x1, matrix products, per_device(): jnp.dot(middle, arrived.reshape(-1, shape_now[2]), preferred_element_type...  6.48 us
    dot_general x1, matrix products, per_device(): jnp.einsum('blr,lw->brw', row_project, lowered, preferred_element_type=jn...  2.35 us
    add x2, other arithmetic, per_device(): running[level_bit + 1:] + partner[1:]  2.17 us
    dot_general x1, matrix products, per_device(): lax.dot_general(compress, lowered, contract_first, preferred_element_type...  2.12 us
    slice x3, local copies, waits for them, and re-layouts, per_device(): siblings.append(partner[0])  1.83 us
  transfers between devices with their start and end apart: 7, of which 5 were waited for; matrix products, arithmetic and copies ran while one was open for 23% of the time, Pallas kernels for 33%

profile of v2, /device:TPU:0, one launch (start us, length us, event | category | flops | bytes accessed | tf_op | source)
XLA Modules:
  0.0 86.6 jit_solution(15581558547598428826)
XLA Ops:
  0.0 0.0 copy-start
  0.0 0.0 copy-start.4
  0.0 1.2 %convert_element_type.16 = bf16[1024,128]{1,0:T(8,128)(2,1)S(1)} convert(f32[1024,128]{1,0:T(8,128)} %param.12) | non-fusion elementwise | flops 131072 | bytes 786432 | tf_op jit(solution)/shard_map/convert_element_type | solution.py:85
  1.2 2.4 %fusion.6 = f32[3,256,128]{2,1,0:T(8,128)S(1)} fusion(bf16[3,1024,256]{2,1,0:T(8,128)(2,1)} %param.17, bf16[1024,128]{1,0:T(8,128)(2,1)S(1)} %convert_element_type.16), kind=kOutput, calls=%fused_computation.20 | convolution fusion | flops 201326592 | bytes 2228224 | tf_op jit(solution)/shard_map/blr,lw->brw/dot_general | solution.py:90
  3.6 0.0 copy-start.5
  3.6 1.4 %convolution_bitcast_fusion.3 = f32[1,256,128]{2,1,0:T(8,128)S(1)} fusion(bf16[1024,256]{1,0:T(8,128)(2,1)} %param.19, bf16[1024,128]{1,0:T(8,128)(2,1)S(1)} %convert_element_type.16), kind=kOutput, calls=%fused_computation.11 | convolution fusion | flops 67108864 | bytes 917504 | tf_op jit(solution)/shard_map/dot_general | solution.py:87
  5.0 0.8 pad_maximum_fusion
  5.8 0.0 collective-permute-start
  5.8 0.0 copy-done.4
  5.8 2.1 %convolution_convert_fusion.1 = bf16[2048,128]{1,0:T(8,128)(2,1)} fusion(bf16[1024,2048]{1,0:T(8,128)(2,1)S(1)} %copy-done.4, bf16[1024,128]{1,0:T(8,128)(2,1)S(1)} %convert_element_type.16), kind=kOutput, calls=%fused_computation.3 | convolution fusion | flops 537133056 | bytes 4980736 | tf_op jit(solution)/shard_map/dot_general | solution.py:94
  7.9 0.0 copy-done.5
  8.0 1.3 %sort.17 = (s32[16]{0:T(128)}, s32[16]{0:T(128)S(1)}) sort(s32[16]{0:T(128)S(1)} %copy-done.5, s32[16]{0:T(128)S(1)} %iota.4), dimensions={0}, to_apply=%region_0.0 | sort | flops 64 | bytes 256 | tf_op jit(solution)/shard_map/jit(argsort)/sort | solution.py:99
  9.3 1.7 %gather_fusion = bf16[16,128,128]{2,1,0:T(8,128)(2,1)S(1)} fusion(bf16[16,128,128]{2,1,0:T(8,128)(2,1)} %bitcast.43, s32[1024]{0:T(1024)S(1)} %pad_clamp_fusion.1), kind=kCustom, calls=%fused_computation.clone | custom fusion | bytes 1048640 | tf_op jit(solution)/shard_map/jit(_take)/gather | solution.py:100
  11.0 0.9 %broadcast_select_fusion.1.x_ref = bf16[16,128,128]{2,1,0:T(8,128)(2,1)} fusion(bf16[16,128,128]{2,1,0:T(8,128)(2,1)S(1)} %gather_fusion, pred[16]{0:T(512)(128)(4,1)S(1)} %compare_and_fusion.1), kind=kLoop, calls=%fused_computation.16 | loop fusion | flops 262144 | bytes 1048592 | tf_op jit(solution)/shard_map/jit(_take)/select_n | solution.py:100
  11.9 14.8 %shard_map.100 = bf16[16,128,128]{2,1,0:T(8,128)(2,1)} custom-call(bf16[16,128,128]{2,1,0:T(8,128)(2,1)} %broadcast_select_fusion.1.x_ref), custom_call_target="tpu_custom_call" | custom-call | tf_op jit(solution)/shard_map/pallas_call | solution.py:59
  26.7 0.0 collective-permute-done
  26.7 1.0 %fusion.5 = f32[3,256,128]{2,1,0:T(8,128)S(1)} fusion(f32[3,256,128]{2,1,0:T(8,128)S(1)} %fusion.6, f32[1,256,128]{2,1,0:T(8,128)S(1)} %convolution_bitcast_fusion.3, f32[4,256,128]{2,1,0:T(8,128)} %collective-permute-done), kind=kLoop, calls=%fused_computation.18 | loop fusion | flops 196608 | bytes 1310720 | tf_op jit(solution)/shard_map/add | solution.py:118
  27.8 1.6 %collective-permute-start.1 = (f32[3,256,128]{2,1,0:T(8,128)S(1)}, f32[3,256,128]{2,1,0:T(8,128)}, u32[]{:S(2)}, u32[]{:S(2)}) collective-permute-start(f32[3,256,128]{2,1,0:T(8,128)S(1)} %fusion.5), channel_id=1, source_target_pairs={{0,32},{16,48},{32,0},{48,16},{64,96},{80,112},{96,64},{112,80},{1... | collective-permute-start | bytes 1179656 | tf_op jit(solution)/shard_map/ppermute | solution.py:15
  29.3 6.5 %fusion = bf16[2048,128]{0,1:T(8,128)(2,1)S(1)} fusion(bf16[2048,128]{1,0:T(8,128)(2,1)} %bitcast.40, bf16[2048,2048]{1,0:T(8,128)(2,1)} %param.15), kind=kOutput, calls=%fused_computation.4 | convolution fusion | flops 1074003968 | bytes 9437184 | tf_op jit(solution)/shard_map/dot_general | solution.py:103
  35.8 1.0 %copy.11 = bf16[2048,128]{1,0:T(8,128)(2,1)} copy(bf16[2048,128]{0,1:T(8,128)(2,1)S(1)} %fusion) | data formatting | bytes 1048576 | tf_op jit(solution)/shard_map/convert_element_type | solution.py:106
  36.8 13.7 %shard_map.101 = bf16[16,128,128]{2,1,0:T(8,128)(2,1)} custom-call(bf16[16,128,128]{2,1,0:T(8,128)(2,1)} %bitcast.42), custom_call_target="tpu_custom_call" | custom-call | tf_op jit(solution)/shard_map/pallas_call | solution.py:59
  50.5 1.7 %gather_fusion.1 = bf16[16,128,128]{2,1,0:T(8,128)(2,1)S(1)} fusion(bf16[16,128,128]{2,1,0:T(8,128)(2,1)} %shard_map.101, s32[1024]{0:T(1024)S(1)} %pad_clamp_fusion), kind=kCustom, calls=%fused_computation.1.clone | custom fusion | bytes 1048640 | tf_op jit(solution)/shard_map/jit(_take)/gather | solution.py:108
  52.2 0.0 copy-start.1
  52.2 0.0 collective-permute-done.1
  52.2 1.1 %slice_add_fusion = f32[2,256,128]{2,1,0:T(8,128)S(1)} fusion(f32[3,256,128]{2,1,0:T(8,128)} %collective-permute-done.1, f32[3,256,128]{2,1,0:T(8,128)S(1)} %fusion.5), kind=kLoop, calls=%fused_computation.19 | loop fusion | flops 65536 | bytes 786432 | tf_op jit(solution)/shard_map/add | solution.py:118
  53.4 2.8 %collective-permute-start.2 = (f32[2,256,128]{2,1,0:T(8,128)S(1)}, f32[2,256,128]{2,1,0:T(8,128)S(1)}, u32[]{:S(2)}, u32[]{:S(2)}) collective-permute-start(f32[2,256,128]{2,1,0:T(8,128)S(1)} %slice_add_fusion), channel_id=1, source_target_pairs={{0,64},{16,80},{32,96},{48,112},{64,0},{80,16},{96,32},{112,48},{1... | collective-permute-start | bytes 786440 | tf_op jit(solution)/shard_map/ppermute | solution.py:15
  56.2 0.0 copy-done
  56.2 0.7 fusion.15
  56.9 4.4 %collective-permute-done.2 = f32[2,256,128]{2,1,0:T(8,128)S(1)} collective-permute-done((f32[2,256,128]{2,1,0:T(8,128)S(1)}, f32[2,256,128]{2,1,0:T(8,128)S(1)}, u32[]{:S(2)}, u32[]{:S(2)}) %collective-permute-start.2) | collective-permute-done | bytes 262176 | tf_op jit(solution)/shard_map/ppermute | solution.py:15
  61.3 0.6 collective-permute-start.3
  62.0 4.4 %collective-permute-done.3 = f32[256,128]{1,0:T(8,128)S(1)} collective-permute-done((f32[256,128]{1,0:T(8,128)S(1)}, f32[256,128]{1,0:T(8,128)S(1)}, u32[]{:S(2)}, u32[]{:S(2)}) %collective-permute-start.3) | collective-permute-done | bytes 131104 | tf_op jit(solution)/shard_map/ppermute | solution.py:15
  66.4 3.8 %collective-permute-start.4 = (f32[256,128]{1,0:T(8,128)S(1)}, f32[256,128]{1,0:T(8,128)S(1)}, u32[]{:S(2)}, u32[]{:S(2)}) collective-permute-start(f32[256,128]{1,0:T(8,128)S(1)} %add.38), channel_id=1, source_target_pairs={{0,2},{1,3},{2,0},{3,1},{4,6},{5,7},{6,4},{7,5},{8,10},{9,11},{10,... | collective-permute-start | bytes 393224 | tf_op jit(solution)/shard_map/ppermute | solution.py:15
  70.2 0.1 broadcast_select_fusion
  70.3 0.0 copy-start.2
  70.4 2.8 %collective-permute-done.4 = f32[256,128]{1,0:T(8,128)S(1)} collective-permute-done((f32[256,128]{1,0:T(8,128)S(1)}, f32[256,128]{1,0:T(8,128)S(1)}, u32[]{:S(2)}, u32[]{:S(2)}) %collective-permute-start.4) | collective-permute-done | bytes 131104 | tf_op jit(solution)/shard_map/ppermute | solution.py:15
  73.2 0.1 collective-permute-start.5
  73.3 0.0 copy-done.1
  73.3 0.0 copy-start.3
  73.3 1.3 %fusion.2 = f32[1024,128]{1,0:T(8,128)S(1)} fusion(f32[1024,128]{1,0:T(8,128)S(1)} %fusion.15, bf16[1024,2048]{1,0:T(8,128)(2,1)S(1)} %copy-done.1, bf16[2048,128]{1,0:T(8,128)(2,1)S(1)} %bitcast.41), kind=kOutput, calls=%fused_computation.9 | convolution fusion | flops 537001984 | bytes 5767168 | tf_op jit(solution)/shard_map/dot_general | solution.py:109
  74.6 0.9 %slice.73 = bf16[1,256,128]{2,1,0:T(8,128)(2,1)S(1)} slice(f32[4,256,128]{2,1,0:T(8,128)} %collective-permute-done), slice={[0:1], [0:256], [0:128]} | slice | bytes 131072 | tf_op jit(solution)/shard_map/slice | solution.py:116
  75.5 0.9 %slice.72 = bf16[1,256,128]{2,1,0:T(8,128)(2,1)S(1)} slice(f32[3,256,128]{2,1,0:T(8,128)} %collective-permute-done.1), slice={[0:1], [0:256], [0:128]} | slice | bytes 131072 | tf_op jit(solution)/shard_map/slice | solution.py:116
  76.4 2.5 %collective-permute-done.5 = f32[256,128]{1,0:T(8,128)S(1)} collective-permute-done((f32[256,128]{1,0:T(8,128)S(1)}, f32[256,128]{1,0:T(8,128)S(1)}, u32[]{:S(2)}, u32[]{:S(2)}) %collective-permute-start.5) | collective-permute-done | bytes 131104 | tf_op jit(solution)/shard_map/ppermute | solution.py:15
  78.9 2.0 %collective-permute-start.6 = (f32[256,128]{1,0:T(8,128)S(1)}, f32[256,128]{1,0:T(8,128)S(1)}, u32[]{:S(2)}, u32[]{:S(2)}) collective-permute-start(f32[256,128]{1,0:T(8,128)S(1)} %add.40), channel_id=1, source_target_pairs={{0,8},{1,9},{2,10},{3,11},{4,12},{5,13},{6,14},{7,15},{8,0},{9,1},... | collective-permute-start | bytes 393224 | tf_op jit(solution)/shard_map/ppermute | solution.py:15
  80.9 0.0 copy-done.2
  80.9 0.6 fusion.3
  81.5 4.0 %collective-permute-done.6 = f32[256,128]{1,0:T(8,128)S(1)} collective-permute-done((f32[256,128]{1,0:T(8,128)S(1)}, f32[256,128]{1,0:T(8,128)S(1)}, u32[]{:S(2)}, u32[]{:S(2)}) %collective-permute-start.6) | collective-permute-done | bytes 131104 | tf_op jit(solution)/shard_map/ppermute | solution.py:15
  85.5 0.0 copy-done.3
  85.5 1.1 %fusion.1 = f32[1024,128]{1,0:T(8,128)} fusion(f32[1024,128]{1,0:T(8,128)S(1)} %fusion.3, bf16[1024,256]{1,0:T(8,128)(2,1)S(1)} %copy-done.3, f32[256,128]{1,0:T(8,128)S(1)} %add.40, f32[256,128]{1,0:T(8,128)S(1)} %collective-permute-done.6), kind=kOutput, calls=%fused_computation.7 | convolution fusion | flops 67305472 | bytes 1835008 | tf_op jit(solution)/shard_map/dot_general | solution.py:130
  (12 shorter events, 0.1 us)
Async XLA Ops:
  0.0 56.2 %copy-start = (bf16[1024,1024]{1,0:T(8,128)(2,1)S(1)}, bf16[1024,1024]{1,0:T(8,128)(2,1)}, u32[]{:S(2)}) copy-start(bf16[1024,1024]{1,0:T(8,128)(2,1)} %param.13) | copy-start | bytes 6291460
  0.0 5.8 %copy-start.4 = (bf16[1024,2048]{1,0:T(8,128)(2,1)S(1)}, bf16[1024,2048]{1,0:T(8,128)(2,1)}, u32[]{:S(2)}) copy-start(bf16[1024,2048]{1,0:T(8,128)(2,1)} %param.14) | copy-start | bytes 12582916
  3.6 4.4 %copy-start.5 = (s32[16]{0:T(128)S(1)}, s32[16]{0:T(128)}, u32[]{:S(2)}) copy-start(s32[16]{0:T(128)} %param.21) | copy-start | bytes 196
  5.8 20.9 %collective-permute-start = (f32[4,256,128]{2,1,0:T(8,128)}, f32[4,256,128]{2,1,0:T(8,128)}, u32[]{:S(2)}, u32[]{:S(2)}) collective-permute-start(f32[4,256,128]{2,1,0:T(8,128)} %pad_maximum_fusion), channel_id=1, source_target_pairs={{0,16},{16,0},{32,48},{48,32},{64,80},{80,64},{96,112},{112,96},{1... | collective-permute-start | bytes 1572872 | tf_op jit(solution)/shard_map/ppermute | solution.py:15
  27.8 24.5 %collective-permute-start.1 = (f32[3,256,128]{2,1,0:T(8,128)S(1)}, f32[3,256,128]{2,1,0:T(8,128)}, u32[]{:S(2)}, u32[]{:S(2)}) collective-permute-start(f32[3,256,128]{2,1,0:T(8,128)S(1)} %fusion.5), channel_id=1, source_target_pairs={{0,32},{16,48},{32,0},{48,16},{64,96},{80,112},{96,64},{112,80},{1... | collective-permute-start | bytes 1179656 | tf_op jit(solution)/shard_map/ppermute | solution.py:15
  52.2 21.1 %copy-start.1 = (bf16[1024,2048]{1,0:T(8,128)(2,1)S(1)}, bf16[1024,2048]{1,0:T(8,128)(2,1)}, u32[]{:S(2)}) copy-start(bf16[1024,2048]{1,0:T(8,128)(2,1)} %param.16) | copy-start | bytes 12582916
  53.4 8.0 %collective-permute-start.2 = (f32[2,256,128]{2,1,0:T(8,128)S(1)}, f32[2,256,128]{2,1,0:T(8,128)S(1)}, u32[]{:S(2)}, u32[]{:S(2)}) collective-permute-start(f32[2,256,128]{2,1,0:T(8,128)S(1)} %slice_add_fusion), channel_id=1, source_target_pairs={{0,64},{16,80},{32,96},{48,112},{64,0},{80,16},{96,32},{112,48},{1... | collective-permute-start | bytes 786440 | tf_op jit(solution)/shard_map/ppermute | solution.py:15
  61.3 5.0 %collective-permute-start.3 = (f32[256,128]{1,0:T(8,128)S(1)}, f32[256,128]{1,0:T(8,128)S(1)}, u32[]{:S(2)}, u32[]{:S(2)}) collective-permute-start(f32[256,128]{1,0:T(8,128)S(1)} %fusion.13), channel_id=1, source_target_pairs={{0,1},{1,0},{2,3},{3,2},{4,5},{5,4},{6,7},{7,6},{8,9},{9,8},{10,11... | collective-permute-start | bytes 393224 | tf_op jit(solution)/shard_map/ppermute | solution.py:15
  66.4 6.8 %collective-permute-start.4 = (f32[256,128]{1,0:T(8,128)S(1)}, f32[256,128]{1,0:T(8,128)S(1)}, u32[]{:S(2)}, u32[]{:S(2)}) collective-permute-start(f32[256,128]{1,0:T(8,128)S(1)} %add.38), channel_id=1, source_target_pairs={{0,2},{1,3},{2,0},{3,1},{4,6},{5,7},{6,4},{7,5},{8,10},{9,11},{10,... | collective-permute-start | bytes 393224 | tf_op jit(solution)/shard_map/ppermute | solution.py:15
  70.3 10.6 %copy-start.2 = (bf16[3,1024,256]{2,1,0:T(8,128)(2,1)S(1)}, bf16[3,1024,256]{2,1,0:T(8,128)(2,1)}, u32[]{:S(2)}) copy-start(bf16[3,1024,256]{2,1,0:T(8,128)(2,1)} %param.18) | copy-start | bytes 4718596
  73.2 5.7 %collective-permute-start.5 = (f32[256,128]{1,0:T(8,128)S(1)}, f32[256,128]{1,0:T(8,128)S(1)}, u32[]{:S(2)}, u32[]{:S(2)}) collective-permute-start(f32[256,128]{1,0:T(8,128)S(1)} %add.39), channel_id=1, source_target_pairs={{0,4},{1,5},{2,6},{3,7},{4,0},{5,1},{6,2},{7,3},{8,12},{9,13},{10,... | collective-permute-start | bytes 393224 | tf_op jit(solution)/shard_map/ppermute | solution.py:15
  73.3 12.2 %copy-start.3 = (bf16[1024,256]{1,0:T(8,128)(2,1)S(1)}, bf16[1024,256]{1,0:T(8,128)(2,1)}, u32[]{:S(2)}) copy-start(bf16[1024,256]{1,0:T(8,128)(2,1)} %param.20) | copy-start | bytes 1572868
  78.9 6.6 %collective-permute-start.6 = (f32[256,128]{1,0:T(8,128)S(1)}, f32[256,128]{1,0:T(8,128)S(1)}, u32[]{:S(2)}, u32[]{:S(2)}) collective-permute-start(f32[256,128]{1,0:T(8,128)S(1)} %add.40), channel_id=1, source_target_pairs={{0,8},{1,9},{2,10},{3,11},{4,12},{5,13},{6,14},{7,15},{8,0},{9,1},... | collective-permute-start | bytes 393224 | tf_op jit(solution)/shard_map/ppermute | solution.py:15

commit v3 on v1

--- a/solution.py
+++ b/solution.py
@@ -1,13 +1,163 @@
+import functools
+
 import jax
 import jax.numpy as jnp
 from jax import lax
+from jax.experimental import pallas as pl
+from jax.experimental.pallas import tpu as pltpu
 from jax.sharding import PartitionSpec as P
 
 contract_first = (((0,), (0,)), ((), ()))
+MESH_ID = pl.DeviceIdType.MESH
 
 
 def swapped(x, axis, bit):
     return lax.ppermute(x, axis, [(i, i ^ 1 << bit) for i in range(lax.axis_size(axis))])
+
+
+def col_peers(n):
+    me = lax.axis_index("col")
+    return [(s, lax.rem(me + s, n), lax.rem(me + n - s, n)) for s in range(1, n)]
+
+
+def scatter_kernel(n, x_ref, r_ref, o_ref, share_ref, got, sems, local_sems):
+    me = lax.axis_index("col")
+    row = lax.axis_index("row")
+    barrier = pltpu.get_barrier_semaphore()
+    for s, peer, _ in col_peers(n):
+        pl.semaphore_signal(barrier, inc=1, device_id=(row, peer), device_id_type=MESH_ID)
+    pl.semaphore_wait(barrier, n - 1)
+
+    local = pltpu.make_async_copy(x_ref.at[me], o_ref.at[me], local_sems.at[0])
+    local.start()
+    own = pltpu.make_async_copy(r_ref.at[me], got.at[me], local_sems.at[1])
+    own.start()
+
+    def piece(s, peer, slot):
+        return pltpu.make_async_remote_copy(
+            src_ref=x_ref.at[peer], dst_ref=o_ref.at[slot],
+            send_sem=sems.at[0, s], recv_sem=sems.at[1, s],
+            device_id=(row, peer), device_id_type=MESH_ID,
+        )
+
+    def share(s, peer, slot):
+        return pltpu.make_async_remote_copy(
+            src_ref=r_ref.at[peer], dst_ref=got.at[slot],
+            send_sem=sems.at[2, s], recv_sem=sems.at[3, s],
+            device_id=(row, peer), device_id_type=MESH_ID,
+        )
+
+    for s, peer, _ in col_peers(n):
+        share(s, peer, me).start()
+        piece(s, peer, me).start()
+    for s, peer, source in col_peers(n):
+        share(s, peer, me).wait_send()
+        share(s, source, source).wait_recv()
+    own.wait()
+    share_ref[...] = jnp.sum(got[...], axis=0)
+    for s, peer, source in col_peers(n):
+        piece(s, peer, me).wait_send()
+        piece(s, source, source).wait_recv()
+    local.wait()
+
+
+def scatter(x, r):
+    n = x.shape[0]
+    return pl.pallas_call(
+        functools.partial(scatter_kernel, n),
+        out_shape=(
+            jax.ShapeDtypeStruct(x.shape, x.dtype),
+            jax.ShapeDtypeStruct(r.shape[1:], r.dtype),
+        ),
+        in_specs=[pl.BlockSpec(memory_space=pl.ANY), pl.BlockSpec(memory_space=pltpu.VMEM)],
+        out_specs=(pl.BlockSpec(memory_space=pl.ANY), pl.BlockSpec(memory_space=pltpu.VMEM)),
+        scratch_shapes=[
+            pltpu.VMEM(r.shape, r.dtype),
+            pltpu.SemaphoreType.DMA((4, n)),
+            pltpu.SemaphoreType.DMA((2,)),
+        ],
+        compiler_params=pltpu.CompilerParams(collective_id=0, has_side_effects=True),
+    )(x, r)
+
+
+def gather_kernel(n, m, x_ref, share_ref, o_ref, full_ref, rows_got, total, sems, row_sems, local_sems):
+    me = lax.axis_index("col")
+    row = lax.axis_index("row")
+    row_peers = [(s, lax.rem(row + s, m), lax.rem(row + m - s, m)) for s in range(1, m)]
+    barrier = pltpu.get_barrier_semaphore()
+    for s, peer, _ in col_peers(n):
+        pl.semaphore_signal(barrier, inc=1, device_id=(row, peer), device_id_type=MESH_ID)
+    for s, peer, _ in row_peers:
+        pl.semaphore_signal(barrier, inc=1, device_id=(peer, me), device_id_type=MESH_ID)
+    pl.semaphore_wait(barrier, n - 1 + m - 1)
+
+    local = pltpu.make_async_copy(x_ref.at[me], o_ref.at[me], local_sems.at[0])
+    local.start()
+    own = pltpu.make_async_copy(share_ref, rows_got.at[row], local_sems.at[1])
+    own.start()
+
+    def piece(s, peer, slot):
+        return pltpu.make_async_remote_copy(
+            src_ref=x_ref.at[peer], dst_ref=o_ref.at[slot],
+            send_sem=sems.at[0, s], recv_sem=sems.at[1, s],
+            device_id=(row, peer), device_id_type=MESH_ID,
+        )
+
+    def part(s, peer, slot):
+        return pltpu.make_async_remote_copy(
+            src_ref=share_ref, dst_ref=rows_got.at[slot],
+            send_sem=row_sems.at[0, s], recv_sem=row_sems.at[1, s],
+            device_id=(peer, me), device_id_type=MESH_ID,
+        )
+
+    def spread(s, peer, slot):
+        return pltpu.make_async_remote_copy(
+            src_ref=total, dst_ref=full_ref.at[slot],
+            send_sem=sems.at[2, s], recv_sem=sems.at[3, s],
+            device_id=(row, peer), device_id_type=MESH_ID,
+        )
+
+    for s, peer, _ in row_peers:
+        part(s, peer, row).start()
+    for s, peer, _ in col_peers(n):
+        piece(s, peer, me).start()
+    for s, peer, source in row_peers:
+        part(s, peer, row).wait_send()
+        part(s, source, source).wait_recv()
+    own.wait()
+    total[...] = jnp.sum(rows_got[...], axis=0)
+    mine = pltpu.make_async_copy(total, full_ref.at[me], local_sems.at[2])
+    mine.start()
+    for s, peer, _ in col_peers(n):
+        spread(s, peer, me).start()
+    for s, peer, source in col_peers(n):
+        spread(s, peer, me).wait_send()
+        spread(s, source, source).wait_recv()
+        piece(s, peer, me).wait_send()
+        piece(s, source, source).wait_recv()
+    mine.wait()
+    local.wait()
+
+
+def gather(x, share, m):
+    n = x.shape[0]
+    return pl.pallas_call(
+        functools.partial(gather_kernel, n, m),
+        out_shape=(
+            jax.ShapeDtypeStruct(x.shape, x.dtype),
+            jax.ShapeDtypeStruct((n,) + share.shape, share.dtype),
+        ),
+        in_specs=[pl.BlockSpec(memory_space=pl.ANY), pl.BlockSpec(memory_space=pltpu.VMEM)],
+        out_specs=(pl.BlockSpec(memory_space=pl.ANY), pl.BlockSpec(memory_space=pltpu.VMEM)),
+        scratch_shapes=[
+            pltpu.VMEM((m,) + share.shape, share.dtype),
+            pltpu.VMEM(share.shape, share.dtype),
+            pltpu.SemaphoreType.DMA((4, n)),
+            pltpu.SemaphoreType.DMA((2, m)),
+            pltpu.SemaphoreType.DMA((3,)),
+        ],
+        compiler_params=pltpu.CompilerParams(collective_id=1, has_side_effects=True),
+    )(x, share)
 
 
 def per_device(
@@ -24,6 +174,12 @@
 ):
     lowered = right_side.astype(jnp.bfloat16)
     columns = lowered.shape[1]
+    root_term = lax.dot_general(
+        root_project, lowered, contract_first, preferred_element_type=jnp.float32
+    )
+    level_coeffs = jnp.einsum(
+        "blr,lw->brw", row_project, lowered, preferred_element_type=jnp.float32
+    )
     dense_part = jnp.dot(leaf_inverse, lowered, preferred_element_type=jnp.float32)
     coeffs = lax.dot_general(
         compress, lowered, contract_first, preferred_element_type=jnp.float32
@@ -32,21 +188,17 @@
     pieces = coeffs.reshape(col_count, -1, columns)
     inverse = jnp.argsort(owner_map)
     outgoing = jnp.take(pieces, inverse, axis=0)
-    arrived = lax.all_to_all(outgoing, "col", split_axis=0, concat_axis=0, tiled=True)
+    root_shares = root_term.reshape(col_count, -1, columns)
+    arrived, root_share = scatter(outgoing, root_shares)
     shape_now = arrived.shape
     mixed_rows = jnp.dot(
         middle, arrived.reshape(-1, shape_now[2]), preferred_element_type=jnp.float32
     )
     mixed_rows = mixed_rows.astype(jnp.bfloat16).reshape(shape_now)
-    returned = lax.all_to_all(mixed_rows, "col", split_axis=0, concat_axis=0, tiled=True)
+    returned, root_full = gather(mixed_rows, root_share, lax.axis_size("row"))
     ordered = jnp.take(returned, owner_map, axis=0).reshape(-1, columns)
     cluster_part = jnp.dot(expand, ordered, preferred_element_type=jnp.float32)
-    level_coeffs = jnp.einsum(
-        "blr,lw->brw", row_project, lowered, preferred_element_type=jnp.float32
-    )
-    root_term = lax.dot_general(
-        root_project, lowered, contract_first, preferred_element_type=jnp.float32
-    )
+
     levels = lax.axis_size("row").bit_length() - 1
     running = level_coeffs
     siblings = []
@@ -57,7 +209,7 @@
             [running[: level_bit + 1], running[level_bit + 1 :] + partner[1:]], axis=0
         )
     sibling_sum = jnp.stack(siblings, axis=0)
-    root_sum = jnp.sum(lax.all_gather(lax.psum(root_term, "row"), "col", axis=0), axis=0)
+    root_sum = root_full.reshape(-1, columns)
     coupled = jnp.einsum(
         "blr,brw->lw",
         row_expand,

time: 140 us -> 80.3 us (0.57)
  the two profiles are of different devices: /device:TPU:6 before, /device:TPU:0 now
where the time goes in v3:
time: 80.3 us; the launch traced here: 79.9 us
  Pallas kernels  37.5 us (47%)
  matrix products  18.5 us (23%)
  waiting for transfers between devices  8.93 us (11%)
  other arithmetic  7.61 us (9%)
  local copies, waits for them, and re-layouts  5.32 us (7%)
  starting transfers between devices  1.86 us (2%)
    pallas_call x1, Pallas kernels, gather(): pl.pallas_call(functools.partial(gather_kernel, n, m), out_shape=(jax.Sha...  19.6 us
    pallas_call x1, Pallas kernels, scatter(): pl.pallas_call(functools.partial(scatter_kernel, n), out_shape=(jax.Shape...  17.9 us
    ppermute x3, waiting for transfers between devices, swapped(): lax.ppermute(x, axis, [(i, i ^ 1 << bit) for i in range(lax.axis_size(axi...  8.93 us
    dot_general x1, matrix products, per_device(): jnp.dot(middle, arrived.reshape(-1, shape_now[2]), preferred_element_type...  6.48 us
    dot_general x1, matrix products, per_device(): lax.dot_general(compress, lowered, contract_first, preferred_element_type...  4.29 us
    dot_general x1, matrix products, per_device(): lax.dot_general(root_project, lowered, contract_first, preferred_element_...  2.05 us
    dot_general x1, matrix products, per_device(): jnp.einsum('blr,lw->brw', row_project, lowered, preferred_element_type=jn...  2.02 us
    sort x1, other arithmetic, per_device(): inverse = jnp.argsort(owner_map)  1.9 us
  transfers between devices with their start and end apart: 3, of which 2 were waited for; matrix products, arithmetic and copies ran while one was open for 32% of the time, Pallas kernels for 47%

profile of v3, /device:TPU:0, one launch (start us, length us, event | category | flops | bytes accessed | tf_op | source)
XLA Modules:
  0.0 79.9 jit_solution(10201175991436406166)
XLA Ops:
  0.0 0.0 copy-start
  0.0 1.2 %convert_element_type.19 = bf16[1024,128]{1,0:T(8,128)(2,1)S(1)} convert(f32[1024,128]{1,0:T(8,128)} %param.12) | non-fusion elementwise | flops 131072 | bytes 786432 | tf_op jit(solution)/shard_map/convert_element_type | solution.py:175
  1.2 2.0 %fusion.4 = f32[3,256,128]{2,1,0:T(8,128)S(1)} fusion(bf16[3,1024,256]{2,1,0:T(8,128)(2,1)} %param.17, bf16[1024,128]{1,0:T(8,128)(2,1)S(1)} %convert_element_type.19), kind=kOutput, calls=%fused_computation.14 | convolution fusion | flops 201326592 | bytes 2228224 | tf_op jit(solution)/shard_map/blr,lw->brw/dot_general | solution.py:180
  3.2 0.1 collective-permute-start
  3.3 0.7 compare_and_fusion
  4.0 0.7 compare_select_fusion
  4.7 1.9 %sort.17 = (s32[16]{0:T(128)}, s32[16]{0:T(128)S(1)}) sort(s32[16]{0:T(128)} %param.21, s32[16]{0:T(128)S(1)} %iota.4), dimensions={0}, to_apply=%region_0.0 | sort | flops 64 | bytes 256 | tf_op jit(solution)/shard_map/jit(argsort)/sort | solution.py:189
  6.6 2.0 %fusion.14 = f32[256,128]{1,0:T(8,128)} fusion(bf16[1024,256]{1,0:T(8,128)(2,1)} %param.19, bf16[1024,128]{1,0:T(8,128)(2,1)S(1)} %convert_element_type.19), kind=kOutput, calls=%fused_computation.33 | convolution fusion | flops 67108864 | bytes 917504 | tf_op jit(solution)/shard_map/dot_general | solution.py:177
  8.6 4.3 %convolution_convert_fusion.1 = bf16[2048,128]{1,0:T(8,128)(2,1)} fusion(bf16[1024,2048]{1,0:T(8,128)(2,1)} %param.14, bf16[1024,128]{1,0:T(8,128)(2,1)S(1)} %convert_element_type.19), kind=kOutput, calls=%fused_computation.3 | convolution fusion | flops 537133056 | bytes 4980736 | tf_op jit(solution)/shard_map/dot_general | solution.py:184
  12.9 1.7 %gather_fusion = bf16[16,128,128]{2,1,0:T(8,128)(2,1)S(1)} fusion(bf16[16,128,128]{2,1,0:T(8,128)(2,1)} %bitcast.43, s32[1024]{0:T(1024)S(1)} %pad_clamp_fusion.1), kind=kCustom, calls=%fused_computation.clone | custom fusion | bytes 1048640 | tf_op jit(solution)/shard_map/jit(_take)/gather | solution.py:190
  14.6 0.9 %broadcast_select_fusion.1.x_ref = bf16[16,128,128]{2,1,0:T(8,128)(2,1)} fusion(bf16[16,128,128]{2,1,0:T(8,128)(2,1)S(1)} %gather_fusion, pred[16]{0:T(512)(128)(4,1)S(1)} %compare_and_fusion.1), kind=kLoop, calls=%fused_computation.12 | loop fusion | flops 262144 | bytes 1048592 | tf_op jit(solution)/shard_map/jit(_take)/select_n | solution.py:190
  15.5 17.9 %shard_map.100 = (bf16[16,128,128]{2,1,0:T(8,128)(2,1)}, f32[16,128]{1,0:T(8,128)}) custom-call(bf16[16,128,128]{2,1,0:T(8,128)(2,1)} %broadcast_select_fusion.1.x_ref, f32[16,16,128]{2,1,0:T(8,128)} %bitcast.42), custom_call_target="tpu_custom_call" | custom-call | tf_op jit(solution)/shard_map/pallas_call | solution.py:66
  33.4 6.5 %fusion = bf16[2048,128]{0,1:T(8,128)(2,1)S(1)} fusion(bf16[2048,128]{1,0:T(8,128)(2,1)} %bitcast.41, bf16[2048,2048]{1,0:T(8,128)(2,1)} %param.15), kind=kOutput, calls=%fused_computation.4 | convolution fusion | flops 1074003968 | bytes 9437184 | tf_op jit(solution)/shard_map/dot_general | solution.py:194
  39.9 1.0 %copy.11 = bf16[2048,128]{1,0:T(8,128)(2,1)} copy(bf16[2048,128]{0,1:T(8,128)(2,1)S(1)} %fusion) | data formatting | bytes 1048576 | tf_op jit(solution)/shard_map/convert_element_type | solution.py:197
  40.9 19.6 %shard_map.101 = (bf16[16,128,128]{2,1,0:T(8,128)(2,1)}, f32[16,16,128]{2,1,0:T(8,128)}) custom-call(bf16[16,128,128]{2,1,0:T(8,128)(2,1)} %bitcast.40, f32[16,128]{1,0:T(8,128)} %get-tuple-element.13.share_ref), custom_call_target="tpu_custom_call" | custom-call | tf_op jit(solution)/shard_map/pallas_call | solution.py:144
  60.6 1.7 %gather_fusion.1 = bf16[16,128,128]{2,1,0:T(8,128)(2,1)S(1)} fusion(bf16[16,128,128]{2,1,0:T(8,128)(2,1)} %get-tuple-element.14, s32[1024]{0:T(1024)S(1)} %pad_clamp_fusion), kind=kCustom, calls=%fused_computation.1.clone | custom fusion | bytes 1048640 | tf_op jit(solution)/shard_map/jit(_take)/gather | solution.py:199
  62.3 0.0 copy-start.1
  62.3 0.1 broadcast_select_fusion
  62.4 1.1 %convert_element_type.23 = bf16[16,16,128]{2,1,0:T(8,128)(2,1)S(1)} convert(f32[16,16,128]{2,1,0:T(8,128)} %get-tuple-element.15) | non-fusion elementwise | flops 32768 | bytes 196608 | tf_op jit(solution)/shard_map/convert_element_type | solution.py:220
  63.5 0.0 copy-done
  63.5 0.7 fusion.13
  64.2 0.0 copy-start.3
  64.2 0.0 collective-permute-done
  64.2 1.0 %slice_add_fusion = f32[2,256,128]{2,1,0:T(8,128)S(1)} fusion(f32[3,256,128]{2,1,0:T(8,128)} %collective-permute-done, f32[3,256,128]{2,1,0:T(8,128)S(1)} %fusion.4), kind=kLoop, calls=%fused_computation.13 | loop fusion | flops 65536 | bytes 786432 | tf_op jit(solution)/shard_map/add | solution.py:209
  65.2 0.7 collective-permute-start.1
  65.9 0.0 copy-done.1
  65.9 0.0 copy-start.2
  65.9 1.3 %fusion.1 = f32[1024,128]{1,0:T(8,128)S(1)} fusion(f32[1024,128]{1,0:T(8,128)S(1)} %fusion.13, bf16[1024,2048]{1,0:T(8,128)(2,1)S(1)} %copy-done.1, bf16[2048,128]{1,0:T(8,128)(2,1)S(1)} %bitcast.39), kind=kOutput, calls=%fused_computation.8 | convolution fusion | flops 537001984 | bytes 5767168 | tf_op jit(solution)/shard_map/dot_general | solution.py:200
  67.2 5.4 %collective-permute-done.1 = f32[2,256,128]{2,1,0:T(8,128)S(1)} collective-permute-done((f32[2,256,128]{2,1,0:T(8,128)S(1)}, f32[2,256,128]{2,1,0:T(8,128)S(1)}, u32[]{:S(2)}, u32[]{:S(2)}) %collective-permute-start.1) | collective-permute-done | bytes 262176 | tf_op jit(solution)/shard_map/ppermute | solution.py:15
  72.6 1.1 %collective-permute-start.2 = (bf16[1,256,128]{2,1,0:T(8,128)(2,1)S(1)}, bf16[1,256,128]{2,1,0:T(8,128)(2,1)S(1)}, u32[]{:S(2)}, u32[]{:S(2)}) collective-permute-start(bf16[1,256,128]{2,1,0:T(8,128)(2,1)S(1)} %get-tuple-element.17), channel_id=1, source_target_pairs={{0,64},{16,80},{32,96},{48,112},{64,0},{80,16},{96,32},{112,48},{1... | collective-permute-start | bytes 196616 | tf_op jit(solution)/shard_map/ppermute | solution.py:15
  73.7 0.0 copy-done.3
  73.7 0.3 convolution_bitcast_fusion
  74.0 0.9 %slice.43 = bf16[1,256,128]{2,1,0:T(8,128)(2,1)S(1)} slice(f32[3,256,128]{2,1,0:T(8,128)} %collective-permute-done), slice={[0:1], [0:256], [0:128]} | slice | bytes 131072 | tf_op jit(solution)/shard_map/slice | solution.py:207
  74.9 3.5 %collective-permute-done.2 = bf16[1,256,128]{2,1,0:T(8,128)(2,1)S(1)} collective-permute-done((bf16[1,256,128]{2,1,0:T(8,128)(2,1)S(1)}, bf16[1,256,128]{2,1,0:T(8,128)(2,1)S(1)}, u32[]{:S(2)}, u32[]{:S(2)}) %collective-permute-start.2) | collective-permute-done | bytes 65568 | tf_op jit(solution)/shard_map/ppermute | solution.py:15
  78.5 0.0 copy-done.2
  78.5 1.4 %fusion.3 = f32[1024,128]{1,0:T(8,128)} fusion(f32[1024,128]{1,0:T(8,128)S(1)} %convolution_bitcast_fusion, f32[1024,128]{1,0:T(8,128)S(1)} %fusion.1, bf16[3,1024,256]{2,1,0:T(8,128)(2,1)S(1)} %copy-done.2, bf16[1,256,128]{2,1,0:T(8,128)(2,1)S(1)} %collective-permute-done.2, bf16[1,256,128]{2,1,0:T(8,128)(2,1)S(1)} %get-tuple-element.16, ...), kind=kOutput, calls=%fused_computation.10 | convolution fusion | flops 201785344 | bytes 3342336 | tf_op jit(solution)/shard_map/blr,brw->lw/dot_general | solution.py:213
  (6 shorter events, 0.1 us)
Async XLA Ops:
  0.0 63.5 %copy-start = (bf16[1024,1024]{1,0:T(8,128)(2,1)S(1)}, bf16[1024,1024]{1,0:T(8,128)(2,1)}, u32[]{:S(2)}) copy-start(bf16[1024,1024]{1,0:T(8,128)(2,1)} %param.13) | copy-start | bytes 6291460
  3.2 60.9 %collective-permute-start = (f32[3,256,128]{2,1,0:T(8,128)S(1)}, f32[3,256,128]{2,1,0:T(8,128)}, u32[]{:S(2)}, u32[]{:S(2)}) collective-permute-start(f32[3,256,128]{2,1,0:T(8,128)S(1)} %fusion.4), channel_id=1, source_target_pairs={{0,16},{16,0},{32,48},{48,32},{64,80},{80,64},{96,112},{112,96},{1... | collective-permute-start | bytes 1179656 | tf_op jit(solution)/shard_map/ppermute | solution.py:15
  62.3 3.7 %copy-start.1 = (bf16[1024,2048]{1,0:T(8,128)(2,1)S(1)}, bf16[1024,2048]{1,0:T(8,128)(2,1)}, u32[]{:S(2)}) copy-start(bf16[1024,2048]{1,0:T(8,128)(2,1)} %param.16) | copy-start | bytes 12582916
  64.2 9.6 %copy-start.3 = (bf16[1024,256]{1,0:T(8,128)(2,1)S(1)}, bf16[1024,256]{1,0:T(8,128)(2,1)}, u32[]{:S(2)}) copy-start(bf16[1024,256]{1,0:T(8,128)(2,1)} %param.20) | copy-start | bytes 1572868
  65.2 7.4 %collective-permute-start.1 = (f32[2,256,128]{2,1,0:T(8,128)S(1)}, f32[2,256,128]{2,1,0:T(8,128)S(1)}, u32[]{:S(2)}, u32[]{:S(2)}) collective-permute-start(f32[2,256,128]{2,1,0:T(8,128)S(1)} %slice_add_fusion), channel_id=1, source_target_pairs={{0,32},{16,48},{32,0},{48,16},{64,96},{80,112},{96,64},{112,80},{1... | collective-permute-start | bytes 786440 | tf_op jit(solution)/shard_map/ppermute | solution.py:15
  65.9 12.6 %copy-start.2 = (bf16[3,1024,256]{2,1,0:T(8,128)(2,1)S(1)}, bf16[3,1024,256]{2,1,0:T(8,128)(2,1)}, u32[]{:S(2)}) copy-start(bf16[3,1024,256]{2,1,0:T(8,128)(2,1)} %param.18) | copy-start | bytes 4718596
  72.6 5.8 %collective-permute-start.2 = (bf16[1,256,128]{2,1,0:T(8,128)(2,1)S(1)}, bf16[1,256,128]{2,1,0:T(8,128)(2,1)S(1)}, u32[]{:S(2)}, u32[]{:S(2)}) collective-permute-start(bf16[1,256,128]{2,1,0:T(8,128)(2,1)S(1)} %get-tuple-element.17), channel_id=1, source_target_pairs={{0,64},{16,80},{32,96},{48,112},{64,0},{80,16},{96,32},{112,48},{1... | collective-permute-start | bytes 196616 | tf_op jit(solution)/shard_map/ppermute | solution.py:15

commit v4 on v3

--- a/solution.py
+++ b/solution.py
@@ -186,8 +186,12 @@
     ).astype(jnp.bfloat16)
     col_count = lax.axis_size("col")
     pieces = coeffs.reshape(col_count, -1, columns)
-    inverse = jnp.argsort(owner_map)
-    outgoing = jnp.take(pieces, inverse, axis=0)
+    chosen = (owner_map[:, None] == jnp.arange(col_count, dtype=owner_map.dtype)[None, :]).astype(
+        jnp.bfloat16
+    )
+    outgoing = jnp.einsum(
+        "kd,kxw->dxw", chosen, pieces, preferred_element_type=jnp.float32
+    ).astype(jnp.bfloat16)
     root_shares = root_term.reshape(col_count, -1, columns)
     arrived, root_share = scatter(outgoing, root_shares)
     shape_now = arrived.shape
@@ -196,7 +200,9 @@
     )
     mixed_rows = mixed_rows.astype(jnp.bfloat16).reshape(shape_now)
     returned, root_full = gather(mixed_rows, root_share, lax.axis_size("row"))
-    ordered = jnp.take(returned, owner_map, axis=0).reshape(-1, columns)
+    ordered = jnp.einsum(
+        "jd,dxw->jxw", chosen, returned, preferred_element_type=jnp.float32
+    ).astype(jnp.bfloat16).reshape(-1, columns)
     cluster_part = jnp.dot(expand, ordered, preferred_element_type=jnp.float32)
 
     levels = lax.axis_size("row").bit_length() - 1

time: 80.3 us -> 74.8 us (0.932)
  other arithmetic: 7.61 us -> 3.19 us
  local copies, waits for them, and re-layouts: 5.32 us -> 3.01 us
  matrix products: 18.5 us -> 19.8 us
    gather x2 -> x0, local copies, waits for them, and re-layouts: 3.38 us -> none  [the longest x1 1.69 us: per_device(): ordered = jnp.take(returned, owner_map, axis=0).reshape(-1, columns)]
    dot_general x0 -> x2, matrix products: none -> 2.11 us  [the longest x1 1.62 us: per_device(): jnp.einsum('jd,dxw->jxw', chosen, returned, preferred_element_type=jnp.fl...]
    sort x1 -> x0, other arithmetic: 1.9 us -> none  [per_device(): inverse = jnp.argsort(owner_map)]
    select_n x4 -> x0, other arithmetic: 1.68 us -> none  [the longest x2 0.91 us: per_device(): outgoing = jnp.take(pieces, inverse, axis=0)]
    dot_general x0 -> x1, local copies, waits for them, and re-layouts: none -> 0.93 us  [per_device(): jnp.einsum('kd,kxw->dxw', chosen, pieces, preferred_element_type=jnp.floa...]
  transfers between devices with their start and end apart: 3 -> 3, of which waited for: 2 -> 2; matrix products, arithmetic and copies ran while one was open for 32% -> 27% of each run, Pallas kernels for 47% -> 50%
where the time goes in v4:
time: 74.8 us; the launch traced here: 74.4 us
  Pallas kernels  37.5 us (50%)
  matrix products  19.8 us (26%)
  waiting for transfers between devices  8.97 us (12%)
  other arithmetic  3.19 us (4%)
  local copies, waits for them, and re-layouts  3.01 us (4%)
  starting transfers between devices  1.85 us (2%)
    pallas_call x1, Pallas kernels, gather(): pl.pallas_call(functools.partial(gather_kernel, n, m), out_shape=(jax.Sha...  19.6 us
    pallas_call x1, Pallas kernels, scatter(): pl.pallas_call(functools.partial(scatter_kernel, n), out_shape=(jax.Shape...  17.9 us
    ppermute x3, waiting for transfers between devices, swapped(): lax.ppermute(x, axis, [(i, i ^ 1 << bit) for i in range(lax.axis_size(axi...  8.97 us
    dot_general x1, matrix products, per_device(): jnp.dot(middle, arrived.reshape(-1, shape_now[2]), preferred_element_type...  6.48 us
    dot_general x1, matrix products, per_device(): lax.dot_general(compress, lowered, contract_first, preferred_element_type...  3.49 us
    dot_general x1, matrix products, per_device(): lax.dot_general(root_project, lowered, contract_first, preferred_element_...  2.03 us
    dot_general x1, matrix products, per_device(): jnp.einsum('blr,lw->brw', row_project, lowered, preferred_element_type=jn...  2.02 us
    ppermute x3, starting transfers between devices, swapped(): lax.ppermute(x, axis, [(i, i ^ 1 << bit) for i in range(lax.axis_size(axi...  1.85 us
  transfers between devices with their start and end apart: 3, of which 2 were waited for; matrix products, arithmetic and copies ran while one was open for 27% of the time, Pallas kernels for 50%

profile of v4, /device:TPU:0, one launch (start us, length us, event | category | flops | bytes accessed | tf_op | source)
XLA Modules:
  0.0 74.4 jit_solution(11768194982302262445)
XLA Ops:
  0.0 0.0 copy-start
  0.0 1.2 %convert_element_type.26 = bf16[1024,128]{1,0:T(8,128)(2,1)S(1)} convert(f32[1024,128]{1,0:T(8,128)} %param.10) | non-fusion elementwise | flops 131072 | bytes 786432 | tf_op jit(solution)/shard_map/convert_element_type | solution.py:175
  1.2 0.0 copy-start.4
  1.2 2.0 %fusion.7 = f32[3,256,128]{2,1,0:T(8,128)S(1)} fusion(bf16[3,1024,256]{2,1,0:T(8,128)(2,1)} %param.15, bf16[1024,128]{1,0:T(8,128)(2,1)S(1)} %convert_element_type.26), kind=kOutput, calls=%fused_computation.15 | convolution fusion | flops 201326592 | bytes 2228224 | tf_op jit(solution)/shard_map/blr,lw->brw/dot_general | solution.py:180
  3.3 0.1 collective-permute-start
  3.4 2.0 %fusion.22 = f32[256,128]{1,0:T(8,128)} fusion(bf16[1024,256]{1,0:T(8,128)(2,1)} %param.17, bf16[1024,128]{1,0:T(8,128)(2,1)S(1)} %convert_element_type.26), kind=kOutput, calls=%fused_computation.32 | convolution fusion | flops 67108864 | bytes 917504 | tf_op jit(solution)/shard_map/dot_general | solution.py:177
  5.4 3.5 %convolution_convert_fusion.1 = bf16[2048,128]{1,0:T(8,128)(2,1)S(1)} fusion(bf16[1024,2048]{1,0:T(8,128)(2,1)} %param.12, bf16[1024,128]{1,0:T(8,128)(2,1)S(1)} %convert_element_type.26), kind=kOutput, calls=%fused_computation.1 | convolution fusion | flops 537133056 | bytes 4980736 | tf_op jit(solution)/shard_map/dot_general | solution.py:184
  8.9 0.0 copy-done.4
  8.9 0.5 fusion.5
  9.4 0.9 %copy.45.x_ref = bf16[16,128,128]{2,1,0:T(8,128)(2,1)} copy(bf16[16,128,128]{2,0,1:T(8,128)(2,1)S(1)} %fusion.5) | data formatting | bytes 1048576 | tf_op jit(solution)/shard_map/kd,kxw->dxw/dot_general | solution.py:192
  10.3 17.9 %shard_map.100 = (bf16[16,128,128]{2,1,0:T(8,128)(2,1)}, f32[16,128]{1,0:T(8,128)}) custom-call(bf16[16,128,128]{2,1,0:T(8,128)(2,1)} %copy.45.x_ref, f32[16,16,128]{2,1,0:T(8,128)} %bitcast.47), custom_call_target="tpu_custom_call" | custom-call | tf_op jit(solution)/shard_map/pallas_call | solution.py:66
  28.2 6.5 %fusion = bf16[2048,128]{0,1:T(8,128)(2,1)S(1)} fusion(bf16[2048,128]{1,0:T(8,128)(2,1)} %bitcast.46, bf16[2048,2048]{1,0:T(8,128)(2,1)} %param.13), kind=kOutput, calls=%fused_computation.2 | convolution fusion | flops 1074003968 | bytes 9437184 | tf_op jit(solution)/shard_map/dot_general | solution.py:198
  34.7 1.0 %copy.24 = bf16[2048,128]{1,0:T(8,128)(2,1)} copy(bf16[2048,128]{0,1:T(8,128)(2,1)S(1)} %fusion) | data formatting | bytes 1048576 | tf_op jit(solution)/shard_map/convert_element_type | solution.py:201
  35.7 19.6 %shard_map.101 = (bf16[16,128,128]{2,1,0:T(8,128)(2,1)}, f32[16,16,128]{2,1,0:T(8,128)}) custom-call(bf16[16,128,128]{2,1,0:T(8,128)(2,1)} %bitcast.45, f32[16,128]{1,0:T(8,128)} %get-tuple-element.10.share_ref), custom_call_target="tpu_custom_call" | custom-call | tf_op jit(solution)/shard_map/pallas_call | solution.py:144
  55.3 0.0 copy-start.1
  55.3 1.6 %convolution_convert_fusion.2 = bf16[16,128,128]{2,0,1:T(8,128)(2,1)S(1)} fusion(bf16[16,128,128]{2,1,0:T(8,128)(2,1)} %get-tuple-element.11, s32[16]{0:T(128)S(1)} %copy-done.4), kind=kOutput, calls=%fused_computation.3 | convolution fusion | flops 8651008 | bytes 1048640 | tf_op jit(solution)/shard_map/jd,dxw->jxw/dot_general | solution.py:203
  57.0 0.1 copy.26
  57.1 0.9 %convert_element_type.32 = bf16[16,16,128]{2,1,0:T(8,128)(2,1)S(1)} convert(f32[16,16,128]{2,1,0:T(8,128)} %get-tuple-element.12) | non-fusion elementwise | flops 32768 | bytes 196608 | tf_op jit(solution)/shard_map/convert_element_type | solution.py:226
  58.0 0.0 copy-done
  58.0 0.7 fusion.21
  58.7 0.0 copy-start.3
  58.8 0.0 collective-permute-done
  58.8 1.0 %slice_add_fusion = f32[2,256,128]{2,1,0:T(8,128)S(1)} fusion(f32[3,256,128]{2,1,0:T(8,128)} %collective-permute-done, f32[3,256,128]{2,1,0:T(8,128)S(1)} %fusion.7), kind=kLoop, calls=%fused_computation.14 | loop fusion | flops 65536 | bytes 786432 | tf_op jit(solution)/shard_map/add | solution.py:215
  59.8 0.7 collective-permute-start.1
  60.5 0.0 copy-done.1
  60.5 0.0 copy-start.2
  60.5 1.3 %fusion.1 = f32[1024,128]{1,0:T(8,128)S(1)} fusion(f32[1024,128]{1,0:T(8,128)S(1)} %fusion.21, bf16[1024,2048]{1,0:T(8,128)(2,1)S(1)} %copy-done.1, bf16[2048,128]{1,0:T(8,128)(2,1)S(1)} %bitcast.44), kind=kOutput, calls=%fused_computation.7 | convolution fusion | flops 537001984 | bytes 5767168 | tf_op jit(solution)/shard_map/dot_general | solution.py:206
  61.7 5.4 %collective-permute-done.1 = f32[2,256,128]{2,1,0:T(8,128)S(1)} collective-permute-done((f32[2,256,128]{2,1,0:T(8,128)S(1)}, f32[2,256,128]{2,1,0:T(8,128)S(1)}, u32[]{:S(2)}, u32[]{:S(2)}) %collective-permute-start.1) | collective-permute-done | bytes 262176 | tf_op jit(solution)/shard_map/ppermute | solution.py:15
  67.2 1.1 %collective-permute-start.2 = (bf16[1,256,128]{2,1,0:T(8,128)(2,1)S(1)}, bf16[1,256,128]{2,1,0:T(8,128)(2,1)S(1)}, u32[]{:S(2)}, u32[]{:S(2)}) collective-permute-start(bf16[1,256,128]{2,1,0:T(8,128)(2,1)S(1)} %get-tuple-element.14), channel_id=1, source_target_pairs={{0,64},{16,80},{32,96},{48,112},{64,0},{80,16},{96,32},{112,48},{1... | collective-permute-start | bytes 196616 | tf_op jit(solution)/shard_map/ppermute | solution.py:15
  68.3 0.0 copy-done.3
  68.3 0.3 convolution_bitcast_fusion
  68.6 0.9 %slice.39 = bf16[1,256,128]{2,1,0:T(8,128)(2,1)S(1)} slice(f32[3,256,128]{2,1,0:T(8,128)} %collective-permute-done), slice={[0:1], [0:256], [0:128]} | slice | bytes 131072 | tf_op jit(solution)/shard_map/slice | solution.py:213
  69.5 3.5 %collective-permute-done.2 = bf16[1,256,128]{2,1,0:T(8,128)(2,1)S(1)} collective-permute-done((bf16[1,256,128]{2,1,0:T(8,128)(2,1)S(1)}, bf16[1,256,128]{2,1,0:T(8,128)(2,1)S(1)}, u32[]{:S(2)}, u32[]{:S(2)}) %collective-permute-start.2) | collective-permute-done | bytes 65568 | tf_op jit(solution)/shard_map/ppermute | solution.py:15
  73.1 0.0 copy-done.2
  73.1 1.4 %fusion.3 = f32[1024,128]{1,0:T(8,128)} fusion(f32[1024,128]{1,0:T(8,128)S(1)} %convolution_bitcast_fusion, f32[1024,128]{1,0:T(8,128)S(1)} %fusion.1, bf16[3,1024,256]{2,1,0:T(8,128)(2,1)S(1)} %copy-done.2, bf16[1,256,128]{2,1,0:T(8,128)(2,1)S(1)} %collective-permute-done.2, bf16[1,256,128]{2,1,0:T(8,128)(2,1)S(1)} %get-tuple-element.13, ...), kind=kOutput, calls=%fused_computation.9 | convolution fusion | flops 201785344 | bytes 3342336 | tf_op jit(solution)/shard_map/blr,brw->lw/dot_general | solution.py:219
  (1 shorter events, 0.0 us)
Async XLA Ops:
  0.0 58.0 %copy-start = (bf16[1024,1024]{1,0:T(8,128)(2,1)S(1)}, bf16[1024,1024]{1,0:T(8,128)(2,1)}, u32[]{:S(2)}) copy-start(bf16[1024,1024]{1,0:T(8,128)(2,1)} %param.11) | copy-start | bytes 6291460
  1.2 7.7 %copy-start.4 = (s32[16]{0:T(128)S(1)}, s32[16]{0:T(128)}, u32[]{:S(2)}) copy-start(s32[16]{0:T(128)} %param.19) | copy-start | bytes 196
  3.3 55.5 %collective-permute-start = (f32[3,256,128]{2,1,0:T(8,128)S(1)}, f32[3,256,128]{2,1,0:T(8,128)}, u32[]{:S(2)}, u32[]{:S(2)}) collective-permute-start(f32[3,256,128]{2,1,0:T(8,128)S(1)} %fusion.7), channel_id=1, source_target_pairs={{0,16},{16,0},{32,48},{48,32},{64,80},{80,64},{96,112},{112,96},{1... | collective-permute-start | bytes 1179656 | tf_op jit(solution)/shard_map/ppermute | solution.py:15
  55.3 5.2 %copy-start.1 = (bf16[1024,2048]{1,0:T(8,128)(2,1)S(1)}, bf16[1024,2048]{1,0:T(8,128)(2,1)}, u32[]{:S(2)}) copy-start(bf16[1024,2048]{1,0:T(8,128)(2,1)} %param.14) | copy-start | bytes 12582916
  58.7 9.6 %copy-start.3 = (bf16[1024,256]{1,0:T(8,128)(2,1)S(1)}, bf16[1024,256]{1,0:T(8,128)(2,1)}, u32[]{:S(2)}) copy-start(bf16[1024,256]{1,0:T(8,128)(2,1)} %param.18) | copy-start | bytes 1572868
  59.8 7.4 %collective-permute-start.1 = (f32[2,256,128]{2,1,0:T(8,128)S(1)}, f32[2,256,128]{2,1,0:T(8,128)S(1)}, u32[]{:S(2)}, u32[]{:S(2)}) collective-permute-start(f32[2,256,128]{2,1,0:T(8,128)S(1)} %slice_add_fusion), channel_id=1, source_target_pairs={{0,32},{16,48},{32,0},{48,16},{64,96},{80,112},{96,64},{112,80},{1... | collective-permute-start | bytes 786440 | tf_op jit(solution)/shard_map/ppermute | solution.py:15
  60.5 12.6 %copy-start.2 = (bf16[3,1024,256]{2,1,0:T(8,128)(2,1)S(1)}, bf16[3,1024,256]{2,1,0:T(8,128)(2,1)}, u32[]{:S(2)}) copy-start(bf16[3,1024,256]{2,1,0:T(8,128)(2,1)} %param.16) | copy-start | bytes 4718596
  67.2 5.8 %collective-permute-start.2 = (bf16[1,256,128]{2,1,0:T(8,128)(2,1)S(1)}, bf16[1,256,128]{2,1,0:T(8,128)(2,1)S(1)}, u32[]{:S(2)}, u32[]{:S(2)}) collective-permute-start(bf16[1,256,128]{2,1,0:T(8,128)(2,1)S(1)} %get-tuple-element.14), channel_id=1, source_target_pairs={{0,64},{16,80},{32,96},{48,112},{64,0},{80,16},{96,32},{112,48},{1... | collective-permute-start | bytes 196616 | tf_op jit(solution)/shard_map/ppermute | solution.py:15

commit v5 on v4

--- a/solution.py
+++ b/solution.py
@@ -15,19 +15,31 @@
     return lax.ppermute(x, axis, [(i, i ^ 1 << bit) for i in range(lax.axis_size(axis))])
 
 
+def flipped(index, bit):
+    return index + bit - 2 * bit * lax.rem(index // bit, 2)
+
+
 def col_peers(n):
     me = lax.axis_index("col")
     return [(s, lax.rem(me + s, n), lax.rem(me + n - s, n)) for s in range(1, n)]
 
 
-def scatter_kernel(n, x_ref, r_ref, o_ref, share_ref, got, sems, local_sems):
+def scatter_kernel(n, x_ref, r_ref, lv_ref, o_ref, share_ref, pair_ref, got, sems, local_sems, pair_sems):
     me = lax.axis_index("col")
     row = lax.axis_index("row")
     barrier = pltpu.get_barrier_semaphore()
     for s, peer, _ in col_peers(n):
         pl.semaphore_signal(barrier, inc=1, device_id=(row, peer), device_id_type=MESH_ID)
-    pl.semaphore_wait(barrier, n - 1)
-
+    partner = flipped(row, 1)
+    pl.semaphore_signal(barrier, inc=1, device_id=(partner, me), device_id_type=MESH_ID)
+    pl.semaphore_wait(barrier, n)
+
+    levels = pltpu.make_async_remote_copy(
+        src_ref=lv_ref, dst_ref=pair_ref,
+        send_sem=pair_sems.at[0], recv_sem=pair_sems.at[1],
+        device_id=(partner, me), device_id_type=MESH_ID,
+    )
+    levels.start()
     local = pltpu.make_async_copy(x_ref.at[me], o_ref.at[me], local_sems.at[0])
     local.start()
     own = pltpu.make_async_copy(r_ref.at[me], got.at[me], local_sems.at[1])
@@ -59,28 +71,42 @@
         piece(s, peer, me).wait_send()
         piece(s, source, source).wait_recv()
     local.wait()
-
-
-def scatter(x, r):
+    levels.wait()
+
+
+def scatter(x, r, lv):
     n = x.shape[0]
     return pl.pallas_call(
         functools.partial(scatter_kernel, n),
         out_shape=(
             jax.ShapeDtypeStruct(x.shape, x.dtype),
             jax.ShapeDtypeStruct(r.shape[1:], r.dtype),
-        ),
-        in_specs=[pl.BlockSpec(memory_space=pl.ANY), pl.BlockSpec(memory_space=pltpu.VMEM)],
-        out_specs=(pl.BlockSpec(memory_space=pl.ANY), pl.BlockSpec(memory_space=pltpu.VMEM)),
+            jax.ShapeDtypeStruct(lv.shape, lv.dtype),
+        ),
+        in_specs=[
+            pl.BlockSpec(memory_space=pl.ANY),
+            pl.BlockSpec(memory_space=pltpu.VMEM),
+            pl.BlockSpec(memory_space=pl.ANY),
+        ],
+        out_specs=(
+            pl.BlockSpec(memory_space=pl.ANY),
+            pl.BlockSpec(memory_space=pltpu.VMEM),
+            pl.BlockSpec(memory_space=pl.ANY),
+        ),
         scratch_shapes=[
             pltpu.VMEM(r.shape, r.dtype),
             pltpu.SemaphoreType.DMA((4, n)),
             pltpu.SemaphoreType.DMA((2,)),
+            pltpu.SemaphoreType.DMA((2,)),
         ],
         compiler_params=pltpu.CompilerParams(collective_id=0, has_side_effects=True),
-    )(x, r)
-
-
-def gather_kernel(n, m, x_ref, share_ref, o_ref, full_ref, rows_got, total, sems, row_sems, local_sems):
+    )(x, r, lv)
+
+
+def gather_kernel(
+    n, m, x_ref, share_ref, c1_ref, c2_ref, o_ref, full_ref, got1, got2,
+    rows_got, total, sems, row_sems, local_sems, sib_sems,
+):
     me = lax.axis_index("col")
     row = lax.axis_index("row")
     row_peers = [(s, lax.rem(row + s, m), lax.rem(row + m - s, m)) for s in range(1, m)]
@@ -117,6 +143,20 @@
             device_id=(row, peer), device_id_type=MESH_ID,
         )
 
+    sends = [
+        (c1_ref, got1, flipped(row, 1 * 2)),
+        (c2_ref, got2.at[0], flipped(row, 4)),
+        (c2_ref, got2.at[1], flipped(flipped(row, 4), 2)),
+    ]
+    sibs = []
+    for i, (src_ref, dst_ref, peer) in enumerate(sends):
+        sib = pltpu.make_async_remote_copy(
+            src_ref=src_ref, dst_ref=dst_ref,
+            send_sem=sib_sems.at[0, i], recv_sem=sib_sems.at[1, i],
+            device_id=(peer, me), device_id_type=MESH_ID,
+        )
+        sib.start()
+        sibs.append(sib)
     for s, peer, _ in row_peers:
         part(s, peer, row).start()
     for s, peer, _ in col_peers(n):
@@ -137,27 +177,42 @@
         piece(s, source, source).wait_recv()
     mine.wait()
     local.wait()
-
-
-def gather(x, share, m):
+    for sib in sibs:
+        sib.wait()
+
+
+def gather(x, share, c1, c2, m):
     n = x.shape[0]
     return pl.pallas_call(
         functools.partial(gather_kernel, n, m),
         out_shape=(
             jax.ShapeDtypeStruct(x.shape, x.dtype),
             jax.ShapeDtypeStruct((n,) + share.shape, share.dtype),
-        ),
-        in_specs=[pl.BlockSpec(memory_space=pl.ANY), pl.BlockSpec(memory_space=pltpu.VMEM)],
-        out_specs=(pl.BlockSpec(memory_space=pl.ANY), pl.BlockSpec(memory_space=pltpu.VMEM)),
+            jax.ShapeDtypeStruct(c1.shape, c1.dtype),
+            jax.ShapeDtypeStruct((2,) + c2.shape, c2.dtype),
+        ),
+        in_specs=[
+            pl.BlockSpec(memory_space=pl.ANY),
+            pl.BlockSpec(memory_space=pltpu.VMEM),
+            pl.BlockSpec(memory_space=pl.ANY),
+            pl.BlockSpec(memory_space=pl.ANY),
+        ],
+        out_specs=(
+            pl.BlockSpec(memory_space=pl.ANY),
+            pl.BlockSpec(memory_space=pltpu.VMEM),
+            pl.BlockSpec(memory_space=pl.ANY),
+            pl.BlockSpec(memory_space=pl.ANY),
+        ),
         scratch_shapes=[
             pltpu.VMEM((m,) + share.shape, share.dtype),
             pltpu.VMEM(share.shape, share.dtype),
             pltpu.SemaphoreType.DMA((4, n)),
             pltpu.SemaphoreType.DMA((2, m)),
             pltpu.SemaphoreType.DMA((3,)),
+            pltpu.SemaphoreType.DMA((2, 3)),
         ],
         compiler_params=pltpu.CompilerParams(collective_id=1, has_side_effects=True),
-    )(x, share)
+    )(x, share, c1, c2)
 
 
 def per_device(
@@ -193,28 +248,22 @@
         "kd,kxw->dxw", chosen, pieces, preferred_element_type=jnp.float32
     ).astype(jnp.bfloat16)
     root_shares = root_term.reshape(col_count, -1, columns)
-    arrived, root_share = scatter(outgoing, root_shares)
+    arrived, root_share, pair = scatter(outgoing, root_shares, level_coeffs)
     shape_now = arrived.shape
     mixed_rows = jnp.dot(
         middle, arrived.reshape(-1, shape_now[2]), preferred_element_type=jnp.float32
     )
     mixed_rows = mixed_rows.astype(jnp.bfloat16).reshape(shape_now)
-    returned, root_full = gather(mixed_rows, root_share, lax.axis_size("row"))
+    chip_sums = level_coeffs[1:] + pair[1:]
+    returned, root_full, quad_one, quad_two = gather(
+        mixed_rows, root_share, chip_sums[0], chip_sums[1], lax.axis_size("row")
+    )
     ordered = jnp.einsum(
         "jd,dxw->jxw", chosen, returned, preferred_element_type=jnp.float32
     ).astype(jnp.bfloat16).reshape(-1, columns)
     cluster_part = jnp.dot(expand, ordered, preferred_element_type=jnp.float32)
 
-    levels = lax.axis_size("row").bit_length() - 1
-    running = level_coeffs
-    siblings = []
-    for level_bit in range(levels):
-        partner = swapped(running[level_bit:], "row", level_bit)
-        siblings.append(partner[0])
-        running = jnp.concatenate(
-            [running[: level_bit + 1], running[level_bit + 1 :] + partner[1:]], axis=0
-        )
-    sibling_sum = jnp.stack(siblings, axis=0)
+    sibling_sum = jnp.stack([pair[0], quad_one, quad_two[0] + quad_two[1]], axis=0)
     root_sum = root_full.reshape(-1, columns)
     coupled = jnp.einsum(
         "blr,brw->lw",

time: 74.8 us -> 70.7 us (0.945)
  the two profiles are of different devices: /device:TPU:0 before, /device:TPU:1 now
where the time goes in v5:
time: 70.7 us; the launch traced here: 70.3 us
  Pallas kernels  39.4 us (56%)
  matrix products  22 us (31%)
  other arithmetic  5.01 us (7%)
  local copies, waits for them, and re-layouts  3.74 us (5%)
    pallas_call x1, Pallas kernels, gather(): pl.pallas_call(functools.partial(gather_kernel, n, m), out_shape=(jax.Sha...  22.4 us
    pallas_call x1, Pallas kernels, scatter(): pl.pallas_call(functools.partial(scatter_kernel, n), out_shape=(jax.Shape...  17 us
    dot_general x1, matrix products, per_device(): jnp.dot(middle, arrived.reshape(-1, shape_now[2]), preferred_element_type...  6.49 us
    dot_general x1, matrix products, per_device(): lax.dot_general(compress, lowered, contract_first, preferred_element_type...  3.5 us
    dot_general x1, matrix products, per_device(): jnp.einsum('blr,lw->brw', row_project, lowered, preferred_element_type=jn...  2.77 us
    dot_general x1, matrix products, per_device(): lax.dot_general(root_project, lowered, contract_first, preferred_element_...  2.05 us
    dot_general x1, matrix products, per_device(): jnp.einsum('blr,brw->lw', row_expand, sibling_sum.astype(jnp.bfloat16), p...  1.99 us
    dot_general x1, matrix products, per_device(): jnp.einsum('jd,dxw->jxw', chosen, returned, preferred_element_type=jnp.fl...  1.62 us

profile of v5, /device:TPU:1, one launch (start us, length us, event | category | flops | bytes accessed | tf_op | source)
XLA Modules:
  0.0 70.3 jit_solution(13299619472680106149)
XLA Ops:
  0.0 0.0 copy-start
  0.0 1.2 %convert_element_type.26 = bf16[1024,128]{1,0:T(8,128)(2,1)S(1)} convert(f32[1024,128]{1,0:T(8,128)} %param.10) | non-fusion elementwise | flops 131072 | bytes 786432 | tf_op jit(solution)/shard_map/convert_element_type | solution.py:230
  1.2 0.0 copy-start.4
  1.2 2.0 %fusion.21 = f32[256,128]{1,0:T(8,128)} fusion(bf16[1024,256]{1,0:T(8,128)(2,1)} %param.17, bf16[1024,128]{1,0:T(8,128)(2,1)S(1)} %convert_element_type.26), kind=kOutput, calls=%fused_computation.33 | convolution fusion | flops 67108864 | bytes 917504 | tf_op jit(solution)/shard_map/dot_general | solution.py:232
  3.3 2.8 %fusion.7.lv_ref = f32[3,256,128]{2,1,0:T(8,128)} fusion(bf16[3,1024,256]{2,1,0:T(8,128)(2,1)} %param.15, bf16[1024,128]{1,0:T(8,128)(2,1)S(1)} %convert_element_type.26), kind=kOutput, calls=%fused_computation.15 | convolution fusion | flops 201326592 | bytes 2228224 | tf_op jit(solution)/shard_map/blr,lw->brw/dot_general | solution.py:235
  6.1 3.5 %convolution_convert_fusion.1 = bf16[2048,128]{1,0:T(8,128)(2,1)S(1)} fusion(bf16[1024,2048]{1,0:T(8,128)(2,1)} %param.12, bf16[1024,128]{1,0:T(8,128)(2,1)S(1)} %convert_element_type.26), kind=kOutput, calls=%fused_computation.1 | convolution fusion | flops 537133056 | bytes 4980736 | tf_op jit(solution)/shard_map/dot_general | solution.py:239
  9.6 0.0 copy-start.2
  9.6 0.0 copy-done.4
  9.6 0.5 fusion.5
  10.1 0.9 %copy.45.x_ref = bf16[16,128,128]{2,1,0:T(8,128)(2,1)} copy(bf16[16,128,128]{2,0,1:T(8,128)(2,1)S(1)} %fusion.5) | data formatting | bytes 1048576 | tf_op jit(solution)/shard_map/kd,kxw->dxw/dot_general | solution.py:247
  11.0 0.0 copy-done
  11.0 0.7 %fusion.20 = f32[1024,128]{1,0:T(8,128)S(1)} fusion(bf16[1024,1024]{1,0:T(8,128)(2,1)S(1)} %copy-done, bf16[1024,128]{1,0:T(8,128)(2,1)S(1)} %convert_element_type.26), kind=kOutput, calls=%fused_computation.32 | convolution fusion | flops 268435456 | bytes 2883584 | tf_op jit(solution)/shard_map/dot_general | solution.py:238
  11.7 17.0 %shard_map.100 = (bf16[16,128,128]{2,1,0:T(8,128)(2,1)}, f32[16,128]{1,0:T(8,128)}, f32[3,256,128]{2,1,0:T(8,128)}) custom-call(bf16[16,128,128]{2,1,0:T(8,128)(2,1)} %copy.45.x_ref, f32[16,16,128]{2,1,0:T(8,128)} %bitcast.54, f32[3,256,128]{2,1,0:T(8,128)} %fusion.7.lv_ref), custom_call_target="tpu_custom_call" | custom-call | tf_op jit(solution)/shard_map/pallas_call | solution.py:79
  28.7 0.0 copy-done.2
  28.7 1.0 %slice_add_fusion = f32[2,256,128]{2,1,0:T(8,128)S(1)} fusion(f32[3,256,128]{2,1,0:T(8,128)S(1)} %copy-done.2, f32[3,256,128]{2,1,0:T(8,128)} %get-tuple-element.14), kind=kLoop, calls=%fused_computation.14 | loop fusion | flops 65536 | bytes 786432 | tf_op jit(solution)/shard_map/add | solution.py:257
  29.7 6.5 %fusion = bf16[2048,128]{0,1:T(8,128)(2,1)S(1)} fusion(bf16[2048,128]{1,0:T(8,128)(2,1)} %bitcast.52, bf16[2048,2048]{1,0:T(8,128)(2,1)} %param.13), kind=kOutput, calls=%fused_computation.2 | convolution fusion | flops 1074003968 | bytes 9437184 | tf_op jit(solution)/shard_map/dot_general | solution.py:253
  36.2 1.0 %copy.25 = bf16[2048,128]{1,0:T(8,128)(2,1)} copy(bf16[2048,128]{0,1:T(8,128)(2,1)S(1)} %fusion) | data formatting | bytes 1048576 | tf_op jit(solution)/shard_map/convert_element_type | solution.py:256
  37.2 0.7 %slice_bitcast_fusion = (f32[256,128]{1,0:T(8,128)}, f32[256,128]{1,0:T(8,128)}) fusion(f32[2,256,128]{2,1,0:T(8,128)S(1)} %slice_add_fusion), kind=kLoop, calls=%fused_computation.23 | loop fusion | bytes 524288 | tf_op jit(solution)/shard_map/squeeze | solution.py:259
  37.9 0.9 %slice.40 = bf16[1,256,128]{2,1,0:T(8,128)(2,1)S(1)} slice(f32[3,256,128]{2,1,0:T(8,128)} %get-tuple-element.14), slice={[0:1], [0:256], [0:128]} | slice | bytes 131072 | tf_op jit(solution)/shard_map/slice | solution.py:266
  38.9 22.4 %shard_map.101 = (bf16[16,128,128]{2,1,0:T(8,128)(2,1)}, f32[16,16,128]{2,1,0:T(8,128)}, f32[256,128]{1,0:T(8,128)}, f32[2,256,128]{2,1,0:T(8,128)}) custom-call(bf16[16,128,128]{2,1,0:T(8,128)(2,1)} %bitcast.50, f32[16,128]{1,0:T(8,128)} %get-tuple-element.13.share_ref, f32[256,128]{1,0:T(8,128)} %get-tuple-element.20.c1_ref, ...), custom_call_target="tpu_custom_call" | custom-call | tf_op jit(solution)/shard_map/pallas_call | solution.py:186
  61.3 0.0 copy-start.1
  61.3 1.6 %convolution_convert_fusion.2 = bf16[16,128,128]{2,0,1:T(8,128)(2,1)S(1)} fusion(bf16[16,128,128]{2,1,0:T(8,128)(2,1)} %get-tuple-element.15, s32[16]{0:T(128)S(1)} %copy-done.4), kind=kOutput, calls=%fused_computation.3 | convolution fusion | flops 8651008 | bytes 1048640 | tf_op jit(solution)/shard_map/jd,dxw->jxw/dot_general | solution.py:261
  62.9 0.1 copy.27
  63.1 0.9 %convert_bitcast_fusion = bf16[1,256,128]{2,1,0:T(8,128)(2,1)S(1)} fusion(f32[256,128]{1,0:T(8,128)} %get-tuple-element.16), kind=kLoop, calls=%fused_computation.26 | loop fusion | flops 32768 | bytes 196608 | tf_op jit(solution)/shard_map/stack | solution.py:266
  64.0 1.0 %add_convert_fusion = bf16[1,256,128]{2,1,0:T(8,128)(2,1)S(1)} fusion(f32[2,256,128]{2,1,0:T(8,128)} %get-tuple-element.17), kind=kLoop, calls=%fused_computation.25 | loop fusion | flops 65536 | bytes 327680 | tf_op jit(solution)/shard_map/convert.2
  65.0 0.9 %convert_element_type.32 = bf16[16,16,128]{2,1,0:T(8,128)(2,1)S(1)} convert(f32[16,16,128]{2,1,0:T(8,128)} %get-tuple-element.18) | non-fusion elementwise | flops 32768 | bytes 196608 | tf_op jit(solution)/shard_map/convert_element_type | solution.py:275
  65.9 2.0 %convolution_bitcast_fusion.1 = f32[1024,128]{1,0:T(8,128)S(1)} fusion(bf16[3,1024,256]{2,1,0:T(8,128)(2,1)} %param.16, bf16[1,256,128]{2,1,0:T(8,128)(2,1)S(1)} %add_convert_fusion, bf16[1,256,128]{2,1,0:T(8,128)(2,1)S(1)} %convert_bitcast_fusion, bf16[1,256,128]{2,1,0:T(8,128)(2,1)S(1)} %slice.40), kind=kOutput, calls=%fused_computation.5 | convolution fusion | flops 201523200 | bytes 2293760 | tf_op jit(solution)/shard_map/blr,brw->lw/dot_general | solution.py:268
  67.9 0.0 copy-done.1
  67.9 0.0 copy-start.3
  67.9 1.3 %fusion.3 = f32[1024,128]{1,0:T(8,128)S(1)} fusion(f32[1024,128]{1,0:T(8,128)S(1)} %convolution_bitcast_fusion.1, f32[1024,128]{1,0:T(8,128)S(1)} %fusion.20, bf16[1024,2048]{1,0:T(8,128)(2,1)S(1)} %copy-done.1, bf16[2048,128]{1,0:T(8,128)(2,1)S(1)} %bitcast.51), kind=kOutput, calls=%fused_computation.9 | convolution fusion | flops 537133056 | bytes 6291456 | tf_op jit(solution)/shard_map/dot_general | solution.py:264
  69.2 0.0 copy-done.3
  69.2 1.1 %fusion.1 = f32[1024,128]{1,0:T(8,128)} fusion(f32[1024,128]{1,0:T(8,128)S(1)} %fusion.3, bf16[1024,256]{1,0:T(8,128)(2,1)S(1)} %copy-done.3, bf16[256,128]{1,0:T(8,128)(2,1)S(1)} %bitcast.55), kind=kOutput, calls=%fused_computation.6 | convolution fusion | flops 67239936 | bytes 1638400 | tf_op jit(solution)/shard_map/dot_general | solution.py:274
Async XLA Ops:
  0.0 11.0 %copy-start = (bf16[1024,1024]{1,0:T(8,128)(2,1)S(1)}, bf16[1024,1024]{1,0:T(8,128)(2,1)}, u32[]{:S(2)}) copy-start(bf16[1024,1024]{1,0:T(8,128)(2,1)} %param.11) | copy-start | bytes 6291460
  1.2 8.3 %copy-start.4 = (s32[16]{0:T(128)S(1)}, s32[16]{0:T(128)}, u32[]{:S(2)}) copy-start(s32[16]{0:T(128)} %param.19) | copy-start | bytes 196
  9.6 19.2 %copy-start.2 = (f32[3,256,128]{2,1,0:T(8,128)S(1)}, f32[3,256,128]{2,1,0:T(8,128)}, u32[]{:S(2)}) copy-start(f32[3,256,128]{2,1,0:T(8,128)} %fusion.7.lv_ref) | copy-start | bytes 1179652
  61.3 6.6 %copy-start.1 = (bf16[1024,2048]{1,0:T(8,128)(2,1)S(1)}, bf16[1024,2048]{1,0:T(8,128)(2,1)}, u32[]{:S(2)}) copy-start(bf16[1024,2048]{1,0:T(8,128)(2,1)} %param.14) | copy-start | bytes 12582916
  67.9 1.3 %copy-start.3 = (bf16[1024,256]{1,0:T(8,128)(2,1)S(1)}, bf16[1024,256]{1,0:T(8,128)(2,1)}, u32[]{:S(2)}) copy-start(bf16[1024,256]{1,0:T(8,128)(2,1)} %param.18) | copy-start | bytes 1572868

commit v6 on v5

--- a/solution.py
+++ b/solution.py
@@ -104,11 +104,12 @@
 
 
 def gather_kernel(
-    n, m, x_ref, share_ref, c1_ref, c2_ref, o_ref, full_ref, got1, got2,
-    rows_got, total, sems, row_sems, local_sems, sib_sems,
+    n, m, a_ref, w_ref, share_ref, cs_ref, o_ref, full_ref, got1, got2,
+    mixed, rows_got, total, sems, row_sems, local_sems, sib_sems,
 ):
     me = lax.axis_index("col")
     row = lax.axis_index("row")
+    piece_rows = mixed.shape[1]
     row_peers = [(s, lax.rem(row + s, m), lax.rem(row + m - s, m)) for s in range(1, m)]
     barrier = pltpu.get_barrier_semaphore()
     for s, peer, _ in col_peers(n):
@@ -117,36 +118,12 @@
         pl.semaphore_signal(barrier, inc=1, device_id=(peer, me), device_id_type=MESH_ID)
     pl.semaphore_wait(barrier, n - 1 + m - 1)
 
-    local = pltpu.make_async_copy(x_ref.at[me], o_ref.at[me], local_sems.at[0])
-    local.start()
     own = pltpu.make_async_copy(share_ref, rows_got.at[row], local_sems.at[1])
     own.start()
-
-    def piece(s, peer, slot):
-        return pltpu.make_async_remote_copy(
-            src_ref=x_ref.at[peer], dst_ref=o_ref.at[slot],
-            send_sem=sems.at[0, s], recv_sem=sems.at[1, s],
-            device_id=(row, peer), device_id_type=MESH_ID,
-        )
-
-    def part(s, peer, slot):
-        return pltpu.make_async_remote_copy(
-            src_ref=share_ref, dst_ref=rows_got.at[slot],
-            send_sem=row_sems.at[0, s], recv_sem=row_sems.at[1, s],
-            device_id=(peer, me), device_id_type=MESH_ID,
-        )
-
-    def spread(s, peer, slot):
-        return pltpu.make_async_remote_copy(
-            src_ref=total, dst_ref=full_ref.at[slot],
-            send_sem=sems.at[2, s], recv_sem=sems.at[3, s],
-            device_id=(row, peer), device_id_type=MESH_ID,
-        )
-
     sends = [
-        (c1_ref, got1, flipped(row, 1 * 2)),
-        (c2_ref, got2.at[0], flipped(row, 4)),
-        (c2_ref, got2.at[1], flipped(flipped(row, 4), 2)),
+        (cs_ref.at[0], got1, flipped(row, 2)),
+        (cs_ref.at[1], got2.at[0], flipped(row, 4)),
+        (cs_ref.at[1], got2.at[1], flipped(flipped(row, 4), 2)),
     ]
     sibs = []
     for i, (src_ref, dst_ref, peer) in enumerate(sends):
@@ -157,10 +134,46 @@
         )
         sib.start()
         sibs.append(sib)
+
+    def part(s, peer, slot):
+        return pltpu.make_async_remote_copy(
+            src_ref=share_ref, dst_ref=rows_got.at[slot],
+            send_sem=row_sems.at[0, s], recv_sem=row_sems.at[1, s],
+            device_id=(peer, me), device_id_type=MESH_ID,
+        )
+
     for s, peer, _ in row_peers:
         part(s, peer, row).start()
-    for s, peer, _ in col_peers(n):
+
+    def piece(s, peer, slot):
+        return pltpu.make_async_remote_copy(
+            src_ref=mixed.at[peer], dst_ref=o_ref.at[slot],
+            send_sem=sems.at[0, s], recv_sem=sems.at[1, s],
+            device_id=(row, peer), device_id_type=MESH_ID,
+        )
+
+    def compute(peer):
+        first = pl.multiple_of(peer * piece_rows, piece_rows)
+        mixed[peer] = jnp.dot(
+            w_ref[pl.ds(first, piece_rows), :], a_ref[...], preferred_element_type=jnp.float32
+        ).astype(mixed.dtype)
+
+    def compute_and_send(s, carry):
+        peer = lax.rem(me + s, n)
+        compute(peer)
         piece(s, peer, me).start()
+        return carry
+
+    half = n // 2
+    lax.fori_loop(1, half, compute_and_send, 0)
+
+    def spread(s, peer, slot):
+        return pltpu.make_async_remote_copy(
+            src_ref=total, dst_ref=full_ref.at[slot],
+            send_sem=sems.at[2, s], recv_sem=sems.at[3, s],
+            device_id=(row, peer), device_id_type=MESH_ID,
+        )
+
     for s, peer, source in row_peers:
         part(s, peer, row).wait_send()
         part(s, source, source).wait_recv()
@@ -170,6 +183,12 @@
     mine.start()
     for s, peer, _ in col_peers(n):
         spread(s, peer, me).start()
+
+    lax.fori_loop(half, n, compute_and_send, 0)
+    compute(me)
+    local = pltpu.make_async_copy(mixed.at[me], o_ref.at[me], local_sems.at[0])
+    local.start()
+
     for s, peer, source in col_peers(n):
         spread(s, peer, me).wait_send()
         spread(s, source, source).wait_recv()
@@ -181,20 +200,21 @@
         sib.wait()
 
 
-def gather(x, share, c1, c2, m):
-    n = x.shape[0]
+def gather(a, w, share, cs, n, m):
+    piece_rows = w.shape[0] // n
+    columns = a.shape[1]
     return pl.pallas_call(
         functools.partial(gather_kernel, n, m),
         out_shape=(
-            jax.ShapeDtypeStruct(x.shape, x.dtype),
+            jax.ShapeDtypeStruct((n, piece_rows, columns), a.dtype),
             jax.ShapeDtypeStruct((n,) + share.shape, share.dtype),
-            jax.ShapeDtypeStruct(c1.shape, c1.dtype),
-            jax.ShapeDtypeStruct((2,) + c2.shape, c2.dtype),
+            jax.ShapeDtypeStruct(cs.shape[1:], cs.dtype),
+            jax.ShapeDtypeStruct(cs.shape, cs.dtype),
         ),
         in_specs=[
-            pl.BlockSpec(memory_space=pl.ANY),
-            pl.BlockSpec(memory_space=pltpu.VMEM),
-            pl.BlockSpec(memory_space=pl.ANY),
+            pl.BlockSpec(memory_space=pltpu.VMEM),
+            pl.BlockSpec(memory_space=pltpu.VMEM),
+            pl.BlockSpec(memory_space=pltpu.VMEM),
             pl.BlockSpec(memory_space=pl.ANY),
         ],
         out_specs=(
@@ -204,6 +224,7 @@
             pl.BlockSpec(memory_space=pl.ANY),
         ),
         scratch_shapes=[
+            pltpu.VMEM((n, piece_rows, columns), a.dtype),
             pltpu.VMEM((m,) + share.shape, share.dtype),
             pltpu.VMEM(share.shape, share.dtype),
             pltpu.SemaphoreType.DMA((4, n)),
@@ -211,8 +232,10 @@
             pltpu.SemaphoreType.DMA((3,)),
             pltpu.SemaphoreType.DMA((2, 3)),
         ],
-        compiler_params=pltpu.CompilerParams(collective_id=1, has_side_effects=True),
-    )(x, share, c1, c2)
+        compiler_params=pltpu.CompilerParams(
+            collective_id=1, has_side_effects=True, vmem_limit_bytes=48 * 1024 * 1024
+        ),
+    )(a, w, share, cs)
 
 
 def per_device(
@@ -249,14 +272,10 @@
     ).astype(jnp.bfloat16)
     root_shares = root_term.reshape(col_count, -1, columns)
     arrived, root_share, pair = scatter(outgoing, root_shares, level_coeffs)
-    shape_now = arrived.shape
-    mixed_rows = jnp.dot(
-        middle, arrived.reshape(-1, shape_now[2]), preferred_element_type=jnp.float32
-    )
-    mixed_rows = mixed_rows.astype(jnp.bfloat16).reshape(shape_now)
     chip_sums = level_coeffs[1:] + pair[1:]
     returned, root_full, quad_one, quad_two = gather(
-        mixed_rows, root_share, chip_sums[0], chip_sums[1], lax.axis_size("row")
+        arrived.reshape(-1, columns), middle, root_share, chip_sums, col_count,
+        lax.axis_size("row"),
     )
     ordered = jnp.einsum(
         "jd,dxw->jxw", chosen, returned, preferred_element_type=jnp.float32

time: 70.7 us -> 65.4 us (0.925)
  matrix products: 22 us -> 12.9 us
  Pallas kernels: 39.4 us -> 45 us
  other arithmetic: 5.01 us -> 2.24 us
  local copies, waits for them, and re-layouts: 3.74 us -> 4.69 us
    dot_general x1 -> x0, matrix products: 6.49 us -> none  [per_device(): jnp.dot(middle, arrived.reshape(-1, shape_now[2]), preferred_element_type...]
    pallas_call x1, Pallas kernels: 22.4 us -> 28.1 us  [gather(): pl.pallas_call(functools.partial(gather_kernel, n, m), out_shape=(jax.Sha...]
    unnamed x10 -> x16, local copies, waits for them, and re-layouts: 0.03 us -> 2.7 us
    dot_general x1, matrix products: 1.99 us -> 0.57 us  [per_device(): jnp.einsum('blr,brw->lw', row_expand, sibling_sum.astype(jnp.bfloat16), p...]
    dot_general x1, matrix products: 1.62 us -> 0.43 us  [per_device(): jnp.einsum('jd,dxw->jxw', chosen, returned, preferred_element_type=jnp.fl...]
    convert_element_type x1 -> x0, local copies, waits for them, and re-layouts: 1 us -> none  [per_device(): mixed_rows = mixed_rows.astype(jnp.bfloat16).reshape(shape_now)]
    another operation x1, other arithmetic: 0.98 us -> 0.02 us
    another operation x1, other arithmetic: 0.91 us -> 0.01 us  [per_device(): jnp.stack([pair[0], quad_one, quad_two[0] + quad_two[1]], axis=0)]
where the time goes in v6:
time: 65.4 us; the launch traced here: 65 us
  Pallas kernels  45 us (69%)
  matrix products  12.9 us (20%)
  local copies, waits for them, and re-layouts  4.69 us (7%)
  other arithmetic  2.24 us (3%)
    pallas_call x1, Pallas kernels, gather(): pl.pallas_call(functools.partial(gather_kernel, n, m), out_shape=(jax.Sha...  28.1 us
    pallas_call x1, Pallas kernels, scatter(): pl.pallas_call(functools.partial(scatter_kernel, n), out_shape=(jax.Shape...  17 us
    dot_general x1, matrix products, per_device(): lax.dot_general(compress, lowered, contract_first, preferred_element_type...  3.51 us
    dot_general x1, matrix products, per_device(): jnp.einsum('blr,lw->brw', row_project, lowered, preferred_element_type=jn...  2.77 us
    unnamed x16, local copies, waits for them, and re-layouts  2.7 us
    dot_general x1, matrix products, per_device(): lax.dot_general(root_project, lowered, contract_first, preferred_element_...  2.04 us

profile of v6, /device:TPU:1, one launch (start us, length us, event | category | flops | bytes accessed | tf_op | source)
XLA Modules:
  0.0 65.0 jit_solution(14624739119229811561)
XLA Ops:
  0.0 0.0 copy-start
  0.0 1.2 %convert_element_type.20 = bf16[1024,128]{1,0:T(8,128)(2,1)S(1)} convert(f32[1024,128]{1,0:T(8,128)} %param.10) | non-fusion elementwise | flops 131072 | bytes 786432 | tf_op jit(solution)/shard_map/convert_element_type | solution.py:253
  1.2 2.0 %fusion.20 = f32[256,128]{1,0:T(8,128)} fusion(bf16[1024,256]{1,0:T(8,128)(2,1)} %param.17, bf16[1024,128]{1,0:T(8,128)(2,1)S(1)} %convert_element_type.20), kind=kOutput, calls=%fused_computation.29 | convolution fusion | flops 67108864 | bytes 917504 | tf_op jit(solution)/shard_map/dot_general | solution.py:255
  3.3 2.8 %fusion.6.lv_ref = f32[3,256,128]{2,1,0:T(8,128)} fusion(bf16[3,1024,256]{2,1,0:T(8,128)(2,1)} %param.15, bf16[1024,128]{1,0:T(8,128)(2,1)S(1)} %convert_element_type.20), kind=kOutput, calls=%fused_computation.13 | convolution fusion | flops 201326592 | bytes 2228224 | tf_op jit(solution)/shard_map/blr,lw->brw/dot_general | solution.py:258
  6.0 0.0 copy-start.7
  6.0 3.5 %convolution_convert_fusion = bf16[2048,128]{1,0:T(8,128)(2,1)S(1)} fusion(bf16[1024,2048]{1,0:T(8,128)(2,1)} %param.12, bf16[1024,128]{1,0:T(8,128)(2,1)S(1)} %convert_element_type.20), kind=kOutput, calls=%fused_computation | convolution fusion | flops 537133056 | bytes 4980736 | tf_op jit(solution)/shard_map/dot_general | solution.py:262
  9.6 0.0 copy-done.7
  9.6 0.5 fusion.4
  10.1 0.9 %copy.43.x_ref = bf16[16,128,128]{2,1,0:T(8,128)(2,1)} copy(bf16[16,128,128]{2,0,1:T(8,128)(2,1)S(1)} %fusion.4) | data formatting | bytes 1048576 | tf_op jit(solution)/shard_map/kd,kxw->dxw/dot_general | solution.py:270
  11.0 0.0 copy-done
  11.0 0.0 copy-start.4
  11.0 0.7 %fusion.19 = f32[1024,128]{1,0:T(8,128)S(1)} fusion(bf16[1024,1024]{1,0:T(8,128)(2,1)S(1)} %copy-done, bf16[1024,128]{1,0:T(8,128)(2,1)S(1)} %convert_element_type.20), kind=kOutput, calls=%fused_computation.28 | convolution fusion | flops 268435456 | bytes 2883584 | tf_op jit(solution)/shard_map/dot_general | solution.py:261
  11.7 17.0 %shard_map.100 = (bf16[16,128,128]{2,1,0:T(8,128)(2,1)}, f32[16,128]{1,0:T(8,128)}, f32[3,256,128]{2,1,0:T(8,128)}) custom-call(bf16[16,128,128]{2,1,0:T(8,128)(2,1)} %copy.43.x_ref, f32[16,16,128]{2,1,0:T(8,128)} %bitcast.44, f32[3,256,128]{2,1,0:T(8,128)} %fusion.6.lv_ref), custom_call_target="tpu_custom_call" | custom-call | tf_op jit(solution)/shard_map/pallas_call | solution.py:79
  28.7 0.0 copy-done.4
  28.7 1.0 %slice_add_fusion.cs_ref = f32[2,256,128]{2,1,0:T(8,128)S(1)} fusion(f32[3,256,128]{2,1,0:T(8,128)S(1)} %copy-done.4, f32[3,256,128]{2,1,0:T(8,128)} %get-tuple-element.14), kind=kLoop, calls=%fused_computation.12 | loop fusion | flops 65536 | bytes 786432 | tf_op jit(solution)/shard_map/add | solution.py:275
  29.7 0.9 %slice.28 = bf16[1,256,128]{2,1,0:T(8,128)(2,1)S(1)} slice(f32[3,256,128]{2,1,0:T(8,128)} %get-tuple-element.14), slice={[0:1], [0:256], [0:128]} | slice | bytes 131072 | tf_op jit(solution)/shard_map/slice | solution.py:285
  30.6 0.0 copy-start.1
  30.6 1.0 %copy-done.1 = bf16[16,128,128]{2,1,0:T(8,128)(2,1)S(1)} copy-done((bf16[16,128,128]{2,1,0:T(8,128)(2,1)S(1)}, bf16[16,128,128]{2,1,0:T(8,128)(2,1)}, u32[]{:S(2)}) %copy-start.1) | copy-done | bytes 524312
  31.7 0.0 copy-start.2
  31.7 0.7 %copy-done.2 = f32[16,128]{1,0:T(8,128)S(1)} copy-done((f32[16,128]{1,0:T(8,128)S(1)}, f32[16,128]{1,0:T(8,128)}, u32[]{:S(2)}) %copy-start.2) | copy-done | bytes 8216
  32.4 0.0 copy-start.5
  32.4 28.1 %shard_map.101 = (bf16[16,128,128]{2,1,0:T(8,128)(2,1)S(1)}, f32[16,16,128]{2,1,0:T(8,128)S(1)}, f32[256,128]{1,0:T(8,128)S(1)}, f32[2,256,128]{2,1,0:T(8,128)S(1)}) custom-call(bf16[2048,128]{1,0:T(8,128)(2,1)S(1)} %bitcast.41, bf16[2048,2048]{1,0:T(8,128)(2,1)} %w_ref.1, f32[16,128]{1,0:T(8,128)S(1)} %copy-done.2, f32[2,256,128]{2,1,0:T(8,128)S(1)} %slice_add_fusion.cs_ref), custom_call_target="tpu_custom_call" | custom-call | tf_op jit(solution)/shard_map/pallas_call | solution.py:206
  60.4 0.0 copy-start.3
  60.4 0.4 convolution_convert_fusion.1
  60.9 0.1 copy.25
  61.1 0.0 copy-done.5
  61.1 0.6 convolution_bitcast_fusion.1
  61.7 0.9 %copy-done.3 = bf16[1024,2048]{1,0:T(8,128)(2,1)S(1)} copy-done((bf16[1024,2048]{1,0:T(8,128)(2,1)S(1)}, bf16[1024,2048]{1,0:T(8,128)(2,1)}, u32[]{:S(2)}) %copy-start.3) | copy-done | bytes 4194328
  62.6 0.0 copy-start.6
  62.6 1.3 %fusion.2 = f32[1024,128]{1,0:T(8,128)S(1)} fusion(f32[1024,128]{1,0:T(8,128)S(1)} %convolution_bitcast_fusion.1, f32[1024,128]{1,0:T(8,128)S(1)} %fusion.19, bf16[1024,2048]{1,0:T(8,128)(2,1)S(1)} %copy-done.3, bf16[2048,128]{1,0:T(8,128)(2,1)S(1)} %bitcast.42), kind=kOutput, calls=%fused_computation.7 | convolution fusion | flops 537133056 | bytes 6291456 | tf_op jit(solution)/shard_map/dot_general | solution.py:283
  63.9 0.0 copy-done.6
  63.9 1.1 %fusion = f32[1024,128]{1,0:T(8,128)} fusion(f32[1024,128]{1,0:T(8,128)S(1)} %fusion.2, bf16[1024,256]{1,0:T(8,128)(2,1)S(1)} %copy-done.6, bf16[256,128]{1,0:T(8,128)(2,1)S(1)} %bitcast.45), kind=kOutput, calls=%fused_computation.4 | convolution fusion | flops 67239936 | bytes 1638400 | tf_op jit(solution)/shard_map/dot_general | solution.py:293
  (3 shorter events, 0.0 us)
Async XLA Ops:
  0.0 11.0 %copy-start = (bf16[1024,1024]{1,0:T(8,128)(2,1)S(1)}, bf16[1024,1024]{1,0:T(8,128)(2,1)}, u32[]{:S(2)}) copy-start(bf16[1024,1024]{1,0:T(8,128)(2,1)} %param.11) | copy-start | bytes 6291460
  6.0 3.5 %copy-start.7 = (s32[16]{0:T(128)S(1)}, s32[16]{0:T(128)}, u32[]{:S(2)}) copy-start(s32[16]{0:T(128)} %param.19) | copy-start | bytes 196
  11.0 17.7 %copy-start.4 = (f32[3,256,128]{2,1,0:T(8,128)S(1)}, f32[3,256,128]{2,1,0:T(8,128)}, u32[]{:S(2)}) copy-start(f32[3,256,128]{2,1,0:T(8,128)} %fusion.6.lv_ref) | copy-start | bytes 1179652
  30.6 1.0 %copy-start.1 = (bf16[16,128,128]{2,1,0:T(8,128)(2,1)S(1)}, bf16[16,128,128]{2,1,0:T(8,128)(2,1)}, u32[]{:S(2)}) copy-start(bf16[16,128,128]{2,1,0:T(8,128)(2,1)} %get-tuple-element.12) | copy-start | bytes 1572868
  31.7 0.7 %copy-start.2 = (f32[16,128]{1,0:T(8,128)S(1)}, f32[16,128]{1,0:T(8,128)}, u32[]{:S(2)}) copy-start(f32[16,128]{1,0:T(8,128)} %get-tuple-element.13.share_ref) | copy-start | bytes 24580
  32.4 28.7 %copy-start.5 = (bf16[3,1024,256]{2,1,0:T(8,128)(2,1)S(1)}, bf16[3,1024,256]{2,1,0:T(8,128)(2,1)}, u32[]{:S(2)}) copy-start(bf16[3,1024,256]{2,1,0:T(8,128)(2,1)} %param.16) | copy-start | bytes 4718596
  60.4 2.2 %copy-start.3 = (bf16[1024,2048]{1,0:T(8,128)(2,1)S(1)}, bf16[1024,2048]{1,0:T(8,128)(2,1)}, u32[]{:S(2)}) copy-start(bf16[1024,2048]{1,0:T(8,128)(2,1)} %param.14) | copy-start | bytes 12582916
  62.6 1.3 %copy-start.6 = (bf16[1024,256]{1,0:T(8,128)(2,1)S(1)}, bf16[1024,256]{1,0:T(8,128)(2,1)}, u32[]{:S(2)}) copy-start(bf16[1024,256]{1,0:T(8,128)(2,1)} %param.18) | copy-start | bytes 1572868

commit v7 on v6

--- a/solution.py
+++ b/solution.py
@@ -272,7 +272,7 @@
     ).astype(jnp.bfloat16)
     root_shares = root_term.reshape(col_count, -1, columns)
     arrived, root_share, pair = scatter(outgoing, root_shares, level_coeffs)
-    chip_sums = level_coeffs[1:] + pair[1:]
+    chip_sums = (level_coeffs[1:] + pair[1:]).astype(jnp.bfloat16)
     returned, root_full, quad_one, quad_two = gather(
         arrived.reshape(-1, columns), middle, root_share, chip_sums, col_count,
         lax.axis_size("row"),
@@ -282,7 +282,14 @@
     ).astype(jnp.bfloat16).reshape(-1, columns)
     cluster_part = jnp.dot(expand, ordered, preferred_element_type=jnp.float32)
 
-    sibling_sum = jnp.stack([pair[0], quad_one, quad_two[0] + quad_two[1]], axis=0)
+    sibling_sum = jnp.stack(
+        [
+            pair[0],
+            quad_one.astype(jnp.float32),
+            quad_two[0].astype(jnp.float32) + quad_two[1].astype(jnp.float32),
+        ],
+        axis=0,
+    )
     root_sum = root_full.reshape(-1, columns)
     coupled = jnp.einsum(
         "blr,brw->lw",

time: 65.4 us -> 61.4 us (0.939)
  Pallas kernels: 45 us -> 42.2 us
  matrix products: 12.9 us -> 11.8 us
    pallas_call x1, Pallas kernels: 28.1 us -> 25.3 us  [gather(): pl.pallas_call(functools.partial(gather_kernel, n, m), out_shape=(jax.Sha...]
    dot_general x1, matrix products: 2.04 us -> 0.98 us  [per_device(): lax.dot_general(root_project, lowered, contract_first, preferred_element_...]
    convert_element_type x0 -> x1, other arithmetic: none -> 0.98 us  [per_device(): chip_sums = (level_coeffs[1:] + pair[1:]).astype(jnp.bfloat16)]
    add x1 -> x0, other arithmetic: 0.98 us -> none  [per_device(): chip_sums = level_coeffs[1:] + pair[1:]]
    unnamed x16 -> x18, local copies, waits for them, and re-layouts: 2.7 us -> 2.64 us
where the time goes in v7:
time: 61.4 us; the launch traced here: 61 us
  Pallas kernels  42.2 us (69%)
  matrix products  11.8 us (19%)
  local copies, waits for them, and re-layouts  4.62 us (8%)
  other arithmetic  2.23 us (4%)
    pallas_call x1, Pallas kernels, gather(): pl.pallas_call(functools.partial(gather_kernel, n, m), out_shape=(jax.Sha...  25.3 us
    pallas_call x1, Pallas kernels, scatter(): pl.pallas_call(functools.partial(scatter_kernel, n), out_shape=(jax.Shape...  16.9 us
    dot_general x1, matrix products, per_device(): lax.dot_general(compress, lowered, contract_first, preferred_element_type...  3.51 us
    dot_general x1, matrix products, per_device(): jnp.einsum('blr,lw->brw', row_project, lowered, preferred_element_type=jn...  2.76 us
    unnamed x18, local copies, waits for them, and re-layouts  2.64 us
    dot_general x1, matrix products, per_device(): cluster_part = jnp.dot(expand, ordered, preferred_element_type=jnp.float32)  1.25 us

profile of v7, /device:TPU:1, one launch (start us, length us, event | category | flops | bytes accessed | tf_op | source)
XLA Modules:
  0.0 61.0 jit_solution(10941669275123569766)
XLA Ops:
  0.0 0.0 copy-start
  0.0 1.2 %convert_element_type.32 = bf16[1024,128]{1,0:T(8,128)(2,1)S(1)} convert(f32[1024,128]{1,0:T(8,128)} %param.10) | non-fusion elementwise | flops 131072 | bytes 786432 | tf_op jit(solution)/shard_map/convert_element_type | solution.py:253
  1.2 2.8 %fusion.7.lv_ref = f32[3,256,128]{2,1,0:T(8,128)} fusion(bf16[3,1024,256]{2,1,0:T(8,128)(2,1)} %param.15, bf16[1024,128]{1,0:T(8,128)(2,1)S(1)} %convert_element_type.32), kind=kOutput, calls=%fused_computation.14 | convolution fusion | flops 201326592 | bytes 2228224 | tf_op jit(solution)/shard_map/blr,lw->brw/dot_general | solution.py:258
  4.0 0.0 copy-start.8
  4.0 3.5 %convolution_convert_fusion = bf16[2048,128]{1,0:T(8,128)(2,1)S(1)} fusion(bf16[1024,2048]{1,0:T(8,128)(2,1)} %param.12, bf16[1024,128]{1,0:T(8,128)(2,1)S(1)} %convert_element_type.32), kind=kOutput, calls=%fused_computation | convolution fusion | flops 537133056 | bytes 4980736 | tf_op jit(solution)/shard_map/dot_general | solution.py:262
  7.5 0.0 copy-start.7
  7.5 0.0 copy-start.4
  7.5 0.0 copy-done.8
  7.5 0.5 fusion.4
  8.0 0.9 %copy.43.x_ref = bf16[16,128,128]{2,1,0:T(8,128)(2,1)} copy(bf16[16,128,128]{2,0,1:T(8,128)(2,1)S(1)} %fusion.4) | data formatting | bytes 1048576 | tf_op jit(solution)/shard_map/kd,kxw->dxw/dot_general | solution.py:270
  9.0 0.0 copy-done.7
  9.0 1.0 %fusion.21 = f32[256,128]{1,0:T(8,128)} fusion(bf16[1024,256]{1,0:T(8,128)(2,1)S(1)} %copy-done.7, bf16[1024,128]{1,0:T(8,128)(2,1)S(1)} %convert_element_type.32), kind=kOutput, calls=%fused_computation.29 | convolution fusion | flops 67108864 | bytes 917504 | tf_op jit(solution)/shard_map/dot_general | solution.py:255
  10.0 16.9 %shard_map.100 = (bf16[16,128,128]{2,1,0:T(8,128)(2,1)}, f32[16,128]{1,0:T(8,128)}, f32[3,256,128]{2,1,0:T(8,128)}) custom-call(bf16[16,128,128]{2,1,0:T(8,128)(2,1)} %copy.43.x_ref, f32[16,16,128]{2,1,0:T(8,128)} %bitcast.44, f32[3,256,128]{2,1,0:T(8,128)} %fusion.7.lv_ref), custom_call_target="tpu_custom_call" | custom-call | tf_op jit(solution)/shard_map/pallas_call | solution.py:79
  26.9 0.0 copy-done.4
  26.9 1.0 %fusion.6.cs_ref = bf16[2,256,128]{2,1,0:T(8,128)(2,1)S(1)} fusion(f32[3,256,128]{2,1,0:T(8,128)S(1)} %copy-done.4, f32[3,256,128]{2,1,0:T(8,128)} %get-tuple-element.14), kind=kLoop, calls=%fused_computation.13 | loop fusion | flops 131072 | bytes 655360 | tf_op jit(solution)/shard_map/convert_element_type | solution.py:275
  27.9 0.0 copy-start.1
  27.9 1.0 %copy-done.1 = bf16[16,128,128]{2,1,0:T(8,128)(2,1)S(1)} copy-done((bf16[16,128,128]{2,1,0:T(8,128)(2,1)S(1)}, bf16[16,128,128]{2,1,0:T(8,128)(2,1)}, u32[]{:S(2)}) %copy-start.1) | copy-done | bytes 524312
  28.9 0.0 copy-start.2
  28.9 0.7 %copy-done.2 = f32[16,128]{1,0:T(8,128)S(1)} copy-done((f32[16,128]{1,0:T(8,128)S(1)}, f32[16,128]{1,0:T(8,128)}, u32[]{:S(2)}) %copy-start.2) | copy-done | bytes 8216
  29.6 25.3 %shard_map.101 = (bf16[16,128,128]{2,1,0:T(8,128)(2,1)S(1)}, f32[16,16,128]{2,1,0:T(8,128)S(1)}, bf16[256,128]{1,0:T(8,128)(2,1)S(1)}, bf16[2,256,128]{2,1,0:T(8,128)(2,1)S(1)}) custom-call(bf16[2048,128]{1,0:T(8,128)(2,1)S(1)} %bitcast.40, bf16[2048,2048]{1,0:T(8,128)(2,1)} %w_ref.1, f32[16,128]{1,0:T(8,128)S(1)} %copy-done.2, ...), custom_call_target="tpu_custom_call" | custom-call | tf_op jit(solution)/shard_map/pallas_call | solution.py:206
  54.9 0.0 copy-start.5
  54.9 0.4 convolution_convert_fusion.1
  55.3 0.1 copy.25
  55.5 0.9 %slice.30 = bf16[1,256,128]{2,1,0:T(8,128)(2,1)S(1)} slice(f32[3,256,128]{2,1,0:T(8,128)} %get-tuple-element.14), slice={[0:1], [0:256], [0:128]} | slice | bytes 131072 | tf_op jit(solution)/shard_map/slice | solution.py:287
  56.4 0.0 copy-done.5
  56.4 0.0 copy-start.3
  56.5 0.6 convolution_bitcast_fusion.1
  57.0 0.0 copy-done
  57.0 0.7 %fusion.20 = f32[1024,128]{1,0:T(8,128)S(1)} fusion(bf16[1024,1024]{1,0:T(8,128)(2,1)S(1)} %copy-done, bf16[1024,128]{1,0:T(8,128)(2,1)S(1)} %convert_element_type.32), kind=kOutput, calls=%fused_computation.28 | convolution fusion | flops 268435456 | bytes 2883584 | tf_op jit(solution)/shard_map/dot_general | solution.py:261
  57.8 0.9 %copy-done.3 = bf16[1024,2048]{1,0:T(8,128)(2,1)S(1)} copy-done((bf16[1024,2048]{1,0:T(8,128)(2,1)S(1)}, bf16[1024,2048]{1,0:T(8,128)(2,1)}, u32[]{:S(2)}) %copy-start.3) | copy-done | bytes 4194328
  58.6 0.0 copy-start.6
  58.6 1.3 %fusion.2 = f32[1024,128]{1,0:T(8,128)S(1)} fusion(f32[1024,128]{1,0:T(8,128)S(1)} %convolution_bitcast_fusion.1, f32[1024,128]{1,0:T(8,128)S(1)} %fusion.20, bf16[1024,2048]{1,0:T(8,128)(2,1)S(1)} %copy-done.3, bf16[2048,128]{1,0:T(8,128)(2,1)S(1)} %bitcast.42), kind=kOutput, calls=%fused_computation.7 | convolution fusion | flops 537133056 | bytes 6291456 | tf_op jit(solution)/shard_map/dot_general | solution.py:283
  59.9 0.0 copy-done.6
  59.9 1.1 %fusion = f32[1024,128]{1,0:T(8,128)} fusion(f32[1024,128]{1,0:T(8,128)S(1)} %fusion.2, bf16[1024,256]{1,0:T(8,128)(2,1)S(1)} %copy-done.6, bf16[256,128]{1,0:T(8,128)(2,1)S(1)} %bitcast.45), kind=kOutput, calls=%fused_computation.4 | convolution fusion | flops 67239936 | bytes 1638400 | tf_op jit(solution)/shard_map/dot_general | solution.py:300
  (2 shorter events, 0.0 us)
Async XLA Ops:
  0.0 57.0 %copy-start = (bf16[1024,1024]{1,0:T(8,128)(2,1)S(1)}, bf16[1024,1024]{1,0:T(8,128)(2,1)}, u32[]{:S(2)}) copy-start(bf16[1024,1024]{1,0:T(8,128)(2,1)} %param.11) | copy-start | bytes 6291460
  4.0 3.5 %copy-start.8 = (s32[16]{0:T(128)S(1)}, s32[16]{0:T(128)}, u32[]{:S(2)}) copy-start(s32[16]{0:T(128)} %param.19) | copy-start | bytes 196
  7.5 1.5 %copy-start.7 = (bf16[1024,256]{1,0:T(8,128)(2,1)S(1)}, bf16[1024,256]{1,0:T(8,128)(2,1)}, u32[]{:S(2)}) copy-start(bf16[1024,256]{1,0:T(8,128)(2,1)} %param.17) | copy-start | bytes 1572868
  7.5 19.4 %copy-start.4 = (f32[3,256,128]{2,1,0:T(8,128)S(1)}, f32[3,256,128]{2,1,0:T(8,128)}, u32[]{:S(2)}) copy-start(f32[3,256,128]{2,1,0:T(8,128)} %fusion.7.lv_ref) | copy-start | bytes 1179652
  27.9 1.0 %copy-start.1 = (bf16[16,128,128]{2,1,0:T(8,128)(2,1)S(1)}, bf16[16,128,128]{2,1,0:T(8,128)(2,1)}, u32[]{:S(2)}) copy-start(bf16[16,128,128]{2,1,0:T(8,128)(2,1)} %get-tuple-element.12) | copy-start | bytes 1572868
  28.9 0.7 %copy-start.2 = (f32[16,128]{1,0:T(8,128)S(1)}, f32[16,128]{1,0:T(8,128)}, u32[]{:S(2)}) copy-start(f32[16,128]{1,0:T(8,128)} %get-tuple-element.13.share_ref) | copy-start | bytes 24580
  54.9 1.5 %copy-start.5 = (bf16[3,1024,256]{2,1,0:T(8,128)(2,1)S(1)}, bf16[3,1024,256]{2,1,0:T(8,128)(2,1)}, u32[]{:S(2)}) copy-start(bf16[3,1024,256]{2,1,0:T(8,128)(2,1)} %param.16) | copy-start | bytes 4718596
  56.4 2.2 %copy-start.3 = (bf16[1024,2048]{1,0:T(8,128)(2,1)S(1)}, bf16[1024,2048]{1,0:T(8,128)(2,1)}, u32[]{:S(2)}) copy-start(bf16[1024,2048]{1,0:T(8,128)(2,1)} %param.14) | copy-start | bytes 12582916
  58.6 1.3 %copy-start.6 = (bf16[1024,256]{1,0:T(8,128)(2,1)S(1)}, bf16[1024,256]{1,0:T(8,128)(2,1)}, u32[]{:S(2)}) copy-start(bf16[1024,256]{1,0:T(8,128)(2,1)} %param.18) | copy-start | bytes 1572868

commit v8 on v6

--- a/solution.py
+++ b/solution.py
@@ -24,22 +24,38 @@
     return [(s, lax.rem(me + s, n), lax.rem(me + n - s, n)) for s in range(1, n)]
 
 
-def scatter_kernel(n, x_ref, r_ref, lv_ref, o_ref, share_ref, pair_ref, got, sems, local_sems, pair_sems):
+def scatter_kernel(
+    n, x_ref, r_ref, lv_ref, o_ref, share_ref, pair_ref, far_ref, got, sems, local_sems, pair_sems,
+):
     me = lax.axis_index("col")
     row = lax.axis_index("row")
     barrier = pltpu.get_barrier_semaphore()
     for s, peer, _ in col_peers(n):
         pl.semaphore_signal(barrier, inc=1, device_id=(row, peer), device_id_type=MESH_ID)
     partner = flipped(row, 1)
-    pl.semaphore_signal(barrier, inc=1, device_id=(partner, me), device_id_type=MESH_ID)
-    pl.semaphore_wait(barrier, n)
-
-    levels = pltpu.make_async_remote_copy(
-        src_ref=lv_ref, dst_ref=pair_ref,
-        send_sem=pair_sems.at[0], recv_sem=pair_sems.at[1],
-        device_id=(partner, me), device_id_type=MESH_ID,
-    )
-    levels.start()
+    far = [flipped(row, 4), flipped(flipped(row, 4), 2)]
+    for peer in [partner] + far:
+        pl.semaphore_signal(barrier, inc=1, device_id=(peer, me), device_id_type=MESH_ID)
+    pl.semaphore_wait(barrier, n + 2)
+
+    low = pair_ref.shape[0]
+    level_copies = [
+        pltpu.make_async_remote_copy(
+            src_ref=lv_ref.at[pl.ds(0, low)], dst_ref=pair_ref,
+            send_sem=pair_sems.at[0, 0], recv_sem=pair_sems.at[1, 0],
+            device_id=(partner, me), device_id_type=MESH_ID,
+        )
+    ]
+    for i, peer in enumerate(far):
+        level_copies.append(
+            pltpu.make_async_remote_copy(
+                src_ref=lv_ref.at[low], dst_ref=far_ref.at[i],
+                send_sem=pair_sems.at[0, i + 1], recv_sem=pair_sems.at[1, i + 1],
+                device_id=(peer, me), device_id_type=MESH_ID,
+            )
+        )
+    for copy in level_copies:
+        copy.start()
     local = pltpu.make_async_copy(x_ref.at[me], o_ref.at[me], local_sems.at[0])
     local.start()
     own = pltpu.make_async_copy(r_ref.at[me], got.at[me], local_sems.at[1])
@@ -71,7 +87,8 @@
         piece(s, peer, me).wait_send()
         piece(s, source, source).wait_recv()
     local.wait()
-    levels.wait()
+    for copy in level_copies:
+        copy.wait()
 
 
 def scatter(x, r, lv):
@@ -81,7 +98,8 @@
         out_shape=(
             jax.ShapeDtypeStruct(x.shape, x.dtype),
             jax.ShapeDtypeStruct(r.shape[1:], r.dtype),
-            jax.ShapeDtypeStruct(lv.shape, lv.dtype),
+            jax.ShapeDtypeStruct((lv.shape[0] - 1,) + lv.shape[1:], lv.dtype),
+            jax.ShapeDtypeStruct((2,) + lv.shape[1:], lv.dtype),
         ),
         in_specs=[
             pl.BlockSpec(memory_space=pl.ANY),
@@ -91,20 +109,21 @@
         out_specs=(
             pl.BlockSpec(memory_space=pl.ANY),
             pl.BlockSpec(memory_space=pltpu.VMEM),
+            pl.BlockSpec(memory_space=pl.ANY),
             pl.BlockSpec(memory_space=pl.ANY),
         ),
         scratch_shapes=[
             pltpu.VMEM(r.shape, r.dtype),
             pltpu.SemaphoreType.DMA((4, n)),
             pltpu.SemaphoreType.DMA((2,)),
-            pltpu.SemaphoreType.DMA((2,)),
+            pltpu.SemaphoreType.DMA((2, 3)),
         ],
         compiler_params=pltpu.CompilerParams(collective_id=0, has_side_effects=True),
     )(x, r, lv)
 
 
 def gather_kernel(
-    n, m, a_ref, w_ref, share_ref, cs_ref, o_ref, full_ref, got1, got2,
+    n, m, a_ref, w_ref, share_ref, c1_ref, p_ref, o_ref, full_ref, got1, got2,
     mixed, rows_got, total, sems, row_sems, local_sems, sib_sems,
 ):
     me = lax.axis_index("col")
@@ -120,11 +139,7 @@
 
     own = pltpu.make_async_copy(share_ref, rows_got.at[row], local_sems.at[1])
     own.start()
-    sends = [
-        (cs_ref.at[0], got1, flipped(row, 2)),
-        (cs_ref.at[1], got2.at[0], flipped(row, 4)),
-        (cs_ref.at[1], got2.at[1], flipped(flipped(row, 4), 2)),
-    ]
+    sends = [(c1_ref, got1, flipped(row, 2)), (p_ref, got2, flipped(row, 1))]
     sibs = []
     for i, (src_ref, dst_ref, peer) in enumerate(sends):
         sib = pltpu.make_async_remote_copy(
@@ -200,7 +215,7 @@
         sib.wait()
 
 
-def gather(a, w, share, cs, n, m):
+def gather(a, w, share, c1, p, n, m):
     piece_rows = w.shape[0] // n
     columns = a.shape[1]
     return pl.pallas_call(
@@ -208,13 +223,14 @@
         out_shape=(
             jax.ShapeDtypeStruct((n, piece_rows, columns), a.dtype),
             jax.ShapeDtypeStruct((n,) + share.shape, share.dtype),
-            jax.ShapeDtypeStruct(cs.shape[1:], cs.dtype),
-            jax.ShapeDtypeStruct(cs.shape, cs.dtype),
+            jax.ShapeDtypeStruct(c1.shape, c1.dtype),
+            jax.ShapeDtypeStruct(p.shape, p.dtype),
         ),
         in_specs=[
             pl.BlockSpec(memory_space=pltpu.VMEM),
             pl.BlockSpec(memory_space=pltpu.VMEM),
             pl.BlockSpec(memory_space=pltpu.VMEM),
+            pl.BlockSpec(memory_space=pl.ANY),
             pl.BlockSpec(memory_space=pl.ANY),
         ],
         out_specs=(
@@ -230,12 +246,12 @@
             pltpu.SemaphoreType.DMA((4, n)),
             pltpu.SemaphoreType.DMA((2, m)),
             pltpu.SemaphoreType.DMA((3,)),
-            pltpu.SemaphoreType.DMA((2, 3)),
+            pltpu.SemaphoreType.DMA((2, 2)),
         ],
         compiler_params=pltpu.CompilerParams(
             collective_id=1, has_side_effects=True, vmem_limit_bytes=48 * 1024 * 1024
         ),
-    )(a, w, share, cs)
+    )(a, w, share, c1, p)
 
 
 def per_device(
@@ -271,10 +287,11 @@
         "kd,kxw->dxw", chosen, pieces, preferred_element_type=jnp.float32
     ).astype(jnp.bfloat16)
     root_shares = root_term.reshape(col_count, -1, columns)
-    arrived, root_share, pair = scatter(outgoing, root_shares, level_coeffs)
-    chip_sums = level_coeffs[1:] + pair[1:]
+    arrived, root_share, pair, far = scatter(outgoing, root_shares, level_coeffs)
+    pair_sum = (level_coeffs[1] + pair[1]).astype(jnp.bfloat16)
+    far_sum = far[0] + far[1]
     returned, root_full, quad_one, quad_two = gather(
-        arrived.reshape(-1, columns), middle, root_share, chip_sums, col_count,
+        arrived.reshape(-1, columns), middle, root_share, pair_sum, far_sum, col_count,
         lax.axis_size("row"),
     )
     ordered = jnp.einsum(
@@ -282,7 +299,9 @@
     ).astype(jnp.bfloat16).reshape(-1, columns)
     cluster_part = jnp.dot(expand, ordered, preferred_element_type=jnp.float32)
 
-    sibling_sum = jnp.stack([pair[0], quad_one, quad_two[0] + quad_two[1]], axis=0)
+    sibling_sum = jnp.stack(
+        [pair[0], quad_one.astype(jnp.float32), far_sum + quad_two], axis=0
+    )
     root_sum = root_full.reshape(-1, columns)
     coupled = jnp.einsum(
         "blr,brw->lw",

time: 65.4 us -> 60.6 us (0.927)
  Pallas kernels: 45 us -> 41.3 us
  matrix products: 12.9 us -> 11.8 us
    pallas_call x1, Pallas kernels: 28.1 us -> 22.6 us  [gather(): pl.pallas_call(functools.partial(gather_kernel, n, m), out_shape=(jax.Sha...]
    pallas_call x1, Pallas kernels: 17 us -> 18.7 us  [scatter(): pl.pallas_call(functools.partial(scatter_kernel, n), out_shape=(jax.Shape...]
    dot_general x1, matrix products: 2.04 us -> 1 us  [per_device(): lax.dot_general(root_project, lowered, contract_first, preferred_element_...]
where the time goes in v8:
time: 60.6 us; the launch traced here: 60.3 us
  Pallas kernels  41.3 us (68%)
  matrix products  11.8 us (19%)
  local copies, waits for them, and re-layouts  4.62 us (8%)
  other arithmetic  2.37 us (4%)
    pallas_call x1, Pallas kernels, gather(): pl.pallas_call(functools.partial(gather_kernel, n, m), out_shape=(jax.Sha...  22.6 us
    pallas_call x1, Pallas kernels, scatter(): pl.pallas_call(functools.partial(scatter_kernel, n), out_shape=(jax.Shape...  18.7 us
    dot_general x1, matrix products, per_device(): lax.dot_general(compress, lowered, contract_first, preferred_element_type...  3.51 us
    dot_general x1, matrix products, per_device(): jnp.einsum('blr,lw->brw', row_project, lowered, preferred_element_type=jn...  2.76 us
    unnamed x16, local copies, waits for them, and re-layouts  2.64 us
    dot_general x1, matrix products, per_device(): cluster_part = jnp.dot(expand, ordered, preferred_element_type=jnp.float32)  1.26 us
    convert_element_type x1, other arithmetic, per_device(): lowered = right_side.astype(jnp.bfloat16)  1.22 us

profile of v8, /device:TPU:1, one launch (start us, length us, event | category | flops | bytes accessed | tf_op | source)
XLA Modules:
  0.0 60.3 jit_solution(16169138079364660173)
XLA Ops:
  0.0 0.0 copy-start
  0.0 1.2 %convert_element_type.26 = bf16[1024,128]{1,0:T(8,128)(2,1)S(1)} convert(f32[1024,128]{1,0:T(8,128)} %param.10) | non-fusion elementwise | flops 131072 | bytes 786432 | tf_op jit(solution)/shard_map/convert_element_type | solution.py:269
  1.2 2.8 %fusion.6.lv_ref = f32[3,256,128]{2,1,0:T(8,128)} fusion(bf16[3,1024,256]{2,1,0:T(8,128)(2,1)} %param.15, bf16[1024,128]{1,0:T(8,128)(2,1)S(1)} %convert_element_type.26), kind=kOutput, calls=%fused_computation.12 | convolution fusion | flops 201326592 | bytes 2228224 | tf_op jit(solution)/shard_map/blr,lw->brw/dot_general | solution.py:274
  4.0 0.0 copy-start.7
  4.0 3.5 %convolution_convert_fusion = bf16[2048,128]{1,0:T(8,128)(2,1)S(1)} fusion(bf16[1024,2048]{1,0:T(8,128)(2,1)} %param.12, bf16[1024,128]{1,0:T(8,128)(2,1)S(1)} %convert_element_type.26), kind=kOutput, calls=%fused_computation | convolution fusion | flops 537133056 | bytes 4980736 | tf_op jit(solution)/shard_map/dot_general | solution.py:278
  7.5 0.0 copy-start.6
  7.5 0.0 copy-done.7
  7.5 0.5 fusion.4
  8.0 0.9 %copy.43.x_ref = bf16[16,128,128]{2,1,0:T(8,128)(2,1)} copy(bf16[16,128,128]{2,0,1:T(8,128)(2,1)S(1)} %fusion.4) | data formatting | bytes 1048576 | tf_op jit(solution)/shard_map/kd,kxw->dxw/dot_general | solution.py:286
  9.0 0.0 copy-done.6
  9.0 1.0 %fusion.23 = f32[256,128]{1,0:T(8,128)} fusion(bf16[1024,256]{1,0:T(8,128)(2,1)S(1)} %copy-done.6, bf16[1024,128]{1,0:T(8,128)(2,1)S(1)} %convert_element_type.26), kind=kOutput, calls=%fused_computation.32 | convolution fusion | flops 67108864 | bytes 917504 | tf_op jit(solution)/shard_map/dot_general | solution.py:271
  10.0 18.7 %shard_map.100 = (bf16[16,128,128]{2,1,0:T(8,128)(2,1)}, f32[16,128]{1,0:T(8,128)}, f32[2,256,128]{2,1,0:T(8,128)}, f32[2,256,128]{2,1,0:T(8,128)}) custom-call(bf16[16,128,128]{2,1,0:T(8,128)(2,1)} %copy.43.x_ref, f32[16,16,128]{2,1,0:T(8,128)} %bitcast.50, f32[3,256,128]{2,1,0:T(8,128)} %fusion.6.lv_ref), custom_call_target="tpu_custom_call" | custom-call | tf_op jit(solution)/shard_map/pallas_call | solution.py:96
  28.7 1.1 %add_bitcast_fusion = (f32[256,128]{1,0:T(8,128)S(1)}, bf16[256,128]{1,0:T(8,128)(2,1)S(1)}) fusion(f32[2,256,128]{2,1,0:T(8,128)} %get-tuple-element.16, f32[2,256,128]{2,1,0:T(8,128)} %get-tuple-element.15, f32[3,256,128]{2,1,0:T(8,128)} %fusion.6.lv_ref), kind=kLoop, calls=%fused_computation.23 | loop fusion | flops 98304 | bytes 720896 | tf_op jit(solution)/shard_map/add | solution.py:292
  29.8 0.0 copy-start.1
  29.8 1.0 %copy-done.1 = bf16[16,128,128]{2,1,0:T(8,128)(2,1)S(1)} copy-done((bf16[16,128,128]{2,1,0:T(8,128)(2,1)S(1)}, bf16[16,128,128]{2,1,0:T(8,128)(2,1)}, u32[]{:S(2)}) %copy-start.1) | copy-done | bytes 524312
  30.9 0.0 copy-start.2
  30.9 0.7 %copy-done.2 = f32[16,128]{1,0:T(8,128)S(1)} copy-done((f32[16,128]{1,0:T(8,128)S(1)}, f32[16,128]{1,0:T(8,128)}, u32[]{:S(2)}) %copy-start.2) | copy-done | bytes 8216
  31.5 22.6 %shard_map.101 = (bf16[16,128,128]{2,1,0:T(8,128)(2,1)S(1)}, f32[16,16,128]{2,1,0:T(8,128)S(1)}, bf16[256,128]{1,0:T(8,128)(2,1)S(1)}, f32[256,128]{1,0:T(8,128)S(1)}) custom-call(bf16[2048,128]{1,0:T(8,128)(2,1)S(1)} %bitcast.46, bf16[2048,2048]{1,0:T(8,128)(2,1)} %w_ref.1, f32[16,128]{1,0:T(8,128)S(1)} %copy-done.2, ...), custom_call_target="tpu_custom_call" | custom-call | tf_op jit(solution)/shard_map/pallas_call | solution.py:221
  54.1 0.0 copy-start.4
  54.2 0.4 convolution_convert_fusion.1
  54.6 0.1 copy.25
  54.8 0.9 %slice.34 = bf16[1,256,128]{2,1,0:T(8,128)(2,1)S(1)} slice(f32[2,256,128]{2,1,0:T(8,128)} %get-tuple-element.15), slice={[0:1], [0:256], [0:128]} | slice | bytes 131072 | tf_op jit(solution)/shard_map/slice | solution.py:303
  55.7 0.0 copy-done.4
  55.7 0.0 copy-start.3
  55.7 0.6 convolution_bitcast_fusion.1
  56.3 0.0 copy-done
  56.3 0.7 %fusion.22 = f32[1024,128]{1,0:T(8,128)S(1)} fusion(bf16[1024,1024]{1,0:T(8,128)(2,1)S(1)} %copy-done, bf16[1024,128]{1,0:T(8,128)(2,1)S(1)} %convert_element_type.26), kind=kOutput, calls=%fused_computation.31 | convolution fusion | flops 268435456 | bytes 2883584 | tf_op jit(solution)/shard_map/dot_general | solution.py:277
  57.0 0.9 %copy-done.3 = bf16[1024,2048]{1,0:T(8,128)(2,1)S(1)} copy-done((bf16[1024,2048]{1,0:T(8,128)(2,1)S(1)}, bf16[1024,2048]{1,0:T(8,128)(2,1)}, u32[]{:S(2)}) %copy-start.3) | copy-done | bytes 4194328
  57.9 0.0 copy-start.5
  57.9 1.3 %fusion.2 = f32[1024,128]{1,0:T(8,128)S(1)} fusion(f32[1024,128]{1,0:T(8,128)S(1)} %convolution_bitcast_fusion.1, f32[1024,128]{1,0:T(8,128)S(1)} %fusion.22, bf16[1024,2048]{1,0:T(8,128)(2,1)S(1)} %copy-done.3, bf16[2048,128]{1,0:T(8,128)(2,1)S(1)} %bitcast.48), kind=kOutput, calls=%fused_computation.7 | convolution fusion | flops 537133056 | bytes 6291456 | tf_op jit(solution)/shard_map/dot_general | solution.py:300
  59.2 0.0 copy-done.5
  59.2 1.1 %fusion = f32[1024,128]{1,0:T(8,128)} fusion(f32[1024,128]{1,0:T(8,128)S(1)} %fusion.2, bf16[1024,256]{1,0:T(8,128)(2,1)S(1)} %copy-done.5, bf16[256,128]{1,0:T(8,128)(2,1)S(1)} %bitcast.51), kind=kOutput, calls=%fused_computation.4 | convolution fusion | flops 67239936 | bytes 1638400 | tf_op jit(solution)/shard_map/dot_general | solution.py:312
  (2 shorter events, 0.0 us)
Async XLA Ops:
  0.0 56.3 %copy-start = (bf16[1024,1024]{1,0:T(8,128)(2,1)S(1)}, bf16[1024,1024]{1,0:T(8,128)(2,1)}, u32[]{:S(2)}) copy-start(bf16[1024,1024]{1,0:T(8,128)(2,1)} %param.11) | copy-start | bytes 6291460
  4.0 3.5 %copy-start.7 = (s32[16]{0:T(128)S(1)}, s32[16]{0:T(128)}, u32[]{:S(2)}) copy-start(s32[16]{0:T(128)} %param.19) | copy-start | bytes 196
  7.5 1.5 %copy-start.6 = (bf16[1024,256]{1,0:T(8,128)(2,1)S(1)}, bf16[1024,256]{1,0:T(8,128)(2,1)}, u32[]{:S(2)}) copy-start(bf16[1024,256]{1,0:T(8,128)(2,1)} %param.17) | copy-start | bytes 1572868
  29.8 1.0 %copy-start.1 = (bf16[16,128,128]{2,1,0:T(8,128)(2,1)S(1)}, bf16[16,128,128]{2,1,0:T(8,128)(2,1)}, u32[]{:S(2)}) copy-start(bf16[16,128,128]{2,1,0:T(8,128)(2,1)} %get-tuple-element.13) | copy-start | bytes 1572868
  30.9 0.7 %copy-start.2 = (f32[16,128]{1,0:T(8,128)S(1)}, f32[16,128]{1,0:T(8,128)}, u32[]{:S(2)}) copy-start(f32[16,128]{1,0:T(8,128)} %get-tuple-element.14.share_ref) | copy-start | bytes 24580
  54.1 1.5 %copy-start.4 = (bf16[3,1024,256]{2,1,0:T(8,128)(2,1)S(1)}, bf16[3,1024,256]{2,1,0:T(8,128)(2,1)}, u32[]{:S(2)}) copy-start(bf16[3,1024,256]{2,1,0:T(8,128)(2,1)} %param.16) | copy-start | bytes 4718596
  55.7 2.2 %copy-start.3 = (bf16[1024,2048]{1,0:T(8,128)(2,1)S(1)}, bf16[1024,2048]{1,0:T(8,128)(2,1)}, u32[]{:S(2)}) copy-start(bf16[1024,2048]{1,0:T(8,128)(2,1)} %param.14) | copy-start | bytes 12582916
  57.9 1.3 %copy-start.5 = (bf16[1024,256]{1,0:T(8,128)(2,1)S(1)}, bf16[1024,256]{1,0:T(8,128)(2,1)}, u32[]{:S(2)}) copy-start(bf16[1024,256]{1,0:T(8,128)(2,1)} %param.18) | copy-start | bytes 1572868

commit v9 on v8

--- a/solution.py
+++ b/solution.py
@@ -118,7 +118,9 @@
             pltpu.SemaphoreType.DMA((2,)),
             pltpu.SemaphoreType.DMA((2, 3)),
         ],
-        compiler_params=pltpu.CompilerParams(collective_id=0, has_side_effects=True),
+        compiler_params=pltpu.CompilerParams(
+            collective_id=0, has_side_effects=True, vmem_limit_bytes=4 * 1024 * 1024
+        ),
     )(x, r, lv)
 
 

time: 60.6 us -> 54.1 us (0.89)
  local copies, waits for them, and re-layouts: 4.62 us -> 2.34 us
  Pallas kernels: 41.3 us -> 39.6 us
  matrix products: 11.8 us -> 10.4 us
  other arithmetic: 2.37 us -> 1.29 us
    pallas_call x1, Pallas kernels: 18.7 us -> 16.9 us  [scatter(): pl.pallas_call(functools.partial(scatter_kernel, n), out_shape=(jax.Shape...]
    add x1, other arithmetic: 1.13 us -> 0.04 us  [per_device(): far_sum = far[0] + far[1]]
    slice x1, local copies, waits for them, and re-layouts: 0.91 us -> 0.01 us  [per_device(): pair[0]]
    dot_general x1, local copies, waits for them, and re-layouts: 0.93 us -> 0.14 us  [per_device(): jnp.einsum('kd,kxw->dxw', chosen, pieces, preferred_element_type=jnp.floa...]
    dot_general x1, matrix products: 2.76 us -> 2.02 us  [per_device(): jnp.einsum('blr,lw->brw', row_project, lowered, preferred_element_type=jn...]
    dot_general x1, matrix products: 1 us -> 0.34 us  [per_device(): lax.dot_general(root_project, lowered, contract_first, preferred_element_...]
    unnamed x16 -> x12, local copies, waits for them, and re-layouts: 2.64 us -> 2.06 us
where the time goes in v9:
time: 54.1 us; the launch traced here: 53.8 us
  Pallas kernels  39.6 us (73%)
  matrix products  10.4 us (19%)
  local copies, waits for them, and re-layouts  2.34 us (4%)
  other arithmetic  1.29 us (2%)
    pallas_call x1, Pallas kernels, gather(): pl.pallas_call(functools.partial(gather_kernel, n, m), out_shape=(jax.Sha...  22.7 us
    pallas_call x1, Pallas kernels, scatter(): pl.pallas_call(functools.partial(scatter_kernel, n), out_shape=(jax.Shape...  16.9 us
    dot_general x1, matrix products, per_device(): lax.dot_general(compress, lowered, contract_first, preferred_element_type...  3.51 us
    unnamed x12, local copies, waits for them, and re-layouts  2.06 us
    dot_general x1, matrix products, per_device(): jnp.einsum('blr,lw->brw', row_project, lowered, preferred_element_type=jn...  2.02 us
    dot_general x1, matrix products, per_device(): cluster_part = jnp.dot(expand, ordered, preferred_element_type=jnp.float32)  1.25 us
    convert_element_type x1, other arithmetic, per_device(): lowered = right_side.astype(jnp.bfloat16)  1.22 us
    dot_general x1, matrix products, per_device(): jnp.dot(root_expand, root_sum.astype(jnp.bfloat16), preferred_element_typ...  1.09 us

profile of v9, /device:TPU:1, one launch (start us, length us, event | category | flops | bytes accessed | tf_op | source)
XLA Modules:
  0.0 53.8 jit_solution(15000712274076915608)
XLA Ops:
  0.0 0.0 copy-start
  0.0 1.2 %convert_element_type.26 = bf16[1024,128]{1,0:T(8,128)(2,1)S(1)} convert(f32[1024,128]{1,0:T(8,128)} %param.10) | non-fusion elementwise | flops 131072 | bytes 786432 | tf_op jit(solution)/shard_map/convert_element_type | solution.py:271
  1.2 2.0 %fusion.6.lv_ref = f32[3,256,128]{2,1,0:T(8,128)S(1)} fusion(bf16[3,1024,256]{2,1,0:T(8,128)(2,1)} %param.15, bf16[1024,128]{1,0:T(8,128)(2,1)S(1)} %convert_element_type.26), kind=kOutput, calls=%fused_computation.12 | convolution fusion | flops 201326592 | bytes 2228224 | tf_op jit(solution)/shard_map/blr,lw->brw/dot_general | solution.py:276
  3.2 0.0 copy-start.5
  3.3 3.5 %convolution_convert_fusion = bf16[2048,128]{1,0:T(8,128)(2,1)S(1)} fusion(bf16[1024,2048]{1,0:T(8,128)(2,1)} %param.12, bf16[1024,128]{1,0:T(8,128)(2,1)S(1)} %convert_element_type.26), kind=kOutput, calls=%fused_computation | convolution fusion | flops 537133056 | bytes 4980736 | tf_op jit(solution)/shard_map/dot_general | solution.py:280
  6.8 0.0 copy-start.4
  6.8 0.0 copy-done.5
  6.8 0.5 fusion.4
  7.3 0.1 copy.43.x_ref
  7.4 0.4 copy-done.4
  7.8 0.3 fusion.23
  8.2 16.9 %shard_map.100 = (bf16[16,128,128]{2,1,0:T(8,128)(2,1)S(1)}, f32[16,128]{1,0:T(8,128)S(1)}, f32[2,256,128]{2,1,0:T(8,128)S(1)}, f32[2,256,128]{2,1,0:T(8,128)S(1)}) custom-call(bf16[16,128,128]{2,1,0:T(8,128)(2,1)S(1)} %copy.43.x_ref, f32[16,16,128]{2,1,0:T(8,128)S(1)} %bitcast.46, f32[3,256,128]{2,1,0:T(8,128)S(1)} %fusion.6.lv_ref), custom_call_target="tpu_custom_call" | custom-call | tf_op jit(solution)/shard_map/pallas_call | solution.py:96
  25.2 22.7 %shard_map.101 = (bf16[16,128,128]{2,1,0:T(8,128)(2,1)S(1)}, f32[16,16,128]{2,1,0:T(8,128)S(1)}, bf16[256,128]{1,0:T(8,128)(2,1)S(1)}, f32[256,128]{1,0:T(8,128)S(1)}) custom-call(bf16[2048,128]{1,0:T(8,128)(2,1)S(1)} %bitcast.47, bf16[2048,2048]{1,0:T(8,128)(2,1)} %w_ref.1, f32[16,128]{1,0:T(8,128)S(1)} %get-tuple-element.14.share_ref, ...), custom_call_target="tpu_custom_call" | custom-call | tf_op jit(solution)/shard_map/pallas_call | solution.py:223
  47.8 0.0 copy-start.2
  47.9 0.4 convolution_convert_fusion.1
  48.3 0.1 copy.25
  48.5 0.8 %copy-done.2 = bf16[3,1024,256]{2,1,0:T(8,128)(2,1)S(1)} copy-done((bf16[3,1024,256]{2,1,0:T(8,128)(2,1)S(1)}, bf16[3,1024,256]{2,1,0:T(8,128)(2,1)}, u32[]{:S(2)}) %copy-start.2) | copy-done | bytes 1572888
  49.3 0.0 copy-start.1
  49.3 0.6 %convolution_bitcast_fusion.1 = f32[1024,128]{1,0:T(8,128)S(1)} fusion(bf16[3,1024,256]{2,1,0:T(8,128)(2,1)S(1)} %copy-done.2, bf16[1,256,128]{2,1,0:T(8,128)(2,1)S(1)} %fusion.14, bf16[1,256,128]{2,1,0:T(8,128)(2,1)S(1)} %bitcast.48, bf16[1,256,128]{2,1,0:T(8,128)(2,1)S(1)} %slice.34), kind=kOutput, calls=%fused_computation.3 | convolution fusion | flops 201523200 | bytes 2293760 | tf_op jit(solution)/shard_map/blr,brw->lw/dot_general | solution.py:308
  49.8 0.0 copy-done
  49.9 0.7 %fusion.22 = f32[1024,128]{1,0:T(8,128)S(1)} fusion(bf16[1024,1024]{1,0:T(8,128)(2,1)S(1)} %copy-done, bf16[1024,128]{1,0:T(8,128)(2,1)S(1)} %convert_element_type.26), kind=kOutput, calls=%fused_computation.31 | convolution fusion | flops 268435456 | bytes 2883584 | tf_op jit(solution)/shard_map/dot_general | solution.py:279
  50.6 0.9 %copy-done.1 = bf16[1024,2048]{1,0:T(8,128)(2,1)S(1)} copy-done((bf16[1024,2048]{1,0:T(8,128)(2,1)S(1)}, bf16[1024,2048]{1,0:T(8,128)(2,1)}, u32[]{:S(2)}) %copy-start.1) | copy-done | bytes 4194328
  51.4 0.0 copy-start.3
  51.5 1.3 %fusion.2 = f32[1024,128]{1,0:T(8,128)S(1)} fusion(f32[1024,128]{1,0:T(8,128)S(1)} %convolution_bitcast_fusion.1, f32[1024,128]{1,0:T(8,128)S(1)} %fusion.22, bf16[1024,2048]{1,0:T(8,128)(2,1)S(1)} %copy-done.1, bf16[2048,128]{1,0:T(8,128)(2,1)S(1)} %bitcast.49), kind=kOutput, calls=%fused_computation.7 | convolution fusion | flops 537133056 | bytes 6291456 | tf_op jit(solution)/shard_map/dot_general | solution.py:302
  52.7 0.0 copy-done.3
  52.7 1.1 %fusion = f32[1024,128]{1,0:T(8,128)} fusion(f32[1024,128]{1,0:T(8,128)S(1)} %fusion.2, bf16[1024,256]{1,0:T(8,128)(2,1)S(1)} %copy-done.3, bf16[256,128]{1,0:T(8,128)(2,1)S(1)} %bitcast.51), kind=kOutput, calls=%fused_computation.4 | convolution fusion | flops 67239936 | bytes 1638400 | tf_op jit(solution)/shard_map/dot_general | solution.py:314
  (4 shorter events, 0.1 us)
Async XLA Ops:
  0.0 49.8 %copy-start = (bf16[1024,1024]{1,0:T(8,128)(2,1)S(1)}, bf16[1024,1024]{1,0:T(8,128)(2,1)}, u32[]{:S(2)}) copy-start(bf16[1024,1024]{1,0:T(8,128)(2,1)} %param.11) | copy-start | bytes 6291460
  3.2 3.5 %copy-start.5 = (s32[16]{0:T(128)S(1)}, s32[16]{0:T(128)}, u32[]{:S(2)}) copy-start(s32[16]{0:T(128)} %param.19) | copy-start | bytes 196
  6.8 1.0 %copy-start.4 = (bf16[1024,256]{1,0:T(8,128)(2,1)S(1)}, bf16[1024,256]{1,0:T(8,128)(2,1)}, u32[]{:S(2)}) copy-start(bf16[1024,256]{1,0:T(8,128)(2,1)} %param.17) | copy-start | bytes 1572868
  47.8 1.4 %copy-start.2 = (bf16[3,1024,256]{2,1,0:T(8,128)(2,1)S(1)}, bf16[3,1024,256]{2,1,0:T(8,128)(2,1)}, u32[]{:S(2)}) copy-start(bf16[3,1024,256]{2,1,0:T(8,128)(2,1)} %param.16) | copy-start | bytes 4718596
  49.3 2.2 %copy-start.1 = (bf16[1024,2048]{1,0:T(8,128)(2,1)S(1)}, bf16[1024,2048]{1,0:T(8,128)(2,1)}, u32[]{:S(2)}) copy-start(bf16[1024,2048]{1,0:T(8,128)(2,1)} %param.14) | copy-start | bytes 12582916
  51.4 1.3 %copy-start.3 = (bf16[1024,256]{1,0:T(8,128)(2,1)S(1)}, bf16[1024,256]{1,0:T(8,128)(2,1)}, u32[]{:S(2)}) copy-start(bf16[1024,256]{1,0:T(8,128)(2,1)} %param.18) | copy-start | bytes 1572868

commit v10 on v9

--- a/solution.py
+++ b/solution.py
@@ -132,6 +132,19 @@
     row = lax.axis_index("row")
     piece_rows = mixed.shape[1]
     row_peers = [(s, lax.rem(row + s, m), lax.rem(row + m - s, m)) for s in range(1, m)]
+
+    def compute(peer):
+        first = pl.multiple_of(peer * piece_rows, piece_rows)
+        mixed[peer] = jnp.dot(
+            w_ref[pl.ds(first, piece_rows), :], a_ref[...], preferred_element_type=jnp.float32
+        ).astype(mixed.dtype)
+
+    def compute_one(peer, carry):
+        compute(peer)
+        return carry
+
+    lax.fori_loop(0, n, compute_one, 0)
+
     barrier = pltpu.get_barrier_semaphore()
     for s, peer, _ in col_peers(n):
         pl.semaphore_signal(barrier, inc=1, device_id=(row, peer), device_id_type=MESH_ID)
@@ -169,20 +182,10 @@
             device_id=(row, peer), device_id_type=MESH_ID,
         )
 
-    def compute(peer):
-        first = pl.multiple_of(peer * piece_rows, piece_rows)
-        mixed[peer] = jnp.dot(
-            w_ref[pl.ds(first, piece_rows), :], a_ref[...], preferred_element_type=jnp.float32
-        ).astype(mixed.dtype)
-
-    def compute_and_send(s, carry):
-        peer = lax.rem(me + s, n)
-        compute(peer)
+    for s, peer, _ in col_peers(n):
         piece(s, peer, me).start()
-        return carry
-
-    half = n // 2
-    lax.fori_loop(1, half, compute_and_send, 0)
+    local = pltpu.make_async_copy(mixed.at[me], o_ref.at[me], local_sems.at[0])
+    local.start()
 
     def spread(s, peer, slot):
         return pltpu.make_async_remote_copy(
@@ -201,10 +204,6 @@
     for s, peer, _ in col_peers(n):
         spread(s, peer, me).start()
 
-    lax.fori_loop(half, n, compute_and_send, 0)
-    compute(me)
-    local = pltpu.make_async_copy(mixed.at[me], o_ref.at[me], local_sems.at[0])
-    local.start()
 
     for s, peer, source in col_peers(n):
         spread(s, peer, me).wait_send()

time: 54.1 us -> 56.3 us (1.041)
  Pallas kernels: 39.6 us -> 41.8 us
    pallas_call x1, Pallas kernels: 22.7 us -> 24.8 us  [gather(): pl.pallas_call(functools.partial(gather_kernel, n, m), out_shape=(jax.Sha...]
where the time goes in v10:
time: 56.3 us; the launch traced here: 56 us
  Pallas kernels  41.8 us (74%)
  matrix products  10.4 us (18%)
  local copies, waits for them, and re-layouts  2.34 us (4%)
  other arithmetic  1.29 us (2%)
    pallas_call x1, Pallas kernels, gather(): pl.pallas_call(functools.partial(gather_kernel, n, m), out_shape=(jax.Sha...  24.8 us
    pallas_call x1, Pallas kernels, scatter(): pl.pallas_call(functools.partial(scatter_kernel, n), out_shape=(jax.Shape...  16.9 us
    dot_general x1, matrix products, per_device(): lax.dot_general(compress, lowered, contract_first, preferred_element_type...  3.51 us
    unnamed x12, local copies, waits for them, and re-layouts  2.06 us
    dot_general x1, matrix products, per_device(): jnp.einsum('blr,lw->brw', row_project, lowered, preferred_element_type=jn...  2.02 us
    dot_general x1, matrix products, per_device(): cluster_part = jnp.dot(expand, ordered, preferred_element_type=jnp.float32)  1.26 us
    convert_element_type x1, other arithmetic, per_device(): lowered = right_side.astype(jnp.bfloat16)  1.22 us

profile of v10, /device:TPU:1, one launch (start us, length us, event | category | flops | bytes accessed | tf_op | source)
XLA Modules:
  0.0 56.0 jit_solution(16751508164827273670)
XLA Ops:
  0.0 0.0 copy-start
  0.0 1.2 %convert_element_type.26 = bf16[1024,128]{1,0:T(8,128)(2,1)S(1)} convert(f32[1024,128]{1,0:T(8,128)} %param.10) | non-fusion elementwise | flops 131072 | bytes 786432 | tf_op jit(solution)/shard_map/convert_element_type | solution.py:270
  1.2 2.0 %fusion.6.lv_ref = f32[3,256,128]{2,1,0:T(8,128)S(1)} fusion(bf16[3,1024,256]{2,1,0:T(8,128)(2,1)} %param.15, bf16[1024,128]{1,0:T(8,128)(2,1)S(1)} %convert_element_type.26), kind=kOutput, calls=%fused_computation.12 | convolution fusion | flops 201326592 | bytes 2228224 | tf_op jit(solution)/shard_map/blr,lw->brw/dot_general | solution.py:275
  3.2 0.0 copy-start.5
  3.3 3.5 %convolution_convert_fusion = bf16[2048,128]{1,0:T(8,128)(2,1)S(1)} fusion(bf16[1024,2048]{1,0:T(8,128)(2,1)} %param.12, bf16[1024,128]{1,0:T(8,128)(2,1)S(1)} %convert_element_type.26), kind=kOutput, calls=%fused_computation | convolution fusion | flops 537133056 | bytes 4980736 | tf_op jit(solution)/shard_map/dot_general | solution.py:279
  6.8 0.0 copy-start.4
  6.8 0.0 copy-done.5
  6.8 0.5 fusion.4
  7.3 0.1 copy.43.x_ref
  7.4 0.4 copy-done.4
  7.8 0.3 fusion.23
  8.2 16.9 %shard_map.100 = (bf16[16,128,128]{2,1,0:T(8,128)(2,1)S(1)}, f32[16,128]{1,0:T(8,128)S(1)}, f32[2,256,128]{2,1,0:T(8,128)S(1)}, f32[2,256,128]{2,1,0:T(8,128)S(1)}) custom-call(bf16[16,128,128]{2,1,0:T(8,128)(2,1)S(1)} %copy.43.x_ref, f32[16,16,128]{2,1,0:T(8,128)S(1)} %bitcast.46, f32[3,256,128]{2,1,0:T(8,128)S(1)} %fusion.6.lv_ref), custom_call_target="tpu_custom_call" | custom-call | tf_op jit(solution)/shard_map/pallas_call | solution.py:96
  25.2 24.8 %shard_map.101 = (bf16[16,128,128]{2,1,0:T(8,128)(2,1)S(1)}, f32[16,16,128]{2,1,0:T(8,128)S(1)}, bf16[256,128]{1,0:T(8,128)(2,1)S(1)}, f32[256,128]{1,0:T(8,128)S(1)}) custom-call(bf16[2048,128]{1,0:T(8,128)(2,1)S(1)} %bitcast.47, bf16[2048,2048]{1,0:T(8,128)(2,1)} %w_ref.1, f32[16,128]{1,0:T(8,128)S(1)} %get-tuple-element.14.share_ref, ...), custom_call_target="tpu_custom_call" | custom-call | tf_op jit(solution)/shard_map/pallas_call | solution.py:222
  50.0 0.0 copy-start.2
  50.0 0.4 convolution_convert_fusion.1
  50.4 0.1 copy.25
  50.6 0.8 %copy-done.2 = bf16[3,1024,256]{2,1,0:T(8,128)(2,1)S(1)} copy-done((bf16[3,1024,256]{2,1,0:T(8,128)(2,1)S(1)}, bf16[3,1024,256]{2,1,0:T(8,128)(2,1)}, u32[]{:S(2)}) %copy-start.2) | copy-done | bytes 1572888
  51.4 0.0 copy-start.1
  51.4 0.6 %convolution_bitcast_fusion.1 = f32[1024,128]{1,0:T(8,128)S(1)} fusion(bf16[3,1024,256]{2,1,0:T(8,128)(2,1)S(1)} %copy-done.2, bf16[1,256,128]{2,1,0:T(8,128)(2,1)S(1)} %fusion.14, bf16[1,256,128]{2,1,0:T(8,128)(2,1)S(1)} %bitcast.48, bf16[1,256,128]{2,1,0:T(8,128)(2,1)S(1)} %slice.34), kind=kOutput, calls=%fused_computation.3 | convolution fusion | flops 201523200 | bytes 2293760 | tf_op jit(solution)/shard_map/blr,brw->lw/dot_general | solution.py:307
  52.0 0.0 copy-done
  52.0 0.7 %fusion.22 = f32[1024,128]{1,0:T(8,128)S(1)} fusion(bf16[1024,1024]{1,0:T(8,128)(2,1)S(1)} %copy-done, bf16[1024,128]{1,0:T(8,128)(2,1)S(1)} %convert_element_type.26), kind=kOutput, calls=%fused_computation.31 | convolution fusion | flops 268435456 | bytes 2883584 | tf_op jit(solution)/shard_map/dot_general | solution.py:278
  52.7 0.9 %copy-done.1 = bf16[1024,2048]{1,0:T(8,128)(2,1)S(1)} copy-done((bf16[1024,2048]{1,0:T(8,128)(2,1)S(1)}, bf16[1024,2048]{1,0:T(8,128)(2,1)}, u32[]{:S(2)}) %copy-start.1) | copy-done | bytes 4194328
  53.6 0.0 copy-start.3
  53.6 1.3 %fusion.2 = f32[1024,128]{1,0:T(8,128)S(1)} fusion(f32[1024,128]{1,0:T(8,128)S(1)} %convolution_bitcast_fusion.1, f32[1024,128]{1,0:T(8,128)S(1)} %fusion.22, bf16[1024,2048]{1,0:T(8,128)(2,1)S(1)} %copy-done.1, bf16[2048,128]{1,0:T(8,128)(2,1)S(1)} %bitcast.49), kind=kOutput, calls=%fused_computation.7 | convolution fusion | flops 537133056 | bytes 6291456 | tf_op jit(solution)/shard_map/dot_general | solution.py:301
  54.9 0.0 copy-done.3
  54.9 1.1 %fusion = f32[1024,128]{1,0:T(8,128)} fusion(f32[1024,128]{1,0:T(8,128)S(1)} %fusion.2, bf16[1024,256]{1,0:T(8,128)(2,1)S(1)} %copy-done.3, bf16[256,128]{1,0:T(8,128)(2,1)S(1)} %bitcast.51), kind=kOutput, calls=%fused_computation.4 | convolution fusion | flops 67239936 | bytes 1638400 | tf_op jit(solution)/shard_map/dot_general | solution.py:313
  (4 shorter events, 0.1 us)
Async XLA Ops:
  0.0 52.0 %copy-start = (bf16[1024,1024]{1,0:T(8,128)(2,1)S(1)}, bf16[1024,1024]{1,0:T(8,128)(2,1)}, u32[]{:S(2)}) copy-start(bf16[1024,1024]{1,0:T(8,128)(2,1)} %param.11) | copy-start | bytes 6291460
  3.2 3.5 %copy-start.5 = (s32[16]{0:T(128)S(1)}, s32[16]{0:T(128)}, u32[]{:S(2)}) copy-start(s32[16]{0:T(128)} %param.19) | copy-start | bytes 196
  6.8 1.0 %copy-start.4 = (bf16[1024,256]{1,0:T(8,128)(2,1)S(1)}, bf16[1024,256]{1,0:T(8,128)(2,1)}, u32[]{:S(2)}) copy-start(bf16[1024,256]{1,0:T(8,128)(2,1)} %param.17) | copy-start | bytes 1572868
  50.0 1.4 %copy-start.2 = (bf16[3,1024,256]{2,1,0:T(8,128)(2,1)S(1)}, bf16[3,1024,256]{2,1,0:T(8,128)(2,1)}, u32[]{:S(2)}) copy-start(bf16[3,1024,256]{2,1,0:T(8,128)(2,1)} %param.16) | copy-start | bytes 4718596
  51.4 2.2 %copy-start.1 = (bf16[1024,2048]{1,0:T(8,128)(2,1)S(1)}, bf16[1024,2048]{1,0:T(8,128)(2,1)}, u32[]{:S(2)}) copy-start(bf16[1024,2048]{1,0:T(8,128)(2,1)} %param.14) | copy-start | bytes 12582916
  53.6 1.3 %copy-start.3 = (bf16[1024,256]{1,0:T(8,128)(2,1)S(1)}, bf16[1024,256]{1,0:T(8,128)(2,1)}, u32[]{:S(2)}) copy-start(bf16[1024,256]{1,0:T(8,128)(2,1)} %param.18) | copy-start | bytes 1572868

commit v11 on v9

--- a/solution.py
+++ b/solution.py
@@ -29,6 +29,7 @@
 ):
     me = lax.axis_index("col")
     row = lax.axis_index("row")
+    width = x_ref.shape[1] // n
     barrier = pltpu.get_barrier_semaphore()
     for s, peer, _ in col_peers(n):
         pl.semaphore_signal(barrier, inc=1, device_id=(row, peer), device_id_type=MESH_ID)
@@ -56,14 +57,18 @@
         )
     for copy in level_copies:
         copy.start()
-    local = pltpu.make_async_copy(x_ref.at[me], o_ref.at[me], local_sems.at[0])
+    local = pltpu.make_async_copy(
+        x_ref.at[:, pl.ds(me * width, width)], o_ref.at[:, pl.ds(me * width, width)],
+        local_sems.at[0],
+    )
     local.start()
     own = pltpu.make_async_copy(r_ref.at[me], got.at[me], local_sems.at[1])
     own.start()
 
     def piece(s, peer, slot):
         return pltpu.make_async_remote_copy(
-            src_ref=x_ref.at[peer], dst_ref=o_ref.at[slot],
+            src_ref=x_ref.at[:, pl.ds(peer * width, width)],
+            dst_ref=o_ref.at[:, pl.ds(slot * width, width)],
             send_sem=sems.at[0, s], recv_sem=sems.at[1, s],
             device_id=(row, peer), device_id_type=MESH_ID,
         )
@@ -92,7 +97,7 @@
 
 
 def scatter(x, r, lv):
-    n = x.shape[0]
+    n = r.shape[0]
     return pl.pallas_call(
         functools.partial(scatter_kernel, n),
         out_shape=(
@@ -126,7 +131,7 @@
 
 def gather_kernel(
     n, m, a_ref, w_ref, share_ref, c1_ref, p_ref, o_ref, full_ref, got1, got2,
-    mixed, rows_got, total, sems, row_sems, local_sems, sib_sems,
+    mixed, rows_got, total, rounded, sems, row_sems, local_sems, sib_sems,
 ):
     me = lax.axis_index("col")
     row = lax.axis_index("row")
@@ -171,8 +176,9 @@
 
     def compute(peer):
         first = pl.multiple_of(peer * piece_rows, piece_rows)
-        mixed[peer] = jnp.dot(
-            w_ref[pl.ds(first, piece_rows), :], a_ref[...], preferred_element_type=jnp.float32
+        mixed[peer] = lax.dot_general(
+            w_ref[pl.ds(first, piece_rows), :], a_ref[...], (((1,), (1,)), ((), ())),
+            preferred_element_type=jnp.float32,
         ).astype(mixed.dtype)
 
     def compute_and_send(s, carry):
@@ -186,7 +192,7 @@
 
     def spread(s, peer, slot):
         return pltpu.make_async_remote_copy(
-            src_ref=total, dst_ref=full_ref.at[slot],
+            src_ref=rounded, dst_ref=full_ref.at[slot],
             send_sem=sems.at[2, s], recv_sem=sems.at[3, s],
             device_id=(row, peer), device_id_type=MESH_ID,
         )
@@ -196,7 +202,8 @@
         part(s, source, source).wait_recv()
     own.wait()
     total[...] = jnp.sum(rows_got[...], axis=0)
-    mine = pltpu.make_async_copy(total, full_ref.at[me], local_sems.at[2])
+    rounded[...] = total[...].astype(rounded.dtype)
+    mine = pltpu.make_async_copy(rounded, full_ref.at[me], local_sems.at[2])
     mine.start()
     for s, peer, _ in col_peers(n):
         spread(s, peer, me).start()
@@ -219,12 +226,12 @@
 
 def gather(a, w, share, c1, p, n, m):
     piece_rows = w.shape[0] // n
-    columns = a.shape[1]
+    columns = a.shape[0]
     return pl.pallas_call(
         functools.partial(gather_kernel, n, m),
         out_shape=(
             jax.ShapeDtypeStruct((n, piece_rows, columns), a.dtype),
-            jax.ShapeDtypeStruct((n,) + share.shape, share.dtype),
+            jax.ShapeDtypeStruct((n,) + share.shape, jnp.bfloat16),
             jax.ShapeDtypeStruct(c1.shape, c1.dtype),
             jax.ShapeDtypeStruct(p.shape, p.dtype),
         ),
@@ -245,6 +252,7 @@
             pltpu.VMEM((n, piece_rows, columns), a.dtype),
             pltpu.VMEM((m,) + share.shape, share.dtype),
             pltpu.VMEM(share.shape, share.dtype),
+            pltpu.VMEM(share.shape, jnp.bfloat16),
             pltpu.SemaphoreType.DMA((4, n)),
             pltpu.SemaphoreType.DMA((2, m)),
             pltpu.SemaphoreType.DMA((3,)),
@@ -271,29 +279,31 @@
     lowered = right_side.astype(jnp.bfloat16)
     columns = lowered.shape[1]
     root_term = lax.dot_general(
-        root_project, lowered, contract_first, preferred_element_type=jnp.float32
+        lowered, root_project, contract_first, preferred_element_type=jnp.float32
     )
     level_coeffs = jnp.einsum(
-        "blr,lw->brw", row_project, lowered, preferred_element_type=jnp.float32
+        "lw,blr->bwr", lowered, row_project, preferred_element_type=jnp.float32
     )
     dense_part = jnp.dot(leaf_inverse, lowered, preferred_element_type=jnp.float32)
     coeffs = lax.dot_general(
-        compress, lowered, contract_first, preferred_element_type=jnp.float32
+        lowered, compress, contract_first, preferred_element_type=jnp.float32
     ).astype(jnp.bfloat16)
     col_count = lax.axis_size("col")
-    pieces = coeffs.reshape(col_count, -1, columns)
+    pieces = coeffs.reshape(columns, col_count, -1)
     chosen = (owner_map[:, None] == jnp.arange(col_count, dtype=owner_map.dtype)[None, :]).astype(
         jnp.bfloat16
     )
     outgoing = jnp.einsum(
-        "kd,kxw->dxw", chosen, pieces, preferred_element_type=jnp.float32
+        "kd,wkx->wdx", chosen, pieces, preferred_element_type=jnp.float32
     ).astype(jnp.bfloat16)
-    root_shares = root_term.reshape(col_count, -1, columns)
-    arrived, root_share, pair, far = scatter(outgoing, root_shares, level_coeffs)
+    root_shares = root_term.reshape(col_count, -1, root_term.shape[1])
+    arrived, root_share, pair, far = scatter(
+        outgoing.reshape(columns, -1), root_shares, level_coeffs
+    )
     pair_sum = (level_coeffs[1] + pair[1]).astype(jnp.bfloat16)
     far_sum = far[0] + far[1]
     returned, root_full, quad_one, quad_two = gather(
-        arrived.reshape(-1, columns), middle, root_share, pair_sum, far_sum, col_count,
+        arrived, middle, root_share, pair_sum, far_sum, col_count,
         lax.axis_size("row"),
     )
     ordered = jnp.einsum(
@@ -304,15 +314,15 @@
     sibling_sum = jnp.stack(
         [pair[0], quad_one.astype(jnp.float32), far_sum + quad_two], axis=0
     )
-    root_sum = root_full.reshape(-1, columns)
+    root_coeffs = root_full.reshape(columns, -1)
     coupled = jnp.einsum(
-        "blr,brw->lw",
+        "blr,bwr->lw",
         row_expand,
         sibling_sum.astype(jnp.bfloat16),
         preferred_element_type=jnp.float32,
     )
-    root_part = jnp.dot(
-        root_expand, root_sum.astype(jnp.bfloat16), preferred_element_type=jnp.float32
+    root_part = lax.dot_general(
+        root_expand, root_coeffs, (((1,), (1,)), ((), ())), preferred_element_type=jnp.float32
     )
     return dense_part + cluster_part + coupled + root_part
 

time: 54.1 us -> 53.1 us (0.982)
  matrix products: 10.4 us -> 9.51 us
    dot_general x6, matrix products: 8.02 us -> 7.12 us  [the longest x1 2.94 us: per_device(): lax.dot_general(lowered, compress, contract_first, preferred_element_type...]
    unnamed x12 -> x14, local copies, waits for them, and re-layouts: 2.06 us -> 2.27 us
where the time goes in v11:
time: 53.1 us; the launch traced here: 52.8 us
  Pallas kernels  39.4 us (74%)
  matrix products  9.51 us (18%)
  local copies, waits for them, and re-layouts  2.42 us (5%)
  other arithmetic  1.28 us (2%)
    pallas_call x1, Pallas kernels, gather(): pl.pallas_call(functools.partial(gather_kernel, n, m), out_shape=(jax.Sha...  22.4 us
    pallas_call x1, Pallas kernels, scatter(): pl.pallas_call(functools.partial(scatter_kernel, n), out_shape=(jax.Shape...  17 us
    dot_general x1, matrix products, per_device(): lax.dot_general(lowered, compress, contract_first, preferred_element_type...  2.94 us
    unnamed x14, local copies, waits for them, and re-layouts  2.27 us
    dot_general x1, matrix products, per_device(): jnp.einsum('lw,blr->bwr', lowered, row_project, preferred_element_type=jn...  1.83 us
    dot_general x1, matrix products, per_device(): cluster_part = jnp.dot(expand, ordered, preferred_element_type=jnp.float32)  1.26 us
    convert_element_type x1, other arithmetic, per_device(): lowered = right_side.astype(jnp.bfloat16)  1.22 us
    dot_general x1, matrix products, per_device(): lax.dot_general(root_expand, root_coeffs, (((1,), (1,)), ((), ())), prefe...  1.1 us

profile of v11, /device:TPU:1, one launch (start us, length us, event | category | flops | bytes accessed | tf_op | source)
XLA Modules:
  0.0 52.8 jit_solution(1743577957636307825)
XLA Ops:
  0.0 0.0 copy-start
  0.0 1.2 %convert_element_type.23 = bf16[1024,128]{1,0:T(8,128)(2,1)S(1)} convert(f32[1024,128]{1,0:T(8,128)} %param.10) | non-fusion elementwise | flops 131072 | bytes 786432 | tf_op jit(solution)/shard_map/convert_element_type | solution.py:279
  1.2 1.8 %convolution_bitcast_fusion.3.lv_ref = f32[3,128,256]{2,1,0:T(8,128)S(1)} fusion(bf16[3,1024,256]{2,1,0:T(8,128)(2,1)} %param.15, bf16[1024,128]{1,0:T(8,128)(2,1)S(1)} %convert_element_type.23), kind=kOutput, calls=%fused_computation.10 | convolution fusion | flops 201326592 | bytes 2228224 | tf_op jit(solution)/shard_map/lw,blr->bwr/dot_general | solution.py:284
  3.1 0.0 copy-start.5
  3.1 2.9 %fusion = bf16[16,8,16,128]{3,1,2,0:T(8,128)(2,1)S(1)} fusion(bf16[1024,128]{1,0:T(8,128)(2,1)S(1)} %convert_element_type.23, bf16[1024,2048]{1,0:T(8,128)(2,1)} %param.12), kind=kOutput, calls=%fused_computation.3 | convolution fusion | flops 537133056 | bytes 4980736 | tf_op jit(solution)/shard_map/dot_general | solution.py:288
  6.0 0.0 copy-start.4
  6.0 0.1 copy.34
  6.2 0.0 copy-done.5
  6.2 0.4 convolution_convert_fusion.2
  6.6 0.1 copy.39
  6.7 0.3 copy-done.4
  7.1 0.3 convolution_bitcast_fusion.4.r_ref
  7.3 17.0 %shard_map.100 = (bf16[128,2048]{1,0:T(8,128)(2,1)S(1)}, f32[8,256]{1,0:T(8,128)S(1)}, f32[2,128,256]{2,1,0:T(8,128)S(1)}, f32[2,128,256]{2,1,0:T(8,128)S(1)}) custom-call(bf16[128,2048]{1,0:T(8,128)(2,1)S(1)} %bitcast.57, f32[16,8,256]{2,1,0:T(8,128)S(1)} %convolution_bitcast_fusion.4.r_ref, f32[3,128,256]{2,1,0:T(8,128)S(1)} %convolution_bitcast_fusion.3.lv_ref), custom_call_target="tpu_custom_call" | custom-call | tf_op jit(solution)/shard_map/pallas_call | solution.py:101
  24.4 22.4 %shard_map.101 = (bf16[16,128,128]{2,1,0:T(8,128)(2,1)S(1)}, bf16[16,8,256]{2,1,0:T(8,128)(2,1)S(1)}, bf16[128,256]{1,0:T(8,128)(2,1)S(1)}, f32[128,256]{1,0:T(8,128)S(1)}) custom-call(bf16[128,2048]{1,0:T(8,128)(2,1)S(1)} %get-tuple-element.13.a_ref, bf16[2048,2048]{1,0:T(8,128)(2,1)} %w_ref.1, f32[8,256]{1,0:T(8,128)S(1)} %get-tuple-element.14.share_ref, ...), custom_call_target="tpu_custom_call" | custom-call | tf_op jit(solution)/shard_map/pallas_call | solution.py:230
  46.8 0.0 copy-start.2
  46.8 0.4 convolution_convert_fusion.1
  47.3 0.1 copy.22
  47.5 0.8 %copy-done.2 = bf16[3,1024,256]{2,1,0:T(8,128)(2,1)S(1)} copy-done((bf16[3,1024,256]{2,1,0:T(8,128)(2,1)S(1)}, bf16[3,1024,256]{2,1,0:T(8,128)(2,1)}, u32[]{:S(2)}) %copy-start.2) | copy-done | bytes 1572888
  48.2 0.0 copy-start.1
  48.2 0.6 %convolution_bitcast_fusion.1 = f32[1024,128]{1,0:T(8,128)S(1)} fusion(bf16[3,1024,256]{2,1,0:T(8,128)(2,1)S(1)} %copy-done.2, bf16[1,128,256]{2,1,0:T(8,128)(2,1)S(1)} %fusion.12, bf16[1,128,256]{2,1,0:T(8,128)(2,1)S(1)} %bitcast.58, bf16[1,128,256]{2,1,0:T(8,128)(2,1)S(1)} %slice.34), kind=kOutput, calls=%fused_computation.5 | convolution fusion | flops 201523200 | bytes 2293760 | tf_op jit(solution)/shard_map/blr,bwr->lw/dot_general | solution.py:318
  48.8 0.0 copy-done
  48.8 0.7 %fusion.21 = f32[1024,128]{1,0:T(8,128)S(1)} fusion(bf16[1024,1024]{1,0:T(8,128)(2,1)S(1)} %copy-done, bf16[1024,128]{1,0:T(8,128)(2,1)S(1)} %convert_element_type.23), kind=kOutput, calls=%fused_computation.33 | convolution fusion | flops 268435456 | bytes 2883584 | tf_op jit(solution)/shard_map/dot_general | solution.py:287
  49.5 0.9 %copy-done.1 = bf16[1024,2048]{1,0:T(8,128)(2,1)S(1)} copy-done((bf16[1024,2048]{1,0:T(8,128)(2,1)S(1)}, bf16[1024,2048]{1,0:T(8,128)(2,1)}, u32[]{:S(2)}) %copy-start.1) | copy-done | bytes 4194328
  50.4 0.0 copy-start.3
  50.4 1.3 %fusion.3 = f32[1024,128]{1,0:T(8,128)S(1)} fusion(f32[1024,128]{1,0:T(8,128)S(1)} %convolution_bitcast_fusion.1, f32[1024,128]{1,0:T(8,128)S(1)} %fusion.21, bf16[1024,2048]{1,0:T(8,128)(2,1)S(1)} %copy-done.1, bf16[2048,128]{1,0:T(8,128)(2,1)S(1)} %bitcast.61), kind=kOutput, calls=%fused_computation.9 | convolution fusion | flops 537133056 | bytes 6291456 | tf_op jit(solution)/shard_map/dot_general | solution.py:312
  51.7 0.0 copy-done.3
  51.7 1.1 %fusion.1 = f32[1024,128]{1,0:T(8,128)} fusion(f32[1024,128]{1,0:T(8,128)S(1)} %fusion.3, bf16[1024,256]{1,0:T(8,128)(2,1)S(1)} %copy-done.3, bf16[16,8,256]{2,1,0:T(8,128)(2,1)S(1)} %get-tuple-element.20), kind=kOutput, calls=%fused_computation.6 | convolution fusion | flops 67239936 | bytes 1638400 | tf_op jit(solution)/shard_map/dot_general | solution.py:324
  (3 shorter events, 0.1 us)
Async XLA Ops:
  0.0 48.8 %copy-start = (bf16[1024,1024]{1,0:T(8,128)(2,1)S(1)}, bf16[1024,1024]{1,0:T(8,128)(2,1)}, u32[]{:S(2)}) copy-start(bf16[1024,1024]{1,0:T(8,128)(2,1)} %param.11) | copy-start | bytes 6291460
  3.1 3.1 %copy-start.5 = (s32[16]{0:T(128)S(1)}, s32[16]{0:T(128)}, u32[]{:S(2)}) copy-start(s32[16]{0:T(128)} %param.19) | copy-start | bytes 196
  6.0 1.0 %copy-start.4 = (bf16[1024,256]{1,0:T(8,128)(2,1)S(1)}, bf16[1024,256]{1,0:T(8,128)(2,1)}, u32[]{:S(2)}) copy-start(bf16[1024,256]{1,0:T(8,128)(2,1)} %param.17) | copy-start | bytes 1572868
  46.8 1.4 %copy-start.2 = (bf16[3,1024,256]{2,1,0:T(8,128)(2,1)S(1)}, bf16[3,1024,256]{2,1,0:T(8,128)(2,1)}, u32[]{:S(2)}) copy-start(bf16[3,1024,256]{2,1,0:T(8,128)(2,1)} %param.16) | copy-start | bytes 4718596
  48.2 2.2 %copy-start.1 = (bf16[1024,2048]{1,0:T(8,128)(2,1)S(1)}, bf16[1024,2048]{1,0:T(8,128)(2,1)}, u32[]{:S(2)}) copy-start(bf16[1024,2048]{1,0:T(8,128)(2,1)} %param.14) | copy-start | bytes 12582916
  50.4 1.3 %copy-start.3 = (bf16[1024,256]{1,0:T(8,128)(2,1)S(1)}, bf16[1024,256]{1,0:T(8,128)(2,1)}, u32[]{:S(2)}) copy-start(bf16[1024,256]{1,0:T(8,128)(2,1)} %param.18) | copy-start | bytes 1572868

commit v12 on v11

--- a/solution.py
+++ b/solution.py
@@ -25,7 +25,7 @@
 
 
 def scatter_kernel(
-    n, x_ref, r_ref, lv_ref, o_ref, share_ref, pair_ref, far_ref, got, sems, local_sems, pair_sems,
+    n, x_ref, r_ref, lv_ref, e0_ref, o_ref, share_ref, pair_ref, far_ref, got, sems, local_sems, pair_sems,
 ):
     me = lax.axis_index("col")
     row = lax.axis_index("row")
@@ -96,7 +96,7 @@
         copy.wait()
 
 
-def scatter(x, r, lv):
+def scatter(x, r, lv, staged):
     n = r.shape[0]
     return pl.pallas_call(
         functools.partial(scatter_kernel, n),
@@ -110,6 +110,7 @@
             pl.BlockSpec(memory_space=pl.ANY),
             pl.BlockSpec(memory_space=pltpu.VMEM),
             pl.BlockSpec(memory_space=pl.ANY),
+            pl.BlockSpec(memory_space=pltpu.VMEM),
         ],
         out_specs=(
             pl.BlockSpec(memory_space=pl.ANY),
@@ -126,11 +127,11 @@
         compiler_params=pltpu.CompilerParams(
             collective_id=0, has_side_effects=True, vmem_limit_bytes=4 * 1024 * 1024
         ),
-    )(x, r, lv)
+    )(x, r, lv, staged)
 
 
 def gather_kernel(
-    n, m, a_ref, w_ref, share_ref, c1_ref, p_ref, o_ref, full_ref, got1, got2,
+    n, m, a_ref, w_ref, share_ref, c1_ref, p_ref, e2_ref, e3_ref, o_ref, full_ref, got1, got2,
     mixed, rows_got, total, rounded, sems, row_sems, local_sems, sib_sems,
 ):
     me = lax.axis_index("col")
@@ -224,7 +225,7 @@
         sib.wait()
 
 
-def gather(a, w, share, c1, p, n, m):
+def gather(a, w, share, c1, p, staged, n, m):
     piece_rows = w.shape[0] // n
     columns = a.shape[0]
     return pl.pallas_call(
@@ -241,7 +242,8 @@
             pl.BlockSpec(memory_space=pltpu.VMEM),
             pl.BlockSpec(memory_space=pl.ANY),
             pl.BlockSpec(memory_space=pl.ANY),
-        ],
+        ]
+        + [pl.BlockSpec(memory_space=pltpu.VMEM)] * len(staged),
         out_specs=(
             pl.BlockSpec(memory_space=pl.ANY),
             pl.BlockSpec(memory_space=pltpu.VMEM),
@@ -261,7 +263,7 @@
         compiler_params=pltpu.CompilerParams(
             collective_id=1, has_side_effects=True, vmem_limit_bytes=48 * 1024 * 1024
         ),
-    )(a, w, share, c1, p)
+    )(a, w, share, c1, p, *staged)
 
 
 def per_device(
@@ -298,12 +300,12 @@
     ).astype(jnp.bfloat16)
     root_shares = root_term.reshape(col_count, -1, root_term.shape[1])
     arrived, root_share, pair, far = scatter(
-        outgoing.reshape(columns, -1), root_shares, level_coeffs
+        outgoing.reshape(columns, -1), root_shares, level_coeffs, expand
     )
     pair_sum = (level_coeffs[1] + pair[1]).astype(jnp.bfloat16)
     far_sum = far[0] + far[1]
     returned, root_full, quad_one, quad_two = gather(
-        arrived, middle, root_share, pair_sum, far_sum, col_count,
+        arrived, middle, root_share, pair_sum, far_sum, (row_expand, root_expand), col_count,
         lax.axis_size("row"),
     )
     ordered = jnp.einsum(

time: 53.1 us -> 51.5 us (0.970)
  local copies, waits for them, and re-layouts: 2.42 us -> 0.77 us
    unnamed x14, local copies, waits for them, and re-layouts: 2.27 us -> 0.62 us
where the time goes in v12:
time: 51.5 us; the launch traced here: 51.3 us
  Pallas kernels  39.4 us (77%)
  matrix products  9.67 us (19%)
  other arithmetic  1.27 us (2%)
  local copies, waits for them, and re-layouts  0.77 us (1%)
    pallas_call x1, Pallas kernels, gather(): pl.pallas_call(functools.partial(gather_kernel, n, m), out_shape=(jax.Sha...  22.4 us
    pallas_call x1, Pallas kernels, scatter(): pl.pallas_call(functools.partial(scatter_kernel, n), out_shape=(jax.Shape...  17 us
    dot_general x1, matrix products, per_device(): lax.dot_general(lowered, compress, contract_first, preferred_element_type...  3.08 us
    dot_general x1, matrix products, per_device(): jnp.einsum('lw,blr->bwr', lowered, row_project, preferred_element_type=jn...  1.83 us
    dot_general x1, matrix products, per_device(): cluster_part = jnp.dot(expand, ordered, preferred_element_type=jnp.float32)  1.27 us
    convert_element_type x1, other arithmetic, per_device(): lowered = right_side.astype(jnp.bfloat16)  1.22 us
    dot_general x1, matrix products, per_device(): lax.dot_general(root_expand, root_coeffs, (((1,), (1,)), ((), ())), prefe...  1.09 us

profile of v12, /device:TPU:1, one launch (start us, length us, event | category | flops | bytes accessed | tf_op | source)
XLA Modules:
  0.0 51.3 jit_solution(1491941192882254981)
XLA Ops:
  0.0 0.0 copy-start
  0.0 1.2 %convert_element_type.23 = bf16[1024,128]{1,0:T(8,128)(2,1)S(1)} convert(f32[1024,128]{1,0:T(8,128)} %param.10) | non-fusion elementwise | flops 131072 | bytes 786432 | tf_op jit(solution)/shard_map/convert_element_type | solution.py:281
  1.2 1.8 %convolution_bitcast_fusion.3.lv_ref = f32[3,128,256]{2,1,0:T(8,128)S(1)} fusion(bf16[3,1024,256]{2,1,0:T(8,128)(2,1)} %param.15, bf16[1024,128]{1,0:T(8,128)(2,1)S(1)} %convert_element_type.23), kind=kOutput, calls=%fused_computation.10 | convolution fusion | flops 201326592 | bytes 2228224 | tf_op jit(solution)/shard_map/lw,blr->bwr/dot_general | solution.py:286
  3.1 0.0 copy-start.5
  3.1 0.0 copy-start.1
  3.1 3.1 %fusion = bf16[16,8,16,128]{3,1,2,0:T(8,128)(2,1)S(1)} fusion(bf16[1024,128]{1,0:T(8,128)(2,1)S(1)} %convert_element_type.23, bf16[1024,2048]{1,0:T(8,128)(2,1)} %param.12), kind=kOutput, calls=%fused_computation.3 | convolution fusion | flops 537133056 | bytes 4980736 | tf_op jit(solution)/shard_map/dot_general | solution.py:290
  6.2 0.0 copy-start.4
  6.2 0.1 copy.34
  6.3 0.0 copy-done.5
  6.3 0.4 convolution_convert_fusion.2
  6.7 0.1 copy.39
  6.9 0.3 copy-done.4
  7.2 0.3 convolution_bitcast_fusion.4.r_ref
  7.5 0.0 copy-done.1
  7.5 0.0 copy-start.2
  7.5 0.0 copy-start.3
  7.5 17.0 %shard_map.100 = (bf16[128,2048]{1,0:T(8,128)(2,1)S(1)}, f32[8,256]{1,0:T(8,128)S(1)}, f32[2,128,256]{2,1,0:T(8,128)S(1)}, f32[2,128,256]{2,1,0:T(8,128)S(1)}) custom-call(bf16[128,2048]{1,0:T(8,128)(2,1)S(1)} %bitcast.57, f32[16,8,256]{2,1,0:T(8,128)S(1)} %convolution_bitcast_fusion.4.r_ref, f32[3,128,256]{2,1,0:T(8,128)S(1)} %convolution_bitcast_fusion.3.lv_ref, ...), custom_call_target="tpu_custom_call" | custom-call | tf_op jit(solution)/shard_map/pallas_call | solution.py:101
  24.5 0.0 copy-done.2
  24.6 0.0 copy-done.3
  24.6 22.4 %shard_map.101 = (bf16[16,128,128]{2,1,0:T(8,128)(2,1)S(1)}, bf16[16,8,256]{2,1,0:T(8,128)(2,1)S(1)}, bf16[128,256]{1,0:T(8,128)(2,1)S(1)}, f32[128,256]{1,0:T(8,128)S(1)}) custom-call(bf16[128,2048]{1,0:T(8,128)(2,1)S(1)} %get-tuple-element.13.a_ref, bf16[2048,2048]{1,0:T(8,128)(2,1)} %w_ref.1, f32[8,256]{1,0:T(8,128)S(1)} %get-tuple-element.14.share_ref, ...), custom_call_target="tpu_custom_call" | custom-call | tf_op jit(solution)/shard_map/pallas_call | solution.py:231
  47.0 0.4 convolution_convert_fusion.1
  47.5 0.1 copy.22
  47.6 0.6 %convolution_bitcast_fusion.1 = f32[1024,128]{1,0:T(8,128)S(1)} fusion(bf16[3,1024,256]{2,1,0:T(8,128)(2,1)S(1)} %copy-done.2, bf16[1,128,256]{2,1,0:T(8,128)(2,1)S(1)} %fusion.12, bf16[1,128,256]{2,1,0:T(8,128)(2,1)S(1)} %bitcast.58, bf16[1,128,256]{2,1,0:T(8,128)(2,1)S(1)} %slice.34), kind=kOutput, calls=%fused_computation.5 | convolution fusion | flops 201523200 | bytes 2293760 | tf_op jit(solution)/shard_map/blr,bwr->lw/dot_general | solution.py:320
  48.2 0.0 copy-done
  48.2 0.7 %fusion.21 = f32[1024,128]{1,0:T(8,128)S(1)} fusion(bf16[1024,1024]{1,0:T(8,128)(2,1)S(1)} %copy-done, bf16[1024,128]{1,0:T(8,128)(2,1)S(1)} %convert_element_type.23), kind=kOutput, calls=%fused_computation.33 | convolution fusion | flops 268435456 | bytes 2883584 | tf_op jit(solution)/shard_map/dot_general | solution.py:289
  48.9 1.3 %fusion.3 = f32[1024,128]{1,0:T(8,128)S(1)} fusion(f32[1024,128]{1,0:T(8,128)S(1)} %convolution_bitcast_fusion.1, f32[1024,128]{1,0:T(8,128)S(1)} %fusion.21, bf16[1024,2048]{1,0:T(8,128)(2,1)S(1)} %copy-done.1, bf16[2048,128]{1,0:T(8,128)(2,1)S(1)} %bitcast.61), kind=kOutput, calls=%fused_computation.9 | convolution fusion | flops 537133056 | bytes 6291456 | tf_op jit(solution)/shard_map/dot_general | solution.py:314
  50.2 1.1 %fusion.1 = f32[1024,128]{1,0:T(8,128)} fusion(f32[1024,128]{1,0:T(8,128)S(1)} %fusion.3, bf16[1024,256]{1,0:T(8,128)(2,1)S(1)} %copy-done.3, bf16[16,8,256]{2,1,0:T(8,128)(2,1)S(1)} %get-tuple-element.20), kind=kOutput, calls=%fused_computation.6 | convolution fusion | flops 67239936 | bytes 1638400 | tf_op jit(solution)/shard_map/dot_general | solution.py:326
  (3 shorter events, 0.1 us)
Async XLA Ops:
  0.0 48.2 %copy-start = (bf16[1024,1024]{1,0:T(8,128)(2,1)S(1)}, bf16[1024,1024]{1,0:T(8,128)(2,1)}, u32[]{:S(2)}) copy-start(bf16[1024,1024]{1,0:T(8,128)(2,1)} %param.11) | copy-start | bytes 6291460
  3.1 3.2 %copy-start.5 = (s32[16]{0:T(128)S(1)}, s32[16]{0:T(128)}, u32[]{:S(2)}) copy-start(s32[16]{0:T(128)} %param.19) | copy-start | bytes 196
  3.1 4.4 %copy-start.1 = (bf16[1024,2048]{1,0:T(8,128)(2,1)S(1)}, bf16[1024,2048]{1,0:T(8,128)(2,1)}, u32[]{:S(2)}) copy-start(bf16[1024,2048]{1,0:T(8,128)(2,1)} %e0_ref.1) | copy-start | bytes 12582916
  6.2 1.0 %copy-start.4 = (bf16[1024,256]{1,0:T(8,128)(2,1)S(1)}, bf16[1024,256]{1,0:T(8,128)(2,1)}, u32[]{:S(2)}) copy-start(bf16[1024,256]{1,0:T(8,128)(2,1)} %param.17) | copy-start | bytes 1572868
  7.5 17.0 %copy-start.2 = (bf16[3,1024,256]{2,1,0:T(8,128)(2,1)S(1)}, bf16[3,1024,256]{2,1,0:T(8,128)(2,1)}, u32[]{:S(2)}) copy-start(bf16[3,1024,256]{2,1,0:T(8,128)(2,1)} %e2_ref.1) | copy-start | bytes 4718596
  7.5 17.0 %copy-start.3 = (bf16[1024,256]{1,0:T(8,128)(2,1)S(1)}, bf16[1024,256]{1,0:T(8,128)(2,1)}, u32[]{:S(2)}) copy-start(bf16[1024,256]{1,0:T(8,128)(2,1)} %e3_ref.1) | copy-start | bytes 1572868

commit v13 on v12

--- a/solution.py
+++ b/solution.py
@@ -25,7 +25,8 @@
 
 
 def scatter_kernel(
-    n, x_ref, r_ref, lv_ref, e0_ref, o_ref, share_ref, pair_ref, far_ref, got, sems, local_sems, pair_sems,
+    n, x_ref, r_ref, lv_ref, e0_ref, li_ref, y_ref, o_ref, share_ref, pair_ref, far_ref, d_ref,
+    got, sems, local_sems, pair_sems,
 ):
     me = lax.axis_index("col")
     row = lax.axis_index("row")
@@ -83,6 +84,7 @@
     for s, peer, _ in col_peers(n):
         share(s, peer, me).start()
         piece(s, peer, me).start()
+    d_ref[...] = jnp.dot(li_ref[...], y_ref[...], preferred_element_type=jnp.float32)
     for s, peer, source in col_peers(n):
         share(s, peer, me).wait_send()
         share(s, source, source).wait_recv()
@@ -96,7 +98,7 @@
         copy.wait()
 
 
-def scatter(x, r, lv, staged):
+def scatter(x, r, lv, staged, li, y):
     n = r.shape[0]
     return pl.pallas_call(
         functools.partial(scatter_kernel, n),
@@ -105,11 +107,14 @@
             jax.ShapeDtypeStruct(r.shape[1:], r.dtype),
             jax.ShapeDtypeStruct((lv.shape[0] - 1,) + lv.shape[1:], lv.dtype),
             jax.ShapeDtypeStruct((2,) + lv.shape[1:], lv.dtype),
+            jax.ShapeDtypeStruct((li.shape[0], y.shape[1]), jnp.float32),
         ),
         in_specs=[
             pl.BlockSpec(memory_space=pl.ANY),
             pl.BlockSpec(memory_space=pltpu.VMEM),
             pl.BlockSpec(memory_space=pl.ANY),
+            pl.BlockSpec(memory_space=pltpu.VMEM),
+            pl.BlockSpec(memory_space=pltpu.VMEM),
             pl.BlockSpec(memory_space=pltpu.VMEM),
         ],
         out_specs=(
@@ -117,6 +122,7 @@
             pl.BlockSpec(memory_space=pltpu.VMEM),
             pl.BlockSpec(memory_space=pl.ANY),
             pl.BlockSpec(memory_space=pl.ANY),
+            pl.BlockSpec(memory_space=pltpu.VMEM),
         ),
         scratch_shapes=[
             pltpu.VMEM(r.shape, r.dtype),
@@ -127,7 +133,7 @@
         compiler_params=pltpu.CompilerParams(
             collective_id=0, has_side_effects=True, vmem_limit_bytes=4 * 1024 * 1024
         ),
-    )(x, r, lv, staged)
+    )(x, r, lv, staged, li, y)
 
 
 def gather_kernel(
@@ -286,7 +292,6 @@
     level_coeffs = jnp.einsum(
         "lw,blr->bwr", lowered, row_project, preferred_element_type=jnp.float32
     )
-    dense_part = jnp.dot(leaf_inverse, lowered, preferred_element_type=jnp.float32)
     coeffs = lax.dot_general(
         lowered, compress, contract_first, preferred_element_type=jnp.float32
     ).astype(jnp.bfloat16)
@@ -299,8 +304,8 @@
         "kd,wkx->wdx", chosen, pieces, preferred_element_type=jnp.float32
     ).astype(jnp.bfloat16)
     root_shares = root_term.reshape(col_count, -1, root_term.shape[1])
-    arrived, root_share, pair, far = scatter(
-        outgoing.reshape(columns, -1), root_shares, level_coeffs, expand
+    arrived, root_share, pair, far, dense_part = scatter(
+        outgoing.reshape(columns, -1), root_shares, level_coeffs, expand, leaf_inverse, lowered
     )
     pair_sum = (level_coeffs[1] + pair[1]).astype(jnp.bfloat16)
     far_sum = far[0] + far[1]

time: 51.5 us -> 50.2 us (0.975)
  matrix products: 9.67 us -> 8.61 us
    dot_general x1, matrix products: 1.83 us -> 0.43 us  [per_device(): jnp.einsum('lw,blr->bwr', lowered, row_project, preferred_element_type=jn...]
    dot_general x1, matrix products: 0.26 us -> 1.31 us  [per_device(): lax.dot_general(lowered, root_project, contract_first, preferred_element_...]
    dot_general x1 -> x0, matrix products: 0.7 us -> none  [per_device(): jnp.dot(leaf_inverse, lowered, preferred_element_type=jnp.float32)]
where the time goes in v13:
time: 50.2 us; the launch traced here: 50 us
  Pallas kernels  39.3 us (78%)
  matrix products  8.61 us (17%)
  other arithmetic  1.25 us (2%)
  local copies, waits for them, and re-layouts  0.74 us (1%)
    pallas_call x1, Pallas kernels, gather(): pl.pallas_call(functools.partial(gather_kernel, n, m), out_shape=(jax.Sha...  22.5 us
    pallas_call x1, Pallas kernels, scatter(): pl.pallas_call(functools.partial(scatter_kernel, n), out_shape=(jax.Shape...  16.8 us
    dot_general x1, matrix products, per_device(): lax.dot_general(lowered, compress, contract_first, preferred_element_type...  3.08 us
    dot_general x1, matrix products, per_device(): lax.dot_general(lowered, root_project, contract_first, preferred_element_...  1.31 us
    dot_general x1, matrix products, per_device(): cluster_part = jnp.dot(expand, ordered, preferred_element_type=jnp.float32)  1.26 us
    convert_element_type x1, other arithmetic, per_device(): lowered = right_side.astype(jnp.bfloat16)  1.19 us
    dot_general x1, matrix products, per_device(): lax.dot_general(root_expand, root_coeffs, (((1,), (1,)), ((), ())), prefe...  1.1 us

profile of v13, /device:TPU:1, one launch (start us, length us, event | category | flops | bytes accessed | tf_op | source)
XLA Modules:
  0.0 50.0 jit_solution(10183293995833607224)
XLA Ops:
  0.0 0.0 copy-start
  0.0 1.2 %convert_element_type.23.y_ref = bf16[1024,128]{1,0:T(8,128)(2,1)S(1)} convert(f32[1024,128]{1,0:T(8,128)} %param.10) | non-fusion elementwise | flops 131072 | bytes 786432 | tf_op jit(solution)/shard_map/convert_element_type | solution.py:287
  1.2 1.3 %convolution_bitcast_fusion.4.r_ref = f32[16,8,256]{2,1,0:T(8,128)S(1)} fusion(bf16[1024,128]{1,0:T(8,128)(2,1)S(1)} %convert_element_type.23.y_ref, bf16[1024,256]{1,0:T(8,128)(2,1)} %param.17), kind=kOutput, calls=%fused_computation.11 | convolution fusion | flops 67108864 | bytes 917504 | tf_op jit(solution)/shard_map/dot_general | solution.py:289
  2.5 0.0 copy-done
  2.5 0.0 copy-start.5
  2.5 0.4 convolution_bitcast_fusion.3.lv_ref
  3.0 0.0 copy-start.1
  3.0 0.0 copy-start.4
  3.0 3.1 %fusion = bf16[16,8,16,128]{3,1,2,0:T(8,128)(2,1)S(1)} fusion(bf16[1024,128]{1,0:T(8,128)(2,1)S(1)} %convert_element_type.23.y_ref, bf16[1024,2048]{1,0:T(8,128)(2,1)} %param.12), kind=kOutput, calls=%fused_computation.3 | convolution fusion | flops 537133056 | bytes 4980736 | tf_op jit(solution)/shard_map/dot_general | solution.py:295
  6.1 0.1 copy.34
  6.2 0.0 copy-done.5
  6.2 0.4 convolution_convert_fusion.2
  6.6 0.1 copy.39
  6.8 0.0 copy-done.1
  6.8 0.3 copy-done.4
  7.1 0.0 copy-start.2
  7.1 0.0 copy-start.3
  7.1 16.8 %shard_map.100 = (bf16[128,2048]{1,0:T(8,128)(2,1)S(1)}, f32[8,256]{1,0:T(8,128)S(1)}, f32[2,128,256]{2,1,0:T(8,128)S(1)}, f32[2,128,256]{2,1,0:T(8,128)S(1)}, f32[1024,128]{1,0:T(8,128)S(1)}) custom-call(bf16[128,2048]{1,0:T(8,128)(2,1)S(1)} %bitcast.55, f32[16,8,256]{2,1,0:T(8,128)S(1)} %convolution_bitcast_fusion.4.r_ref, ...), custom_call_target="tpu_custom_call" | custom-call | tf_op jit(solution)/shard_map/pallas_call | solution.py:103
  24.0 0.0 copy-done.2
  24.0 0.0 copy-done.3
  24.0 22.5 %shard_map.101 = (bf16[16,128,128]{2,1,0:T(8,128)(2,1)S(1)}, bf16[16,8,256]{2,1,0:T(8,128)(2,1)S(1)}, bf16[128,256]{1,0:T(8,128)(2,1)S(1)}, f32[128,256]{1,0:T(8,128)S(1)}) custom-call(bf16[128,2048]{1,0:T(8,128)(2,1)S(1)} %get-tuple-element.15.a_ref, bf16[2048,2048]{1,0:T(8,128)(2,1)} %w_ref.1, f32[8,256]{1,0:T(8,128)S(1)} %get-tuple-element.16.share_ref, ...), custom_call_target="tpu_custom_call" | custom-call | tf_op jit(solution)/shard_map/pallas_call | solution.py:237
  46.5 0.4 convolution_convert_fusion.1
  46.9 0.1 copy.22
  47.1 0.6 %convolution_bitcast_fusion.1 = f32[1024,128]{1,0:T(8,128)S(1)} fusion(bf16[3,1024,256]{2,1,0:T(8,128)(2,1)S(1)} %copy-done.2, bf16[1,128,256]{2,1,0:T(8,128)(2,1)S(1)} %fusion.12, bf16[1,128,256]{2,1,0:T(8,128)(2,1)S(1)} %bitcast.56, bf16[1,128,256]{2,1,0:T(8,128)(2,1)S(1)} %slice.34), kind=kOutput, calls=%fused_computation.5 | convolution fusion | flops 201523200 | bytes 2293760 | tf_op jit(solution)/shard_map/blr,bwr->lw/dot_general | solution.py:325
  47.7 1.3 %fusion.3 = f32[1024,128]{1,0:T(8,128)S(1)} fusion(f32[1024,128]{1,0:T(8,128)S(1)} %convolution_bitcast_fusion.1, f32[1024,128]{1,0:T(8,128)S(1)} %get-tuple-element.14, bf16[1024,2048]{1,0:T(8,128)(2,1)S(1)} %copy-done.1, bf16[2048,128]{1,0:T(8,128)(2,1)S(1)} %bitcast.59), kind=kOutput, calls=%fused_computation.9 | convolution fusion | flops 537133056 | bytes 6291456 | tf_op jit(solution)/shard_map/dot_general | solution.py:319
  48.9 1.1 %fusion.1 = f32[1024,128]{1,0:T(8,128)} fusion(f32[1024,128]{1,0:T(8,128)S(1)} %fusion.3, bf16[1024,256]{1,0:T(8,128)(2,1)S(1)} %copy-done.3, bf16[16,8,256]{2,1,0:T(8,128)(2,1)S(1)} %get-tuple-element.22), kind=kOutput, calls=%fused_computation.6 | convolution fusion | flops 67239936 | bytes 1638400 | tf_op jit(solution)/shard_map/dot_general | solution.py:331
  (3 shorter events, 0.1 us)
Async XLA Ops:
  0.0 2.5 %copy-start = (bf16[3,1024,256]{2,1,0:T(8,128)(2,1)S(1)}, bf16[3,1024,256]{2,1,0:T(8,128)(2,1)}, u32[]{:S(2)}) copy-start(bf16[3,1024,256]{2,1,0:T(8,128)(2,1)} %param.15) | copy-start | bytes 4718596
  2.5 3.7 %copy-start.5 = (s32[16]{0:T(128)S(1)}, s32[16]{0:T(128)}, u32[]{:S(2)}) copy-start(s32[16]{0:T(128)} %param.19) | copy-start | bytes 196
  3.0 3.8 %copy-start.1 = (bf16[1024,2048]{1,0:T(8,128)(2,1)S(1)}, bf16[1024,2048]{1,0:T(8,128)(2,1)}, u32[]{:S(2)}) copy-start(bf16[1024,2048]{1,0:T(8,128)(2,1)} %e0_ref.1) | copy-start | bytes 12582916
  3.0 4.1 %copy-start.4 = (bf16[1024,1024]{1,0:T(8,128)(2,1)S(1)}, bf16[1024,1024]{1,0:T(8,128)(2,1)}, u32[]{:S(2)}) copy-start(bf16[1024,1024]{1,0:T(8,128)(2,1)} %li_ref.1) | copy-start | bytes 6291460
  7.1 16.9 %copy-start.2 = (bf16[3,1024,256]{2,1,0:T(8,128)(2,1)S(1)}, bf16[3,1024,256]{2,1,0:T(8,128)(2,1)}, u32[]{:S(2)}) copy-start(bf16[3,1024,256]{2,1,0:T(8,128)(2,1)} %e2_ref.1) | copy-start | bytes 4718596
  7.1 16.9 %copy-start.3 = (bf16[1024,256]{1,0:T(8,128)(2,1)S(1)}, bf16[1024,256]{1,0:T(8,128)(2,1)}, u32[]{:S(2)}) copy-start(bf16[1024,256]{1,0:T(8,128)(2,1)} %e3_ref.1) | copy-start | bytes 1572868

commit v14 on v13

--- a/solution.py
+++ b/solution.py
@@ -137,7 +137,8 @@
 
 
 def gather_kernel(
-    n, m, a_ref, w_ref, share_ref, c1_ref, p_ref, e2_ref, e3_ref, o_ref, full_ref, got1, got2,
+    n, m, a_ref, w_ref, share_ref, c1_ref, p_ref, s0_ref, e2_ref, e3_ref, o_ref, full_ref, got1, got2,
+    cpl_ref,
     mixed, rows_got, total, rounded, sems, row_sems, local_sems, sib_sems,
 ):
     me = lax.axis_index("col")
@@ -220,6 +221,12 @@
     local = pltpu.make_async_copy(mixed.at[me], o_ref.at[me], local_sems.at[0])
     local.start()
 
+    sibs[0].wait()
+    cpl_ref[...] = lax.dot_general(
+        e2_ref[0], s0_ref[...], (((1,), (1,)), ((), ())), preferred_element_type=jnp.float32
+    ) + lax.dot_general(
+        e2_ref[1], got1[...], (((1,), (1,)), ((), ())), preferred_element_type=jnp.float32
+    )
     for s, peer, source in col_peers(n):
         spread(s, peer, me).wait_send()
         spread(s, source, source).wait_recv()
@@ -227,11 +234,10 @@
         piece(s, source, source).wait_recv()
     mine.wait()
     local.wait()
-    for sib in sibs:
-        sib.wait()
-
-
-def gather(a, w, share, c1, p, staged, n, m):
+    sibs[1].wait()
+
+
+def gather(a, w, share, c1, p, s0, staged, n, m):
     piece_rows = w.shape[0] // n
     columns = a.shape[0]
     return pl.pallas_call(
@@ -241,20 +247,23 @@
             jax.ShapeDtypeStruct((n,) + share.shape, jnp.bfloat16),
             jax.ShapeDtypeStruct(c1.shape, c1.dtype),
             jax.ShapeDtypeStruct(p.shape, p.dtype),
+            jax.ShapeDtypeStruct((staged[0].shape[1], a.shape[0]), jnp.float32),
         ),
         in_specs=[
             pl.BlockSpec(memory_space=pltpu.VMEM),
             pl.BlockSpec(memory_space=pltpu.VMEM),
             pl.BlockSpec(memory_space=pltpu.VMEM),
-            pl.BlockSpec(memory_space=pl.ANY),
-            pl.BlockSpec(memory_space=pl.ANY),
+            pl.BlockSpec(memory_space=pltpu.VMEM),
+            pl.BlockSpec(memory_space=pl.ANY),
+            pl.BlockSpec(memory_space=pltpu.VMEM),
         ]
         + [pl.BlockSpec(memory_space=pltpu.VMEM)] * len(staged),
         out_specs=(
             pl.BlockSpec(memory_space=pl.ANY),
             pl.BlockSpec(memory_space=pltpu.VMEM),
-            pl.BlockSpec(memory_space=pl.ANY),
-            pl.BlockSpec(memory_space=pl.ANY),
+            pl.BlockSpec(memory_space=pltpu.VMEM),
+            pl.BlockSpec(memory_space=pl.ANY),
+            pl.BlockSpec(memory_space=pltpu.VMEM),
         ),
         scratch_shapes=[
             pltpu.VMEM((n, piece_rows, columns), a.dtype),
@@ -269,7 +278,7 @@
         compiler_params=pltpu.CompilerParams(
             collective_id=1, has_side_effects=True, vmem_limit_bytes=48 * 1024 * 1024
         ),
-    )(a, w, share, c1, p, *staged)
+    )(a, w, share, c1, p, s0, *staged)
 
 
 def per_device(
@@ -309,8 +318,9 @@
     )
     pair_sum = (level_coeffs[1] + pair[1]).astype(jnp.bfloat16)
     far_sum = far[0] + far[1]
-    returned, root_full, quad_one, quad_two = gather(
-        arrived, middle, root_share, pair_sum, far_sum, (row_expand, root_expand), col_count,
+    returned, root_full, quad_one, quad_two, near_coupled = gather(
+        arrived, middle, root_share, pair_sum, far_sum, pair[0].astype(jnp.bfloat16),
+        (row_expand, root_expand), col_count,
         lax.axis_size("row"),
     )
     ordered = jnp.einsum(
@@ -318,14 +328,11 @@
     ).astype(jnp.bfloat16).reshape(-1, columns)
     cluster_part = jnp.dot(expand, ordered, preferred_element_type=jnp.float32)
 
-    sibling_sum = jnp.stack(
-        [pair[0], quad_one.astype(jnp.float32), far_sum + quad_two], axis=0
-    )
     root_coeffs = root_full.reshape(columns, -1)
-    coupled = jnp.einsum(
-        "blr,bwr->lw",
-        row_expand,
-        sibling_sum.astype(jnp.bfloat16),
+    coupled = near_coupled + lax.dot_general(
+        row_expand[2],
+        (far_sum + quad_two).astype(jnp.bfloat16),
+        (((1,), (1,)), ((), ())),
         preferred_element_type=jnp.float32,
     )
     root_part = lax.dot_general(

time: 50.2 us -> 50.5 us (level)
  Pallas kernels: 39.3 us -> 39.9 us
    dot_general x1, matrix products: 1.1 us -> 0.29 us  [per_device(): lax.dot_general(root_expand, root_coeffs, (((1,), (1,)), ((), ())), prefe...]
    pallas_call x1, Pallas kernels: 22.5 us -> 23.1 us  [gather(): pl.pallas_call(functools.partial(gather_kernel, n, m), out_shape=(jax.Sha...]
    dot_general x1, matrix products: 0.58 us -> 1.11 us  [per_device(): lax.dot_general(row_expand[2], (far_sum + quad_two).astype(jnp.bfloat16),...]
where the time goes in v14:
time: 50.5 us; the launch traced here: 50.4 us
  Pallas kernels  39.9 us (79%)
  matrix products  8.32 us (16%)
  other arithmetic  1.23 us (2%)
  local copies, waits for them, and re-layouts  0.74 us (1%)
    pallas_call x1, Pallas kernels, gather(): pl.pallas_call(functools.partial(gather_kernel, n, m), out_shape=(jax.Sha...  23.1 us
    pallas_call x1, Pallas kernels, scatter(): pl.pallas_call(functools.partial(scatter_kernel, n), out_shape=(jax.Shape...  16.8 us
    dot_general x1, matrix products, per_device(): lax.dot_general(lowered, compress, contract_first, preferred_element_type...  3.08 us
    dot_general x1, matrix products, per_device(): lax.dot_general(lowered, root_project, contract_first, preferred_element_...  1.31 us
    dot_general x1, matrix products, per_device(): cluster_part = jnp.dot(expand, ordered, preferred_element_type=jnp.float32)  1.26 us
    convert_element_type x1, other arithmetic, per_device(): lowered = right_side.astype(jnp.bfloat16)  1.19 us
    dot_general x1, matrix products, per_device(): lax.dot_general(row_expand[2], (far_sum + quad_two).astype(jnp.bfloat16),...  1.11 us

profile of v14, /device:TPU:1, one launch (start us, length us, event | category | flops | bytes accessed | tf_op | source)
XLA Modules:
  0.0 50.4 jit_solution(6706325209384719751)
XLA Ops:
  0.0 0.0 copy-start
  0.0 1.2 %convert_element_type.27.y_ref = bf16[1024,128]{1,0:T(8,128)(2,1)S(1)} convert(f32[1024,128]{1,0:T(8,128)} %param.10) | non-fusion elementwise | flops 131072 | bytes 786432 | tf_op jit(solution)/shard_map/convert_element_type | solution.py:296
  1.2 1.3 %convolution_bitcast_fusion.4.r_ref = f32[16,8,256]{2,1,0:T(8,128)S(1)} fusion(bf16[1024,128]{1,0:T(8,128)(2,1)S(1)} %convert_element_type.27.y_ref, bf16[1024,256]{1,0:T(8,128)(2,1)} %param.17), kind=kOutput, calls=%fused_computation.12 | convolution fusion | flops 67108864 | bytes 917504 | tf_op jit(solution)/shard_map/dot_general | solution.py:298
  2.5 0.0 copy-done
  2.5 0.0 copy-start.5
  2.5 0.4 convolution_bitcast_fusion.3.lv_ref
  3.0 0.0 copy-start.1
  3.0 0.0 copy-start.4
  3.0 3.1 %fusion = bf16[16,8,16,128]{3,1,2,0:T(8,128)(2,1)S(1)} fusion(bf16[1024,128]{1,0:T(8,128)(2,1)S(1)} %convert_element_type.27.y_ref, bf16[1024,2048]{1,0:T(8,128)(2,1)} %param.12), kind=kOutput, calls=%fused_computation.3 | convolution fusion | flops 537133056 | bytes 4980736 | tf_op jit(solution)/shard_map/dot_general | solution.py:304
  6.1 0.1 copy.33
  6.2 0.0 copy-done.5
  6.2 0.4 convolution_convert_fusion.2
  6.6 0.1 copy.38
  6.8 0.0 copy-done.1
  6.8 0.3 copy-done.4
  7.1 0.0 copy-start.2
  7.1 0.0 copy-start.3
  7.1 16.8 %shard_map.100 = (bf16[128,2048]{1,0:T(8,128)(2,1)S(1)}, f32[8,256]{1,0:T(8,128)S(1)}, f32[2,128,256]{2,1,0:T(8,128)S(1)}, f32[2,128,256]{2,1,0:T(8,128)S(1)}, f32[1024,128]{1,0:T(8,128)S(1)}) custom-call(bf16[128,2048]{1,0:T(8,128)(2,1)S(1)} %bitcast.56, f32[16,8,256]{2,1,0:T(8,128)S(1)} %convolution_bitcast_fusion.4.r_ref, ...), custom_call_target="tpu_custom_call" | custom-call | tf_op jit(solution)/shard_map/pallas_call | solution.py:103
  24.0 0.0 copy-done.2
  24.0 0.0 copy-done.3
  24.0 23.1 %shard_map.101 = (bf16[16,128,128]{2,1,0:T(8,128)(2,1)S(1)}, bf16[16,8,256]{2,1,0:T(8,128)(2,1)S(1)}, bf16[128,256]{1,0:T(8,128)(2,1)}, f32[128,256]{1,0:T(8,128)S(1)}, f32[1024,128]{1,0:T(8,128)S(1)}) custom-call(bf16[128,2048]{1,0:T(8,128)(2,1)S(1)} %get-tuple-element.15.a_ref, bf16[2048,2048]{1,0:T(8,128)(2,1)} %w_ref.1, ...), custom_call_target="tpu_custom_call" | custom-call | tf_op jit(solution)/shard_map/pallas_call | solution.py:243
  47.1 0.4 convolution_convert_fusion.1
  47.5 0.1 copy.22
  47.7 1.3 %fusion.4 = f32[1024,128]{1,0:T(8,128)S(1)} fusion(f32[1024,128]{1,0:T(8,128)S(1)} %get-tuple-element.14, bf16[1024,2048]{1,0:T(8,128)(2,1)S(1)} %copy-done.1, bf16[2048,128]{1,0:T(8,128)(2,1)S(1)} %bitcast.57), kind=kOutput, calls=%fused_computation.10 | convolution fusion | flops 537001984 | bytes 5767168 | tf_op jit(solution)/shard_map/dot_general | solution.py:329
  49.0 0.3 convolution_bitcast_fusion
  49.2 1.1 %fusion.3 = f32[1024,128]{1,0:T(8,128)} fusion(f32[1024,128]{1,0:T(8,128)S(1)} %convolution_bitcast_fusion, f32[1024,128]{1,0:T(8,128)S(1)} %fusion.4, f32[1024,128]{1,0:T(8,128)S(1)} %get-tuple-element.20, bf16[3,1024,256]{2,1,0:T(8,128)(2,1)S(1)} %copy-done.2, f32[128,256]{1,0:T(8,128)S(1)} %get-tuple-element.23.p_ref, f32[128,256]{1,0:T(8,128)S(1)} %get-tuple-element.21), kind=kOutput, calls=%fused_computation.8 | convolution fusion | flops 67567616 | bytes 2883584 | tf_op jit(solution)/shard_map/dot_general | solution.py:332
  (2 shorter events, 0.0 us)
Async XLA Ops:
  0.0 2.5 %copy-start = (bf16[3,1024,256]{2,1,0:T(8,128)(2,1)S(1)}, bf16[3,1024,256]{2,1,0:T(8,128)(2,1)}, u32[]{:S(2)}) copy-start(bf16[3,1024,256]{2,1,0:T(8,128)(2,1)} %param.15) | copy-start | bytes 4718596
  2.5 3.7 %copy-start.5 = (s32[16]{0:T(128)S(1)}, s32[16]{0:T(128)}, u32[]{:S(2)}) copy-start(s32[16]{0:T(128)} %param.19) | copy-start | bytes 196
  3.0 3.8 %copy-start.1 = (bf16[1024,2048]{1,0:T(8,128)(2,1)S(1)}, bf16[1024,2048]{1,0:T(8,128)(2,1)}, u32[]{:S(2)}) copy-start(bf16[1024,2048]{1,0:T(8,128)(2,1)} %e0_ref.1) | copy-start | bytes 12582916
  3.0 4.1 %copy-start.4 = (bf16[1024,1024]{1,0:T(8,128)(2,1)S(1)}, bf16[1024,1024]{1,0:T(8,128)(2,1)}, u32[]{:S(2)}) copy-start(bf16[1024,1024]{1,0:T(8,128)(2,1)} %li_ref.1) | copy-start | bytes 6291460
  7.1 16.9 %copy-start.2 = (bf16[3,1024,256]{2,1,0:T(8,128)(2,1)S(1)}, bf16[3,1024,256]{2,1,0:T(8,128)(2,1)}, u32[]{:S(2)}) copy-start(bf16[3,1024,256]{2,1,0:T(8,128)(2,1)} %e2_ref.1) | copy-start | bytes 4718596
  7.1 16.9 %copy-start.3 = (bf16[1024,256]{1,0:T(8,128)(2,1)S(1)}, bf16[1024,256]{1,0:T(8,128)(2,1)}, u32[]{:S(2)}) copy-start(bf16[1024,256]{1,0:T(8,128)(2,1)} %e3_ref.1) | copy-start | bytes 1572868

commit v15 on v13

--- a/solution.py
+++ b/solution.py
@@ -194,7 +194,7 @@
         piece(s, peer, me).start()
         return carry
 
-    half = n // 2
+    half = n // 4
     lax.fori_loop(1, half, compute_and_send, 0)
 
     def spread(s, peer, slot):

time: 50.2 us -> 52.2 us (1.040)
  Pallas kernels: 39.3 us -> 41.3 us
    pallas_call x1, Pallas kernels: 22.5 us -> 24.5 us  [gather(): pl.pallas_call(functools.partial(gather_kernel, n, m), out_shape=(jax.Sha...]
where the time goes in v15:
time: 52.2 us; the launch traced here: 52.1 us
  Pallas kernels  41.3 us (79%)
  matrix products  8.61 us (16%)
  other arithmetic  1.25 us (2%)
  local copies, waits for them, and re-layouts  0.74 us (1%)
    pallas_call x1, Pallas kernels, gather(): pl.pallas_call(functools.partial(gather_kernel, n, m), out_shape=(jax.Sha...  24.5 us
    pallas_call x1, Pallas kernels, scatter(): pl.pallas_call(functools.partial(scatter_kernel, n), out_shape=(jax.Shape...  16.8 us
    dot_general x1, matrix products, per_device(): lax.dot_general(lowered, compress, contract_first, preferred_element_type...  3.08 us
    dot_general x1, matrix products, per_device(): lax.dot_general(lowered, root_project, contract_first, preferred_element_...  1.31 us
    dot_general x1, matrix products, per_device(): cluster_part = jnp.dot(expand, ordered, preferred_element_type=jnp.float32)  1.27 us
    convert_element_type x1, other arithmetic, per_device(): lowered = right_side.astype(jnp.bfloat16)  1.19 us
    dot_general x1, matrix products, per_device(): lax.dot_general(root_expand, root_coeffs, (((1,), (1,)), ((), ())), prefe...  1.1 us

profile of v15, /device:TPU:1, one launch (start us, length us, event | category | flops | bytes accessed | tf_op | source)
XLA Modules:
  0.0 52.1 jit_solution(11797724388507451983)
XLA Ops:
  0.0 0.0 copy-start
  0.0 1.2 %convert_element_type.23.y_ref = bf16[1024,128]{1,0:T(8,128)(2,1)S(1)} convert(f32[1024,128]{1,0:T(8,128)} %param.10) | non-fusion elementwise | flops 131072 | bytes 786432 | tf_op jit(solution)/shard_map/convert_element_type | solution.py:287
  1.2 1.3 %convolution_bitcast_fusion.4.r_ref = f32[16,8,256]{2,1,0:T(8,128)S(1)} fusion(bf16[1024,128]{1,0:T(8,128)(2,1)S(1)} %convert_element_type.23.y_ref, bf16[1024,256]{1,0:T(8,128)(2,1)} %param.17), kind=kOutput, calls=%fused_computation.11 | convolution fusion | flops 67108864 | bytes 917504 | tf_op jit(solution)/shard_map/dot_general | solution.py:289
  2.5 0.0 copy-done
  2.5 0.0 copy-start.5
  2.5 0.4 convolution_bitcast_fusion.3.lv_ref
  3.0 0.0 copy-start.1
  3.0 0.0 copy-start.4
  3.0 3.1 %fusion = bf16[16,8,16,128]{3,1,2,0:T(8,128)(2,1)S(1)} fusion(bf16[1024,128]{1,0:T(8,128)(2,1)S(1)} %convert_element_type.23.y_ref, bf16[1024,2048]{1,0:T(8,128)(2,1)} %param.12), kind=kOutput, calls=%fused_computation.3 | convolution fusion | flops 537133056 | bytes 4980736 | tf_op jit(solution)/shard_map/dot_general | solution.py:295
  6.1 0.1 copy.34
  6.2 0.0 copy-done.5
  6.2 0.4 convolution_convert_fusion.2
  6.6 0.1 copy.39
  6.8 0.0 copy-done.1
  6.8 0.3 copy-done.4
  7.1 0.0 copy-start.2
  7.1 0.0 copy-start.3
  7.1 16.8 %shard_map.100 = (bf16[128,2048]{1,0:T(8,128)(2,1)S(1)}, f32[8,256]{1,0:T(8,128)S(1)}, f32[2,128,256]{2,1,0:T(8,128)S(1)}, f32[2,128,256]{2,1,0:T(8,128)S(1)}, f32[1024,128]{1,0:T(8,128)S(1)}) custom-call(bf16[128,2048]{1,0:T(8,128)(2,1)S(1)} %bitcast.55, f32[16,8,256]{2,1,0:T(8,128)S(1)} %convolution_bitcast_fusion.4.r_ref, ...), custom_call_target="tpu_custom_call" | custom-call | tf_op jit(solution)/shard_map/pallas_call | solution.py:103
  24.0 0.0 copy-done.2
  24.0 0.0 copy-done.3
  24.0 24.5 %shard_map.101 = (bf16[16,128,128]{2,1,0:T(8,128)(2,1)S(1)}, bf16[16,8,256]{2,1,0:T(8,128)(2,1)S(1)}, bf16[128,256]{1,0:T(8,128)(2,1)S(1)}, f32[128,256]{1,0:T(8,128)S(1)}) custom-call(bf16[128,2048]{1,0:T(8,128)(2,1)S(1)} %get-tuple-element.15.a_ref, bf16[2048,2048]{1,0:T(8,128)(2,1)} %w_ref.1, f32[8,256]{1,0:T(8,128)S(1)} %get-tuple-element.16.share_ref, ...), custom_call_target="tpu_custom_call" | custom-call | tf_op jit(solution)/shard_map/pallas_call | solution.py:237
  48.5 0.4 convolution_convert_fusion.1
  49.0 0.1 copy.22
  49.1 0.6 %convolution_bitcast_fusion.1 = f32[1024,128]{1,0:T(8,128)S(1)} fusion(bf16[3,1024,256]{2,1,0:T(8,128)(2,1)S(1)} %copy-done.2, bf16[1,128,256]{2,1,0:T(8,128)(2,1)S(1)} %fusion.12, bf16[1,128,256]{2,1,0:T(8,128)(2,1)S(1)} %bitcast.56, bf16[1,128,256]{2,1,0:T(8,128)(2,1)S(1)} %slice.34), kind=kOutput, calls=%fused_computation.5 | convolution fusion | flops 201523200 | bytes 2293760 | tf_op jit(solution)/shard_map/blr,bwr->lw/dot_general | solution.py:325
  49.7 1.3 %fusion.3 = f32[1024,128]{1,0:T(8,128)S(1)} fusion(f32[1024,128]{1,0:T(8,128)S(1)} %convolution_bitcast_fusion.1, f32[1024,128]{1,0:T(8,128)S(1)} %get-tuple-element.14, bf16[1024,2048]{1,0:T(8,128)(2,1)S(1)} %copy-done.1, bf16[2048,128]{1,0:T(8,128)(2,1)S(1)} %bitcast.59), kind=kOutput, calls=%fused_computation.9 | convolution fusion | flops 537133056 | bytes 6291456 | tf_op jit(solution)/shard_map/dot_general | solution.py:319
  51.0 1.1 %fusion.1 = f32[1024,128]{1,0:T(8,128)} fusion(f32[1024,128]{1,0:T(8,128)S(1)} %fusion.3, bf16[1024,256]{1,0:T(8,128)(2,1)S(1)} %copy-done.3, bf16[16,8,256]{2,1,0:T(8,128)(2,1)S(1)} %get-tuple-element.22), kind=kOutput, calls=%fused_computation.6 | convolution fusion | flops 67239936 | bytes 1638400 | tf_op jit(solution)/shard_map/dot_general | solution.py:331
  (3 shorter events, 0.1 us)
Async XLA Ops:
  0.0 2.5 %copy-start = (bf16[3,1024,256]{2,1,0:T(8,128)(2,1)S(1)}, bf16[3,1024,256]{2,1,0:T(8,128)(2,1)}, u32[]{:S(2)}) copy-start(bf16[3,1024,256]{2,1,0:T(8,128)(2,1)} %param.15) | copy-start | bytes 4718596
  2.5 3.7 %copy-start.5 = (s32[16]{0:T(128)S(1)}, s32[16]{0:T(128)}, u32[]{:S(2)}) copy-start(s32[16]{0:T(128)} %param.19) | copy-start | bytes 196
  3.0 3.8 %copy-start.1 = (bf16[1024,2048]{1,0:T(8,128)(2,1)S(1)}, bf16[1024,2048]{1,0:T(8,128)(2,1)}, u32[]{:S(2)}) copy-start(bf16[1024,2048]{1,0:T(8,128)(2,1)} %e0_ref.1) | copy-start | bytes 12582916
  3.0 4.1 %copy-start.4 = (bf16[1024,1024]{1,0:T(8,128)(2,1)S(1)}, bf16[1024,1024]{1,0:T(8,128)(2,1)}, u32[]{:S(2)}) copy-start(bf16[1024,1024]{1,0:T(8,128)(2,1)} %li_ref.1) | copy-start | bytes 6291460
  7.1 16.9 %copy-start.2 = (bf16[3,1024,256]{2,1,0:T(8,128)(2,1)S(1)}, bf16[3,1024,256]{2,1,0:T(8,128)(2,1)}, u32[]{:S(2)}) copy-start(bf16[3,1024,256]{2,1,0:T(8,128)(2,1)} %e2_ref.1) | copy-start | bytes 4718596
  7.1 16.9 %copy-start.3 = (bf16[1024,256]{1,0:T(8,128)(2,1)S(1)}, bf16[1024,256]{1,0:T(8,128)(2,1)}, u32[]{:S(2)}) copy-start(bf16[1024,256]{1,0:T(8,128)(2,1)} %e3_ref.1) | copy-start | bytes 1572868

commit v16 on v15

--- a/solution.py
+++ b/solution.py
@@ -194,7 +194,7 @@
         piece(s, peer, me).start()
         return carry
 
-    half = n // 4
+    half = n - n // 4
     lax.fori_loop(1, half, compute_and_send, 0)
 
     def spread(s, peer, slot):

time: 52.2 us -> 48.7 us (0.933)
  Pallas kernels: 41.3 us -> 37.8 us
    pallas_call x1, Pallas kernels: 24.5 us -> 20.9 us  [gather(): pl.pallas_call(functools.partial(gather_kernel, n, m), out_shape=(jax.Sha...]
where the time goes in v16:
time: 48.7 us; the launch traced here: 48.5 us
  Pallas kernels  37.8 us (78%)
  matrix products  8.61 us (18%)
  other arithmetic  1.25 us (3%)
  local copies, waits for them, and re-layouts  0.74 us (2%)
    pallas_call x1, Pallas kernels, gather(): pl.pallas_call(functools.partial(gather_kernel, n, m), out_shape=(jax.Sha...  20.9 us
    pallas_call x1, Pallas kernels, scatter(): pl.pallas_call(functools.partial(scatter_kernel, n), out_shape=(jax.Shape...  16.8 us
    dot_general x1, matrix products, per_device(): lax.dot_general(lowered, compress, contract_first, preferred_element_type...  3.08 us
    dot_general x1, matrix products, per_device(): lax.dot_general(lowered, root_project, contract_first, preferred_element_...  1.31 us
    dot_general x1, matrix products, per_device(): cluster_part = jnp.dot(expand, ordered, preferred_element_type=jnp.float32)  1.26 us
    convert_element_type x1, other arithmetic, per_device(): lowered = right_side.astype(jnp.bfloat16)  1.19 us
    dot_general x1, matrix products, per_device(): lax.dot_general(root_expand, root_coeffs, (((1,), (1,)), ((), ())), prefe...  1.1 us

profile of v16, /device:TPU:1, one launch (start us, length us, event | category | flops | bytes accessed | tf_op | source)
XLA Modules:
  0.0 48.5 jit_solution(10244611682725784878)
XLA Ops:
  0.0 0.0 copy-start
  0.0 1.2 %convert_element_type.23.y_ref = bf16[1024,128]{1,0:T(8,128)(2,1)S(1)} convert(f32[1024,128]{1,0:T(8,128)} %param.10) | non-fusion elementwise | flops 131072 | bytes 786432 | tf_op jit(solution)/shard_map/convert_element_type | solution.py:287
  1.2 1.3 %convolution_bitcast_fusion.4.r_ref = f32[16,8,256]{2,1,0:T(8,128)S(1)} fusion(bf16[1024,128]{1,0:T(8,128)(2,1)S(1)} %convert_element_type.23.y_ref, bf16[1024,256]{1,0:T(8,128)(2,1)} %param.17), kind=kOutput, calls=%fused_computation.11 | convolution fusion | flops 67108864 | bytes 917504 | tf_op jit(solution)/shard_map/dot_general | solution.py:289
  2.5 0.0 copy-done
  2.5 0.0 copy-start.5
  2.5 0.4 convolution_bitcast_fusion.3.lv_ref
  3.0 0.0 copy-start.1
  3.0 0.0 copy-start.4
  3.0 3.1 %fusion = bf16[16,8,16,128]{3,1,2,0:T(8,128)(2,1)S(1)} fusion(bf16[1024,128]{1,0:T(8,128)(2,1)S(1)} %convert_element_type.23.y_ref, bf16[1024,2048]{1,0:T(8,128)(2,1)} %param.12), kind=kOutput, calls=%fused_computation.3 | convolution fusion | flops 537133056 | bytes 4980736 | tf_op jit(solution)/shard_map/dot_general | solution.py:295
  6.1 0.1 copy.34
  6.2 0.0 copy-done.5
  6.2 0.4 convolution_convert_fusion.2
  6.6 0.1 copy.39
  6.8 0.0 copy-done.1
  6.8 0.3 copy-done.4
  7.1 0.0 copy-start.2
  7.1 0.0 copy-start.3
  7.1 16.8 %shard_map.100 = (bf16[128,2048]{1,0:T(8,128)(2,1)S(1)}, f32[8,256]{1,0:T(8,128)S(1)}, f32[2,128,256]{2,1,0:T(8,128)S(1)}, f32[2,128,256]{2,1,0:T(8,128)S(1)}, f32[1024,128]{1,0:T(8,128)S(1)}) custom-call(bf16[128,2048]{1,0:T(8,128)(2,1)S(1)} %bitcast.55, f32[16,8,256]{2,1,0:T(8,128)S(1)} %convolution_bitcast_fusion.4.r_ref, ...), custom_call_target="tpu_custom_call" | custom-call | tf_op jit(solution)/shard_map/pallas_call | solution.py:103
  24.0 0.0 copy-done.2
  24.0 0.0 copy-done.3
  24.0 20.9 %shard_map.101 = (bf16[16,128,128]{2,1,0:T(8,128)(2,1)S(1)}, bf16[16,8,256]{2,1,0:T(8,128)(2,1)S(1)}, bf16[128,256]{1,0:T(8,128)(2,1)S(1)}, f32[128,256]{1,0:T(8,128)S(1)}) custom-call(bf16[128,2048]{1,0:T(8,128)(2,1)S(1)} %get-tuple-element.15.a_ref, bf16[2048,2048]{1,0:T(8,128)(2,1)} %w_ref.1, f32[8,256]{1,0:T(8,128)S(1)} %get-tuple-element.16.share_ref, ...), custom_call_target="tpu_custom_call" | custom-call | tf_op jit(solution)/shard_map/pallas_call | solution.py:237
  45.0 0.4 convolution_convert_fusion.1
  45.4 0.1 copy.22
  45.6 0.6 %convolution_bitcast_fusion.1 = f32[1024,128]{1,0:T(8,128)S(1)} fusion(bf16[3,1024,256]{2,1,0:T(8,128)(2,1)S(1)} %copy-done.2, bf16[1,128,256]{2,1,0:T(8,128)(2,1)S(1)} %fusion.12, bf16[1,128,256]{2,1,0:T(8,128)(2,1)S(1)} %bitcast.56, bf16[1,128,256]{2,1,0:T(8,128)(2,1)S(1)} %slice.34), kind=kOutput, calls=%fused_computation.5 | convolution fusion | flops 201523200 | bytes 2293760 | tf_op jit(solution)/shard_map/blr,bwr->lw/dot_general | solution.py:325
  46.2 1.3 %fusion.3 = f32[1024,128]{1,0:T(8,128)S(1)} fusion(f32[1024,128]{1,0:T(8,128)S(1)} %convolution_bitcast_fusion.1, f32[1024,128]{1,0:T(8,128)S(1)} %get-tuple-element.14, bf16[1024,2048]{1,0:T(8,128)(2,1)S(1)} %copy-done.1, bf16[2048,128]{1,0:T(8,128)(2,1)S(1)} %bitcast.59), kind=kOutput, calls=%fused_computation.9 | convolution fusion | flops 537133056 | bytes 6291456 | tf_op jit(solution)/shard_map/dot_general | solution.py:319
  47.4 1.1 %fusion.1 = f32[1024,128]{1,0:T(8,128)} fusion(f32[1024,128]{1,0:T(8,128)S(1)} %fusion.3, bf16[1024,256]{1,0:T(8,128)(2,1)S(1)} %copy-done.3, bf16[16,8,256]{2,1,0:T(8,128)(2,1)S(1)} %get-tuple-element.22), kind=kOutput, calls=%fused_computation.6 | convolution fusion | flops 67239936 | bytes 1638400 | tf_op jit(solution)/shard_map/dot_general | solution.py:331
  (3 shorter events, 0.1 us)
Async XLA Ops:
  0.0 2.5 %copy-start = (bf16[3,1024,256]{2,1,0:T(8,128)(2,1)S(1)}, bf16[3,1024,256]{2,1,0:T(8,128)(2,1)}, u32[]{:S(2)}) copy-start(bf16[3,1024,256]{2,1,0:T(8,128)(2,1)} %param.15) | copy-start | bytes 4718596
  2.5 3.7 %copy-start.5 = (s32[16]{0:T(128)S(1)}, s32[16]{0:T(128)}, u32[]{:S(2)}) copy-start(s32[16]{0:T(128)} %param.19) | copy-start | bytes 196
  3.0 3.8 %copy-start.1 = (bf16[1024,2048]{1,0:T(8,128)(2,1)S(1)}, bf16[1024,2048]{1,0:T(8,128)(2,1)}, u32[]{:S(2)}) copy-start(bf16[1024,2048]{1,0:T(8,128)(2,1)} %e0_ref.1) | copy-start | bytes 12582916
  3.0 4.1 %copy-start.4 = (bf16[1024,1024]{1,0:T(8,128)(2,1)S(1)}, bf16[1024,1024]{1,0:T(8,128)(2,1)}, u32[]{:S(2)}) copy-start(bf16[1024,1024]{1,0:T(8,128)(2,1)} %li_ref.1) | copy-start | bytes 6291460
  7.1 16.9 %copy-start.2 = (bf16[3,1024,256]{2,1,0:T(8,128)(2,1)S(1)}, bf16[3,1024,256]{2,1,0:T(8,128)(2,1)}, u32[]{:S(2)}) copy-start(bf16[3,1024,256]{2,1,0:T(8,128)(2,1)} %e2_ref.1) | copy-start | bytes 4718596
  7.1 16.9 %copy-start.3 = (bf16[1024,256]{1,0:T(8,128)(2,1)S(1)}, bf16[1024,256]{1,0:T(8,128)(2,1)}, u32[]{:S(2)}) copy-start(bf16[1024,256]{1,0:T(8,128)(2,1)} %e3_ref.1) | copy-start | bytes 1572868

commit v17 on v16

--- a/solution.py
+++ b/solution.py
@@ -194,7 +194,7 @@
         piece(s, peer, me).start()
         return carry
 
-    half = n - n // 4
+    half = n
     lax.fori_loop(1, half, compute_and_send, 0)
 
     def spread(s, peer, slot):

time: 48.7 us -> 47.9 us (0.984)
  Pallas kernels: 37.8 us -> 37 us
    pallas_call x1, Pallas kernels: 20.9 us -> 20.1 us  [gather(): pl.pallas_call(functools.partial(gather_kernel, n, m), out_shape=(jax.Sha...]
where the time goes in v17:
time: 47.9 us; the launch traced here: 47.7 us
  Pallas kernels  37 us (77%)
  matrix products  8.61 us (18%)
  other arithmetic  1.25 us (3%)
  local copies, waits for them, and re-layouts  0.74 us (2%)
    pallas_call x1, Pallas kernels, gather(): pl.pallas_call(functools.partial(gather_kernel, n, m), out_shape=(jax.Sha...  20.1 us
    pallas_call x1, Pallas kernels, scatter(): pl.pallas_call(functools.partial(scatter_kernel, n), out_shape=(jax.Shape...  16.8 us
    dot_general x1, matrix products, per_device(): lax.dot_general(lowered, compress, contract_first, preferred_element_type...  3.08 us
    dot_general x1, matrix products, per_device(): lax.dot_general(lowered, root_project, contract_first, preferred_element_...  1.31 us
    dot_general x1, matrix products, per_device(): cluster_part = jnp.dot(expand, ordered, preferred_element_type=jnp.float32)  1.26 us
    convert_element_type x1, other arithmetic, per_device(): lowered = right_side.astype(jnp.bfloat16)  1.19 us
    dot_general x1, matrix products, per_device(): lax.dot_general(root_expand, root_coeffs, (((1,), (1,)), ((), ())), prefe...  1.1 us

profile of v17, /device:TPU:1, one launch (start us, length us, event | category | flops | bytes accessed | tf_op | source)
XLA Modules:
  0.0 47.7 jit_solution(46304343279539158)
XLA Ops:
  0.0 0.0 copy-start
  0.0 1.2 %convert_element_type.23.y_ref = bf16[1024,128]{1,0:T(8,128)(2,1)S(1)} convert(f32[1024,128]{1,0:T(8,128)} %param.10) | non-fusion elementwise | flops 131072 | bytes 786432 | tf_op jit(solution)/shard_map/convert_element_type | solution.py:287
  1.2 1.3 %convolution_bitcast_fusion.4.r_ref = f32[16,8,256]{2,1,0:T(8,128)S(1)} fusion(bf16[1024,128]{1,0:T(8,128)(2,1)S(1)} %convert_element_type.23.y_ref, bf16[1024,256]{1,0:T(8,128)(2,1)} %param.17), kind=kOutput, calls=%fused_computation.11 | convolution fusion | flops 67108864 | bytes 917504 | tf_op jit(solution)/shard_map/dot_general | solution.py:289
  2.5 0.0 copy-done
  2.5 0.0 copy-start.5
  2.5 0.4 convolution_bitcast_fusion.3.lv_ref
  3.0 0.0 copy-start.1
  3.0 0.0 copy-start.4
  3.0 3.1 %fusion = bf16[16,8,16,128]{3,1,2,0:T(8,128)(2,1)S(1)} fusion(bf16[1024,128]{1,0:T(8,128)(2,1)S(1)} %convert_element_type.23.y_ref, bf16[1024,2048]{1,0:T(8,128)(2,1)} %param.12), kind=kOutput, calls=%fused_computation.3 | convolution fusion | flops 537133056 | bytes 4980736 | tf_op jit(solution)/shard_map/dot_general | solution.py:295
  6.1 0.1 copy.34
  6.2 0.0 copy-done.5
  6.2 0.4 convolution_convert_fusion.2
  6.6 0.1 copy.39
  6.8 0.0 copy-done.1
  6.8 0.3 copy-done.4
  7.1 0.0 copy-start.2
  7.1 0.0 copy-start.3
  7.1 16.8 %shard_map.100 = (bf16[128,2048]{1,0:T(8,128)(2,1)S(1)}, f32[8,256]{1,0:T(8,128)S(1)}, f32[2,128,256]{2,1,0:T(8,128)S(1)}, f32[2,128,256]{2,1,0:T(8,128)S(1)}, f32[1024,128]{1,0:T(8,128)S(1)}) custom-call(bf16[128,2048]{1,0:T(8,128)(2,1)S(1)} %bitcast.55, f32[16,8,256]{2,1,0:T(8,128)S(1)} %convolution_bitcast_fusion.4.r_ref, ...), custom_call_target="tpu_custom_call" | custom-call | tf_op jit(solution)/shard_map/pallas_call | solution.py:103
  24.0 0.0 copy-done.2
  24.0 0.0 copy-done.3
  24.0 20.1 %shard_map.101 = (bf16[16,128,128]{2,1,0:T(8,128)(2,1)S(1)}, bf16[16,8,256]{2,1,0:T(8,128)(2,1)S(1)}, bf16[128,256]{1,0:T(8,128)(2,1)S(1)}, f32[128,256]{1,0:T(8,128)S(1)}) custom-call(bf16[128,2048]{1,0:T(8,128)(2,1)S(1)} %get-tuple-element.15.a_ref, bf16[2048,2048]{1,0:T(8,128)(2,1)} %w_ref.1, f32[8,256]{1,0:T(8,128)S(1)} %get-tuple-element.16.share_ref, ...), custom_call_target="tpu_custom_call" | custom-call | tf_op jit(solution)/shard_map/pallas_call | solution.py:237
  44.2 0.4 convolution_convert_fusion.1
  44.6 0.1 copy.22
  44.8 0.6 %convolution_bitcast_fusion.1 = f32[1024,128]{1,0:T(8,128)S(1)} fusion(bf16[3,1024,256]{2,1,0:T(8,128)(2,1)S(1)} %copy-done.2, bf16[1,128,256]{2,1,0:T(8,128)(2,1)S(1)} %fusion.12, bf16[1,128,256]{2,1,0:T(8,128)(2,1)S(1)} %bitcast.56, bf16[1,128,256]{2,1,0:T(8,128)(2,1)S(1)} %slice.34), kind=kOutput, calls=%fused_computation.5 | convolution fusion | flops 201523200 | bytes 2293760 | tf_op jit(solution)/shard_map/blr,bwr->lw/dot_general | solution.py:325
  45.4 1.3 %fusion.3 = f32[1024,128]{1,0:T(8,128)S(1)} fusion(f32[1024,128]{1,0:T(8,128)S(1)} %convolution_bitcast_fusion.1, f32[1024,128]{1,0:T(8,128)S(1)} %get-tuple-element.14, bf16[1024,2048]{1,0:T(8,128)(2,1)S(1)} %copy-done.1, bf16[2048,128]{1,0:T(8,128)(2,1)S(1)} %bitcast.59), kind=kOutput, calls=%fused_computation.9 | convolution fusion | flops 537133056 | bytes 6291456 | tf_op jit(solution)/shard_map/dot_general | solution.py:319
  46.6 1.1 %fusion.1 = f32[1024,128]{1,0:T(8,128)} fusion(f32[1024,128]{1,0:T(8,128)S(1)} %fusion.3, bf16[1024,256]{1,0:T(8,128)(2,1)S(1)} %copy-done.3, bf16[16,8,256]{2,1,0:T(8,128)(2,1)S(1)} %get-tuple-element.22), kind=kOutput, calls=%fused_computation.6 | convolution fusion | flops 67239936 | bytes 1638400 | tf_op jit(solution)/shard_map/dot_general | solution.py:331
  (3 shorter events, 0.1 us)
Async XLA Ops:
  0.0 2.5 %copy-start = (bf16[3,1024,256]{2,1,0:T(8,128)(2,1)S(1)}, bf16[3,1024,256]{2,1,0:T(8,128)(2,1)}, u32[]{:S(2)}) copy-start(bf16[3,1024,256]{2,1,0:T(8,128)(2,1)} %param.15) | copy-start | bytes 4718596
  2.5 3.7 %copy-start.5 = (s32[16]{0:T(128)S(1)}, s32[16]{0:T(128)}, u32[]{:S(2)}) copy-start(s32[16]{0:T(128)} %param.19) | copy-start | bytes 196
  3.0 3.8 %copy-start.1 = (bf16[1024,2048]{1,0:T(8,128)(2,1)S(1)}, bf16[1024,2048]{1,0:T(8,128)(2,1)}, u32[]{:S(2)}) copy-start(bf16[1024,2048]{1,0:T(8,128)(2,1)} %e0_ref.1) | copy-start | bytes 12582916
  3.0 4.1 %copy-start.4 = (bf16[1024,1024]{1,0:T(8,128)(2,1)S(1)}, bf16[1024,1024]{1,0:T(8,128)(2,1)}, u32[]{:S(2)}) copy-start(bf16[1024,1024]{1,0:T(8,128)(2,1)} %li_ref.1) | copy-start | bytes 6291460
  7.1 16.9 %copy-start.2 = (bf16[3,1024,256]{2,1,0:T(8,128)(2,1)S(1)}, bf16[3,1024,256]{2,1,0:T(8,128)(2,1)}, u32[]{:S(2)}) copy-start(bf16[3,1024,256]{2,1,0:T(8,128)(2,1)} %e2_ref.1) | copy-start | bytes 4718596
  7.1 16.9 %copy-start.3 = (bf16[1024,256]{1,0:T(8,128)(2,1)S(1)}, bf16[1024,256]{1,0:T(8,128)(2,1)}, u32[]{:S(2)}) copy-start(bf16[1024,256]{1,0:T(8,128)(2,1)} %e3_ref.1) | copy-start | bytes 1572868

commit v18 on v17

--- a/solution.py
+++ b/solution.py
@@ -194,8 +194,10 @@
         piece(s, peer, me).start()
         return carry
 
-    half = n
-    lax.fori_loop(1, half, compute_and_send, 0)
+    lax.fori_loop(1, n, compute_and_send, 0)
+    compute(me)
+    local = pltpu.make_async_copy(mixed.at[me], o_ref.at[me], local_sems.at[0])
+    local.start()
 
     def spread(s, peer, slot):
         return pltpu.make_async_remote_copy(
@@ -215,10 +217,6 @@
     for s, peer, _ in col_peers(n):
         spread(s, peer, me).start()
 
-    lax.fori_loop(half, n, compute_and_send, 0)
-    compute(me)
-    local = pltpu.make_async_copy(mixed.at[me], o_ref.at[me], local_sems.at[0])
-    local.start()
 
     for s, peer, source in col_peers(n):
         spread(s, peer, me).wait_send()

time: 47.9 us -> 47.9 us (level)
  no operation moved by 1% of the time
where the time goes in v18:
time: 47.9 us; the launch traced here: 47.7 us
  Pallas kernels  37 us (77%)
  matrix products  8.61 us (18%)
  other arithmetic  1.25 us (3%)
  local copies, waits for them, and re-layouts  0.74 us (2%)
    pallas_call x1, Pallas kernels, gather(): pl.pallas_call(functools.partial(gather_kernel, n, m), out_shape=(jax.Sha...  20.1 us
    pallas_call x1, Pallas kernels, scatter(): pl.pallas_call(functools.partial(scatter_kernel, n), out_shape=(jax.Shape...  16.8 us
    dot_general x1, matrix products, per_device(): lax.dot_general(lowered, compress, contract_first, preferred_element_type...  3.08 us
    dot_general x1, matrix products, per_device(): lax.dot_general(lowered, root_project, contract_first, preferred_element_...  1.31 us
    dot_general x1, matrix products, per_device(): cluster_part = jnp.dot(expand, ordered, preferred_element_type=jnp.float32)  1.26 us
    convert_element_type x1, other arithmetic, per_device(): lowered = right_side.astype(jnp.bfloat16)  1.19 us
    dot_general x1, matrix products, per_device(): lax.dot_general(root_expand, root_coeffs, (((1,), (1,)), ((), ())), prefe...  1.1 us

profile of v18, /device:TPU:1, one launch (start us, length us, event | category | flops | bytes accessed | tf_op | source)
XLA Modules:
  0.0 47.7 jit_solution(11486357252131821231)
XLA Ops:
  0.0 0.0 copy-start
  0.0 1.2 %convert_element_type.23.y_ref = bf16[1024,128]{1,0:T(8,128)(2,1)S(1)} convert(f32[1024,128]{1,0:T(8,128)} %param.10) | non-fusion elementwise | flops 131072 | bytes 786432 | tf_op jit(solution)/shard_map/convert_element_type | solution.py:285
  1.2 1.3 %convolution_bitcast_fusion.4.r_ref = f32[16,8,256]{2,1,0:T(8,128)S(1)} fusion(bf16[1024,128]{1,0:T(8,128)(2,1)S(1)} %convert_element_type.23.y_ref, bf16[1024,256]{1,0:T(8,128)(2,1)} %param.17), kind=kOutput, calls=%fused_computation.11 | convolution fusion | flops 67108864 | bytes 917504 | tf_op jit(solution)/shard_map/dot_general | solution.py:287
  2.5 0.0 copy-done
  2.5 0.0 copy-start.5
  2.5 0.4 convolution_bitcast_fusion.3.lv_ref
  3.0 0.0 copy-start.1
  3.0 0.0 copy-start.4
  3.0 3.1 %fusion = bf16[16,8,16,128]{3,1,2,0:T(8,128)(2,1)S(1)} fusion(bf16[1024,128]{1,0:T(8,128)(2,1)S(1)} %convert_element_type.23.y_ref, bf16[1024,2048]{1,0:T(8,128)(2,1)} %param.12), kind=kOutput, calls=%fused_computation.3 | convolution fusion | flops 537133056 | bytes 4980736 | tf_op jit(solution)/shard_map/dot_general | solution.py:293
  6.1 0.1 copy.34
  6.2 0.0 copy-done.5
  6.2 0.4 convolution_convert_fusion.2
  6.6 0.1 copy.39
  6.8 0.0 copy-done.1
  6.8 0.3 copy-done.4
  7.1 0.0 copy-start.2
  7.1 0.0 copy-start.3
  7.1 16.8 %shard_map.100 = (bf16[128,2048]{1,0:T(8,128)(2,1)S(1)}, f32[8,256]{1,0:T(8,128)S(1)}, f32[2,128,256]{2,1,0:T(8,128)S(1)}, f32[2,128,256]{2,1,0:T(8,128)S(1)}, f32[1024,128]{1,0:T(8,128)S(1)}) custom-call(bf16[128,2048]{1,0:T(8,128)(2,1)S(1)} %bitcast.55, f32[16,8,256]{2,1,0:T(8,128)S(1)} %convolution_bitcast_fusion.4.r_ref, ...), custom_call_target="tpu_custom_call" | custom-call | tf_op jit(solution)/shard_map/pallas_call | solution.py:103
  24.0 0.0 copy-done.2
  24.0 0.0 copy-done.3
  24.0 20.1 %shard_map.101 = (bf16[16,128,128]{2,1,0:T(8,128)(2,1)S(1)}, bf16[16,8,256]{2,1,0:T(8,128)(2,1)S(1)}, bf16[128,256]{1,0:T(8,128)(2,1)S(1)}, f32[128,256]{1,0:T(8,128)S(1)}) custom-call(bf16[128,2048]{1,0:T(8,128)(2,1)S(1)} %get-tuple-element.15.a_ref, bf16[2048,2048]{1,0:T(8,128)(2,1)} %w_ref.1, f32[8,256]{1,0:T(8,128)S(1)} %get-tuple-element.16.share_ref, ...), custom_call_target="tpu_custom_call" | custom-call | tf_op jit(solution)/shard_map/pallas_call | solution.py:235
  44.2 0.4 convolution_convert_fusion.1
  44.6 0.1 copy.22
  44.8 0.6 %convolution_bitcast_fusion.1 = f32[1024,128]{1,0:T(8,128)S(1)} fusion(bf16[3,1024,256]{2,1,0:T(8,128)(2,1)S(1)} %copy-done.2, bf16[1,128,256]{2,1,0:T(8,128)(2,1)S(1)} %fusion.12, bf16[1,128,256]{2,1,0:T(8,128)(2,1)S(1)} %bitcast.56, bf16[1,128,256]{2,1,0:T(8,128)(2,1)S(1)} %slice.34), kind=kOutput, calls=%fused_computation.5 | convolution fusion | flops 201523200 | bytes 2293760 | tf_op jit(solution)/shard_map/blr,bwr->lw/dot_general | solution.py:323
  45.4 1.3 %fusion.3 = f32[1024,128]{1,0:T(8,128)S(1)} fusion(f32[1024,128]{1,0:T(8,128)S(1)} %convolution_bitcast_fusion.1, f32[1024,128]{1,0:T(8,128)S(1)} %get-tuple-element.14, bf16[1024,2048]{1,0:T(8,128)(2,1)S(1)} %copy-done.1, bf16[2048,128]{1,0:T(8,128)(2,1)S(1)} %bitcast.59), kind=kOutput, calls=%fused_computation.9 | convolution fusion | flops 537133056 | bytes 6291456 | tf_op jit(solution)/shard_map/dot_general | solution.py:317
  46.6 1.1 %fusion.1 = f32[1024,128]{1,0:T(8,128)} fusion(f32[1024,128]{1,0:T(8,128)S(1)} %fusion.3, bf16[1024,256]{1,0:T(8,128)(2,1)S(1)} %copy-done.3, bf16[16,8,256]{2,1,0:T(8,128)(2,1)S(1)} %get-tuple-element.22), kind=kOutput, calls=%fused_computation.6 | convolution fusion | flops 67239936 | bytes 1638400 | tf_op jit(solution)/shard_map/dot_general | solution.py:329
  (3 shorter events, 0.1 us)
Async XLA Ops:
  0.0 2.5 %copy-start = (bf16[3,1024,256]{2,1,0:T(8,128)(2,1)S(1)}, bf16[3,1024,256]{2,1,0:T(8,128)(2,1)}, u32[]{:S(2)}) copy-start(bf16[3,1024,256]{2,1,0:T(8,128)(2,1)} %param.15) | copy-start | bytes 4718596
  2.5 3.7 %copy-start.5 = (s32[16]{0:T(128)S(1)}, s32[16]{0:T(128)}, u32[]{:S(2)}) copy-start(s32[16]{0:T(128)} %param.19) | copy-start | bytes 196
  3.0 3.8 %copy-start.1 = (bf16[1024,2048]{1,0:T(8,128)(2,1)S(1)}, bf16[1024,2048]{1,0:T(8,128)(2,1)}, u32[]{:S(2)}) copy-start(bf16[1024,2048]{1,0:T(8,128)(2,1)} %e0_ref.1) | copy-start | bytes 12582916
  3.0 4.1 %copy-start.4 = (bf16[1024,1024]{1,0:T(8,128)(2,1)S(1)}, bf16[1024,1024]{1,0:T(8,128)(2,1)}, u32[]{:S(2)}) copy-start(bf16[1024,1024]{1,0:T(8,128)(2,1)} %li_ref.1) | copy-start | bytes 6291460
  7.1 16.9 %copy-start.2 = (bf16[3,1024,256]{2,1,0:T(8,128)(2,1)S(1)}, bf16[3,1024,256]{2,1,0:T(8,128)(2,1)}, u32[]{:S(2)}) copy-start(bf16[3,1024,256]{2,1,0:T(8,128)(2,1)} %e2_ref.1) | copy-start | bytes 4718596
  7.1 16.9 %copy-start.3 = (bf16[1024,256]{1,0:T(8,128)(2,1)S(1)}, bf16[1024,256]{1,0:T(8,128)(2,1)}, u32[]{:S(2)}) copy-start(bf16[1024,256]{1,0:T(8,128)(2,1)} %e3_ref.1) | copy-start | bytes 1572868

commit v19 on v17

--- a/solution.py
+++ b/solution.py
@@ -82,8 +82,9 @@
         )
 
     for s, peer, _ in col_peers(n):
+        piece(s, peer, me).start()
+    for s, peer, _ in col_peers(n):
         share(s, peer, me).start()
-        piece(s, peer, me).start()
     d_ref[...] = jnp.dot(li_ref[...], y_ref[...], preferred_element_type=jnp.float32)
     for s, peer, source in col_peers(n):
         share(s, peer, me).wait_send()

time: 47.9 us -> 48.3 us (level)
  no operation moved by 1% of the time
where the time goes in v19:
time: 48.3 us; the launch traced here: 48.1 us
  Pallas kernels  37.3 us (77%)
  matrix products  8.61 us (18%)
  other arithmetic  1.25 us (3%)
  local copies, waits for them, and re-layouts  0.74 us (2%)
    pallas_call x1, Pallas kernels, gather(): pl.pallas_call(functools.partial(gather_kernel, n, m), out_shape=(jax.Sha...  20 us
    pallas_call x1, Pallas kernels, scatter(): pl.pallas_call(functools.partial(scatter_kernel, n), out_shape=(jax.Shape...  17.3 us
    dot_general x1, matrix products, per_device(): lax.dot_general(lowered, compress, contract_first, preferred_element_type...  3.08 us
    dot_general x1, matrix products, per_device(): lax.dot_general(lowered, root_project, contract_first, preferred_element_...  1.31 us
    dot_general x1, matrix products, per_device(): cluster_part = jnp.dot(expand, ordered, preferred_element_type=jnp.float32)  1.27 us
    convert_element_type x1, other arithmetic, per_device(): lowered = right_side.astype(jnp.bfloat16)  1.19 us
    dot_general x1, matrix products, per_device(): lax.dot_general(root_expand, root_coeffs, (((1,), (1,)), ((), ())), prefe...  1.1 us

profile of v19, /device:TPU:1, one launch (start us, length us, event | category | flops | bytes accessed | tf_op | source)
XLA Modules:
  0.0 48.1 jit_solution(13899741811314770817)
XLA Ops:
  0.0 0.0 copy-start
  0.0 1.2 %convert_element_type.23.y_ref = bf16[1024,128]{1,0:T(8,128)(2,1)S(1)} convert(f32[1024,128]{1,0:T(8,128)} %param.10) | non-fusion elementwise | flops 131072 | bytes 786432 | tf_op jit(solution)/shard_map/convert_element_type | solution.py:288
  1.2 1.3 %convolution_bitcast_fusion.4.r_ref = f32[16,8,256]{2,1,0:T(8,128)S(1)} fusion(bf16[1024,128]{1,0:T(8,128)(2,1)S(1)} %convert_element_type.23.y_ref, bf16[1024,256]{1,0:T(8,128)(2,1)} %param.17), kind=kOutput, calls=%fused_computation.11 | convolution fusion | flops 67108864 | bytes 917504 | tf_op jit(solution)/shard_map/dot_general | solution.py:290
  2.5 0.0 copy-done
  2.5 0.0 copy-start.5
  2.5 0.4 convolution_bitcast_fusion.3.lv_ref
  3.0 0.0 copy-start.1
  3.0 0.0 copy-start.4
  3.0 3.1 %fusion = bf16[16,8,16,128]{3,1,2,0:T(8,128)(2,1)S(1)} fusion(bf16[1024,128]{1,0:T(8,128)(2,1)S(1)} %convert_element_type.23.y_ref, bf16[1024,2048]{1,0:T(8,128)(2,1)} %param.12), kind=kOutput, calls=%fused_computation.3 | convolution fusion | flops 537133056 | bytes 4980736 | tf_op jit(solution)/shard_map/dot_general | solution.py:296
  6.1 0.1 copy.34
  6.2 0.0 copy-done.5
  6.2 0.4 convolution_convert_fusion.2
  6.6 0.1 copy.39
  6.8 0.0 copy-done.1
  6.8 0.3 copy-done.4
  7.1 0.0 copy-start.2
  7.1 0.0 copy-start.3
  7.1 17.3 %shard_map.100 = (bf16[128,2048]{1,0:T(8,128)(2,1)S(1)}, f32[8,256]{1,0:T(8,128)S(1)}, f32[2,128,256]{2,1,0:T(8,128)S(1)}, f32[2,128,256]{2,1,0:T(8,128)S(1)}, f32[1024,128]{1,0:T(8,128)S(1)}) custom-call(bf16[128,2048]{1,0:T(8,128)(2,1)S(1)} %bitcast.55, f32[16,8,256]{2,1,0:T(8,128)S(1)} %convolution_bitcast_fusion.4.r_ref, ...), custom_call_target="tpu_custom_call" | custom-call | tf_op jit(solution)/shard_map/pallas_call | solution.py:104
  24.5 0.0 copy-done.2
  24.5 0.0 copy-done.3
  24.5 20.0 %shard_map.101 = (bf16[16,128,128]{2,1,0:T(8,128)(2,1)S(1)}, bf16[16,8,256]{2,1,0:T(8,128)(2,1)S(1)}, bf16[128,256]{1,0:T(8,128)(2,1)S(1)}, f32[128,256]{1,0:T(8,128)S(1)}) custom-call(bf16[128,2048]{1,0:T(8,128)(2,1)S(1)} %get-tuple-element.15.a_ref, bf16[2048,2048]{1,0:T(8,128)(2,1)} %w_ref.1, f32[8,256]{1,0:T(8,128)S(1)} %get-tuple-element.16.share_ref, ...), custom_call_target="tpu_custom_call" | custom-call | tf_op jit(solution)/shard_map/pallas_call | solution.py:238
  44.6 0.4 convolution_convert_fusion.1
  45.0 0.1 copy.22
  45.1 0.6 %convolution_bitcast_fusion.1 = f32[1024,128]{1,0:T(8,128)S(1)} fusion(bf16[3,1024,256]{2,1,0:T(8,128)(2,1)S(1)} %copy-done.2, bf16[1,128,256]{2,1,0:T(8,128)(2,1)S(1)} %fusion.12, bf16[1,128,256]{2,1,0:T(8,128)(2,1)S(1)} %bitcast.56, bf16[1,128,256]{2,1,0:T(8,128)(2,1)S(1)} %slice.34), kind=kOutput, calls=%fused_computation.5 | convolution fusion | flops 201523200 | bytes 2293760 | tf_op jit(solution)/shard_map/blr,bwr->lw/dot_general | solution.py:326
  45.7 1.3 %fusion.3 = f32[1024,128]{1,0:T(8,128)S(1)} fusion(f32[1024,128]{1,0:T(8,128)S(1)} %convolution_bitcast_fusion.1, f32[1024,128]{1,0:T(8,128)S(1)} %get-tuple-element.14, bf16[1024,2048]{1,0:T(8,128)(2,1)S(1)} %copy-done.1, bf16[2048,128]{1,0:T(8,128)(2,1)S(1)} %bitcast.59), kind=kOutput, calls=%fused_computation.9 | convolution fusion | flops 537133056 | bytes 6291456 | tf_op jit(solution)/shard_map/dot_general | solution.py:320
  47.0 1.1 %fusion.1 = f32[1024,128]{1,0:T(8,128)} fusion(f32[1024,128]{1,0:T(8,128)S(1)} %fusion.3, bf16[1024,256]{1,0:T(8,128)(2,1)S(1)} %copy-done.3, bf16[16,8,256]{2,1,0:T(8,128)(2,1)S(1)} %get-tuple-element.22), kind=kOutput, calls=%fused_computation.6 | convolution fusion | flops 67239936 | bytes 1638400 | tf_op jit(solution)/shard_map/dot_general | solution.py:332
  (3 shorter events, 0.1 us)
Async XLA Ops:
  0.0 2.5 %copy-start = (bf16[3,1024,256]{2,1,0:T(8,128)(2,1)S(1)}, bf16[3,1024,256]{2,1,0:T(8,128)(2,1)}, u32[]{:S(2)}) copy-start(bf16[3,1024,256]{2,1,0:T(8,128)(2,1)} %param.15) | copy-start | bytes 4718596
  2.5 3.7 %copy-start.5 = (s32[16]{0:T(128)S(1)}, s32[16]{0:T(128)}, u32[]{:S(2)}) copy-start(s32[16]{0:T(128)} %param.19) | copy-start | bytes 196
  3.0 3.8 %copy-start.1 = (bf16[1024,2048]{1,0:T(8,128)(2,1)S(1)}, bf16[1024,2048]{1,0:T(8,128)(2,1)}, u32[]{:S(2)}) copy-start(bf16[1024,2048]{1,0:T(8,128)(2,1)} %e0_ref.1) | copy-start | bytes 12582916
  3.0 4.1 %copy-start.4 = (bf16[1024,1024]{1,0:T(8,128)(2,1)S(1)}, bf16[1024,1024]{1,0:T(8,128)(2,1)}, u32[]{:S(2)}) copy-start(bf16[1024,1024]{1,0:T(8,128)(2,1)} %li_ref.1) | copy-start | bytes 6291460
  7.1 17.4 %copy-start.2 = (bf16[3,1024,256]{2,1,0:T(8,128)(2,1)S(1)}, bf16[3,1024,256]{2,1,0:T(8,128)(2,1)}, u32[]{:S(2)}) copy-start(bf16[3,1024,256]{2,1,0:T(8,128)(2,1)} %e2_ref.1) | copy-start | bytes 4718596
  7.1 17.4 %copy-start.3 = (bf16[1024,256]{1,0:T(8,128)(2,1)S(1)}, bf16[1024,256]{1,0:T(8,128)(2,1)}, u32[]{:S(2)}) copy-start(bf16[1024,256]{1,0:T(8,128)(2,1)} %e3_ref.1) | copy-start | bytes 1572868

commit v20 on v17

--- a/solution.py
+++ b/solution.py
@@ -267,7 +267,7 @@
             pltpu.SemaphoreType.DMA((2, 2)),
         ],
         compiler_params=pltpu.CompilerParams(
-            collective_id=1, has_side_effects=True, vmem_limit_bytes=48 * 1024 * 1024
+            collective_id=1, has_side_effects=True, vmem_limit_bytes=16 * 1024 * 1024
         ),
     )(a, w, share, c1, p, *staged)
 

time: 47.9 us -> 45.2 us (0.944)
  Pallas kernels: 37 us -> 33.7 us
  matrix products: 8.61 us -> 9.22 us
    pallas_call x1, Pallas kernels: 20.1 us -> 16.8 us  [gather(): pl.pallas_call(functools.partial(gather_kernel, n, m), out_shape=(jax.Sha...]
    dot_general x1, matrix products: 1.31 us -> 1.94 us  [per_device(): lax.dot_general(lowered, root_project, contract_first, preferred_element_...]
where the time goes in v20:
time: 45.2 us; the launch traced here: 45.1 us
  Pallas kernels  33.7 us (75%)
  matrix products  9.22 us (20%)
  other arithmetic  1.28 us (3%)
  local copies, waits for them, and re-layouts  0.74 us (2%)
    pallas_call x1, Pallas kernels, gather(): pl.pallas_call(functools.partial(gather_kernel, n, m), out_shape=(jax.Sha...  16.8 us
    pallas_call x1, Pallas kernels, scatter(): pl.pallas_call(functools.partial(scatter_kernel, n), out_shape=(jax.Shape...  16.8 us
    dot_general x1, matrix products, per_device(): lax.dot_general(lowered, compress, contract_first, preferred_element_type...  3.08 us
    dot_general x1, matrix products, per_device(): lax.dot_general(lowered, root_project, contract_first, preferred_element_...  1.94 us
    dot_general x1, matrix products, per_device(): cluster_part = jnp.dot(expand, ordered, preferred_element_type=jnp.float32)  1.26 us
    convert_element_type x1, other arithmetic, per_device(): lowered = right_side.astype(jnp.bfloat16)  1.22 us
    dot_general x1, matrix products, per_device(): lax.dot_general(root_expand, root_coeffs, (((1,), (1,)), ((), ())), prefe...  1.1 us

profile of v20, /device:TPU:1, one launch (start us, length us, event | category | flops | bytes accessed | tf_op | source)
XLA Modules:
  0.0 45.1 jit_solution(16775572015051901590)
XLA Ops:
  0.0 0.0 copy-start
  0.0 0.0 slice-start
  0.0 1.2 %convert_element_type.23.y_ref = bf16[1024,128]{1,0:T(8,128)(2,1)S(1)} convert(f32[1024,128]{1,0:T(8,128)} %param.10) | non-fusion elementwise | flops 131072 | bytes 786432 | tf_op jit(solution)/shard_map/convert_element_type | solution.py:287
  1.2 1.9 %convolution_bitcast_fusion.4.r_ref = f32[16,8,256]{2,1,0:T(8,128)S(1)} fusion(bf16[1024,128]{1,0:T(8,128)(2,1)S(1)} %convert_element_type.23.y_ref, bf16[1024,256]{1,0:T(8,128)(2,1)} %param.17), kind=kOutput, calls=%fused_computation.11 | convolution fusion | flops 67108864 | bytes 917504 | tf_op jit(solution)/shard_map/dot_general | solution.py:289
  3.2 0.0 copy-done
  3.2 0.0 copy-start.5
  3.2 0.4 convolution_bitcast_fusion.3.lv_ref
  3.6 0.0 copy-start.1
  3.6 0.0 copy-start.4
  3.7 3.1 %fusion = bf16[16,8,16,128]{3,1,2,0:T(8,128)(2,1)S(1)} fusion(bf16[1024,128]{1,0:T(8,128)(2,1)S(1)} %convert_element_type.23.y_ref, bf16[1024,2048]{1,0:T(8,128)(2,1)} %param.12), kind=kOutput, calls=%fused_computation.3 | convolution fusion | flops 537133056 | bytes 4980736 | tf_op jit(solution)/shard_map/dot_general | solution.py:295
  6.7 0.1 copy.34
  6.9 0.0 copy-done.5
  6.9 0.0 slice-start.1
  6.9 0.4 convolution_convert_fusion.2
  7.3 0.1 copy.39
  7.5 0.0 copy-done.1
  7.5 0.3 copy-done.4
  7.8 0.0 copy-start.2
  7.8 0.0 copy-start.3
  7.8 16.8 %shard_map.100 = (bf16[128,2048]{1,0:T(8,128)(2,1)S(1)}, f32[8,256]{1,0:T(8,128)S(1)}, f32[2,128,256]{2,1,0:T(8,128)S(1)}, f32[2,128,256]{2,1,0:T(8,128)S(1)}, f32[1024,128]{1,0:T(8,128)S(1)}) custom-call(bf16[128,2048]{1,0:T(8,128)(2,1)S(1)} %bitcast.57, f32[16,8,256]{2,1,0:T(8,128)S(1)} %convolution_bitcast_fusion.4.r_ref, ...), custom_call_target="tpu_custom_call" | custom-call | tf_op jit(solution)/shard_map/pallas_call | solution.py:103
  24.7 0.0 slice-done
  24.7 0.0 slice-done.1
  24.7 0.0 copy-done.2
  24.7 0.0 copy-done.3
  24.7 16.8 %shard_map.101 = (bf16[16,128,128]{2,1,0:T(8,128)(2,1)S(1)}, bf16[16,8,256]{2,1,0:T(8,128)(2,1)S(1)}, bf16[128,256]{1,0:T(8,128)(2,1)S(1)}, f32[128,256]{1,0:T(8,128)S(1)}) custom-call(bf16[128,2048]{1,0:T(8,128)(2,1)S(1)} %get-tuple-element.15.a_ref, bf16[2048,2048]{1,0:T(8,128)(2,1)S(1)} %bitcast.56, f32[8,256]{1,0:T(8,128)S(1)} %get-tuple-element.16.share_ref, ...), custom_call_target="tpu_custom_call" | custom-call | tf_op jit(solution)/shard_map/pallas_call | solution.py:237
  41.6 0.4 convolution_convert_fusion.1
  42.0 0.1 copy.22
  42.2 0.6 %convolution_bitcast_fusion.1 = f32[1024,128]{1,0:T(8,128)S(1)} fusion(bf16[3,1024,256]{2,1,0:T(8,128)(2,1)S(1)} %copy-done.2, bf16[1,128,256]{2,1,0:T(8,128)(2,1)S(1)} %fusion.12, bf16[1,128,256]{2,1,0:T(8,128)(2,1)S(1)} %bitcast.58, bf16[1,128,256]{2,1,0:T(8,128)(2,1)S(1)} %slice.34), kind=kOutput, calls=%fused_computation.5 | convolution fusion | flops 201523200 | bytes 2293760 | tf_op jit(solution)/shard_map/blr,bwr->lw/dot_general | solution.py:325
  42.7 1.3 %fusion.3 = f32[1024,128]{1,0:T(8,128)S(1)} fusion(f32[1024,128]{1,0:T(8,128)S(1)} %convolution_bitcast_fusion.1, f32[1024,128]{1,0:T(8,128)S(1)} %get-tuple-element.14, bf16[1024,2048]{1,0:T(8,128)(2,1)S(1)} %copy-done.1, bf16[2048,128]{1,0:T(8,128)(2,1)S(1)} %bitcast.61), kind=kOutput, calls=%fused_computation.9 | convolution fusion | flops 537133056 | bytes 6291456 | tf_op jit(solution)/shard_map/dot_general | solution.py:319
  44.0 1.1 %fusion.1 = f32[1024,128]{1,0:T(8,128)} fusion(f32[1024,128]{1,0:T(8,128)S(1)} %fusion.3, bf16[1024,256]{1,0:T(8,128)(2,1)S(1)} %copy-done.3, bf16[16,8,256]{2,1,0:T(8,128)(2,1)S(1)} %get-tuple-element.22), kind=kOutput, calls=%fused_computation.6 | convolution fusion | flops 67239936 | bytes 1638400 | tf_op jit(solution)/shard_map/dot_general | solution.py:331
  (4 shorter events, 0.1 us)
Async XLA Ops:
  0.0 3.2 %copy-start = (bf16[3,1024,256]{2,1,0:T(8,128)(2,1)S(1)}, bf16[3,1024,256]{2,1,0:T(8,128)(2,1)}, u32[]{:S(2)}) copy-start(bf16[3,1024,256]{2,1,0:T(8,128)(2,1)} %param.15) | copy-start | bytes 4718596
  0.0 24.7 %slice-start = ((s8[8388608]{0:T(1024)(128)(4,1)}), s8[4194304]{0:T(1024)(128)(4,1)S(1)}, s32[]{:S(2)}) async-start(s8[8388608]{0:T(1024)(128)(4,1)} %bitcast.55), calls=%async_computation | async-start | bytes 8388608
  3.2 3.7 %copy-start.5 = (s32[16]{0:T(128)S(1)}, s32[16]{0:T(128)}, u32[]{:S(2)}) copy-start(s32[16]{0:T(128)} %param.19) | copy-start | bytes 196
  3.6 3.8 %copy-start.1 = (bf16[1024,2048]{1,0:T(8,128)(2,1)S(1)}, bf16[1024,2048]{1,0:T(8,128)(2,1)}, u32[]{:S(2)}) copy-start(bf16[1024,2048]{1,0:T(8,128)(2,1)} %e0_ref.1) | copy-start | bytes 12582916
  3.6 4.1 %copy-start.4 = (bf16[1024,1024]{1,0:T(8,128)(2,1)S(1)}, bf16[1024,1024]{1,0:T(8,128)(2,1)}, u32[]{:S(2)}) copy-start(bf16[1024,1024]{1,0:T(8,128)(2,1)} %li_ref.1) | copy-start | bytes 6291460
  6.9 17.8 %slice-start.1 = ((s8[8388608]{0:T(1024)(128)(4,1)}), s8[4194304]{0:T(1024)(128)(4,1)S(1)}, s32[]{:S(2)}) async-start(s8[8388608]{0:T(1024)(128)(4,1)} %bitcast.55), calls=%async_computation.1 | async-start | bytes 8388608
  7.8 16.9 %copy-start.2 = (bf16[3,1024,256]{2,1,0:T(8,128)(2,1)S(1)}, bf16[3,1024,256]{2,1,0:T(8,128)(2,1)}, u32[]{:S(2)}) copy-start(bf16[3,1024,256]{2,1,0:T(8,128)(2,1)} %e2_ref.1) | copy-start | bytes 4718596
  7.8 16.9 %copy-start.3 = (bf16[1024,256]{1,0:T(8,128)(2,1)S(1)}, bf16[1024,256]{1,0:T(8,128)(2,1)}, u32[]{:S(2)}) copy-start(bf16[1024,256]{1,0:T(8,128)(2,1)} %e3_ref.1) | copy-start | bytes 1572868

commit v21 on v20

--- a/solution.py
+++ b/solution.py
@@ -267,7 +267,7 @@
             pltpu.SemaphoreType.DMA((2, 2)),
         ],
         compiler_params=pltpu.CompilerParams(
-            collective_id=1, has_side_effects=True, vmem_limit_bytes=16 * 1024 * 1024
+            collective_id=1, has_side_effects=True, vmem_limit_bytes=8 * 1024 * 1024
         ),
     )(a, w, share, c1, p, *staged)
 

time: 45.2 us -> 45.2 us (level)
  no operation moved by 1% of the time
where the time goes in v21:
time: 45.2 us; the launch traced here: 45.1 us
  Pallas kernels  33.7 us (75%)
  matrix products  9.23 us (20%)
  other arithmetic  1.27 us (3%)
  local copies, waits for them, and re-layouts  0.74 us (2%)
    pallas_call x1, Pallas kernels, gather(): pl.pallas_call(functools.partial(gather_kernel, n, m), out_shape=(jax.Sha...  16.8 us
    pallas_call x1, Pallas kernels, scatter(): pl.pallas_call(functools.partial(scatter_kernel, n), out_shape=(jax.Shape...  16.8 us
    dot_general x1, matrix products, per_device(): lax.dot_general(lowered, compress, contract_first, preferred_element_type...  3.08 us
    dot_general x1, matrix products, per_device(): lax.dot_general(lowered, root_project, contract_first, preferred_element_...  1.94 us
    dot_general x1, matrix products, per_device(): cluster_part = jnp.dot(expand, ordered, preferred_element_type=jnp.float32)  1.26 us
    convert_element_type x1, other arithmetic, per_device(): lowered = right_side.astype(jnp.bfloat16)  1.22 us
    dot_general x1, matrix products, per_device(): lax.dot_general(root_expand, root_coeffs, (((1,), (1,)), ((), ())), prefe...  1.1 us

profile of v21, /device:TPU:1, one launch (start us, length us, event | category | flops | bytes accessed | tf_op | source)
XLA Modules:
  0.0 45.1 jit_solution(17099207000705228757)
XLA Ops:
  0.0 0.0 copy-start
  0.0 0.0 slice-start
  0.0 1.2 %convert_element_type.23.y_ref = bf16[1024,128]{1,0:T(8,128)(2,1)S(1)} convert(f32[1024,128]{1,0:T(8,128)} %param.10) | non-fusion elementwise | flops 131072 | bytes 786432 | tf_op jit(solution)/shard_map/convert_element_type | solution.py:287
  1.2 1.9 %convolution_bitcast_fusion.4.r_ref = f32[16,8,256]{2,1,0:T(8,128)S(1)} fusion(bf16[1024,128]{1,0:T(8,128)(2,1)S(1)} %convert_element_type.23.y_ref, bf16[1024,256]{1,0:T(8,128)(2,1)} %param.17), kind=kOutput, calls=%fused_computation.11 | convolution fusion | flops 67108864 | bytes 917504 | tf_op jit(solution)/shard_map/dot_general | solution.py:289
  3.2 0.0 copy-done
  3.2 0.0 copy-start.5
  3.2 0.4 convolution_bitcast_fusion.3.lv_ref
  3.6 0.0 copy-start.1
  3.6 0.0 copy-start.4
  3.7 3.1 %fusion = bf16[16,8,16,128]{3,1,2,0:T(8,128)(2,1)S(1)} fusion(bf16[1024,128]{1,0:T(8,128)(2,1)S(1)} %convert_element_type.23.y_ref, bf16[1024,2048]{1,0:T(8,128)(2,1)} %param.12), kind=kOutput, calls=%fused_computation.3 | convolution fusion | flops 537133056 | bytes 4980736 | tf_op jit(solution)/shard_map/dot_general | solution.py:295
  6.7 0.1 copy.34
  6.9 0.0 copy-done.5
  6.9 0.0 slice-start.1
  6.9 0.4 convolution_convert_fusion.2
  7.3 0.1 copy.39
  7.5 0.0 copy-done.1
  7.5 0.3 copy-done.4
  7.8 0.0 copy-start.2
  7.8 0.0 copy-start.3
  7.8 16.8 %shard_map.100 = (bf16[128,2048]{1,0:T(8,128)(2,1)S(1)}, f32[8,256]{1,0:T(8,128)S(1)}, f32[2,128,256]{2,1,0:T(8,128)S(1)}, f32[2,128,256]{2,1,0:T(8,128)S(1)}, f32[1024,128]{1,0:T(8,128)S(1)}) custom-call(bf16[128,2048]{1,0:T(8,128)(2,1)S(1)} %bitcast.57, f32[16,8,256]{2,1,0:T(8,128)S(1)} %convolution_bitcast_fusion.4.r_ref, ...), custom_call_target="tpu_custom_call" | custom-call | tf_op jit(solution)/shard_map/pallas_call | solution.py:103
  24.7 0.0 slice-done
  24.7 0.0 slice-done.1
  24.7 0.0 copy-done.2
  24.7 0.0 copy-done.3
  24.7 16.8 %shard_map.101 = (bf16[16,128,128]{2,1,0:T(8,128)(2,1)S(1)}, bf16[16,8,256]{2,1,0:T(8,128)(2,1)S(1)}, bf16[128,256]{1,0:T(8,128)(2,1)S(1)}, f32[128,256]{1,0:T(8,128)S(1)}) custom-call(bf16[128,2048]{1,0:T(8,128)(2,1)S(1)} %get-tuple-element.15.a_ref, bf16[2048,2048]{1,0:T(8,128)(2,1)S(1)} %bitcast.56, f32[8,256]{1,0:T(8,128)S(1)} %get-tuple-element.16.share_ref, ...), custom_call_target="tpu_custom_call" | custom-call | tf_op jit(solution)/shard_map/pallas_call | solution.py:237
  41.6 0.4 convolution_convert_fusion.1
  42.0 0.1 copy.22
  42.2 0.6 %convolution_bitcast_fusion.1 = f32[1024,128]{1,0:T(8,128)S(1)} fusion(bf16[3,1024,256]{2,1,0:T(8,128)(2,1)S(1)} %copy-done.2, bf16[1,128,256]{2,1,0:T(8,128)(2,1)S(1)} %fusion.12, bf16[1,128,256]{2,1,0:T(8,128)(2,1)S(1)} %bitcast.58, bf16[1,128,256]{2,1,0:T(8,128)(2,1)S(1)} %slice.34), kind=kOutput, calls=%fused_computation.5 | convolution fusion | flops 201523200 | bytes 2293760 | tf_op jit(solution)/shard_map/blr,bwr->lw/dot_general | solution.py:325
  42.8 1.3 %fusion.3 = f32[1024,128]{1,0:T(8,128)S(1)} fusion(f32[1024,128]{1,0:T(8,128)S(1)} %convolution_bitcast_fusion.1, f32[1024,128]{1,0:T(8,128)S(1)} %get-tuple-element.14, bf16[1024,2048]{1,0:T(8,128)(2,1)S(1)} %copy-done.1, bf16[2048,128]{1,0:T(8,128)(2,1)S(1)} %bitcast.61), kind=kOutput, calls=%fused_computation.9 | convolution fusion | flops 537133056 | bytes 6291456 | tf_op jit(solution)/shard_map/dot_general | solution.py:319
  44.0 1.1 %fusion.1 = f32[1024,128]{1,0:T(8,128)} fusion(f32[1024,128]{1,0:T(8,128)S(1)} %fusion.3, bf16[1024,256]{1,0:T(8,128)(2,1)S(1)} %copy-done.3, bf16[16,8,256]{2,1,0:T(8,128)(2,1)S(1)} %get-tuple-element.22), kind=kOutput, calls=%fused_computation.6 | convolution fusion | flops 67239936 | bytes 1638400 | tf_op jit(solution)/shard_map/dot_general | solution.py:331
  (4 shorter events, 0.1 us)
Async XLA Ops:
  0.0 3.2 %copy-start = (bf16[3,1024,256]{2,1,0:T(8,128)(2,1)S(1)}, bf16[3,1024,256]{2,1,0:T(8,128)(2,1)}, u32[]{:S(2)}) copy-start(bf16[3,1024,256]{2,1,0:T(8,128)(2,1)} %param.15) | copy-start | bytes 4718596
  0.0 24.7 %slice-start = ((s8[8388608]{0:T(1024)(128)(4,1)}), s8[4194304]{0:T(1024)(128)(4,1)S(1)}, s32[]{:S(2)}) async-start(s8[8388608]{0:T(1024)(128)(4,1)} %bitcast.55), calls=%async_computation | async-start | bytes 8388608
  3.2 3.7 %copy-start.5 = (s32[16]{0:T(128)S(1)}, s32[16]{0:T(128)}, u32[]{:S(2)}) copy-start(s32[16]{0:T(128)} %param.19) | copy-start | bytes 196
  3.6 3.8 %copy-start.1 = (bf16[1024,2048]{1,0:T(8,128)(2,1)S(1)}, bf16[1024,2048]{1,0:T(8,128)(2,1)}, u32[]{:S(2)}) copy-start(bf16[1024,2048]{1,0:T(8,128)(2,1)} %e0_ref.1) | copy-start | bytes 12582916
  3.6 4.1 %copy-start.4 = (bf16[1024,1024]{1,0:T(8,128)(2,1)S(1)}, bf16[1024,1024]{1,0:T(8,128)(2,1)}, u32[]{:S(2)}) copy-start(bf16[1024,1024]{1,0:T(8,128)(2,1)} %li_ref.1) | copy-start | bytes 6291460
  6.9 17.8 %slice-start.1 = ((s8[8388608]{0:T(1024)(128)(4,1)}), s8[4194304]{0:T(1024)(128)(4,1)S(1)}, s32[]{:S(2)}) async-start(s8[8388608]{0:T(1024)(128)(4,1)} %bitcast.55), calls=%async_computation.1 | async-start | bytes 8388608
  7.8 16.9 %copy-start.2 = (bf16[3,1024,256]{2,1,0:T(8,128)(2,1)S(1)}, bf16[3,1024,256]{2,1,0:T(8,128)(2,1)}, u32[]{:S(2)}) copy-start(bf16[3,1024,256]{2,1,0:T(8,128)(2,1)} %e2_ref.1) | copy-start | bytes 4718596
  7.8 16.9 %copy-start.3 = (bf16[1024,256]{1,0:T(8,128)(2,1)S(1)}, bf16[1024,256]{1,0:T(8,128)(2,1)}, u32[]{:S(2)}) copy-start(bf16[1024,256]{1,0:T(8,128)(2,1)} %e3_ref.1) | copy-start | bytes 1572868
